TPU v7x, 32 devices: a whole 2x2x4 slice. The times are simulated.
32 devices in a mesh: wide: 16 (over z, y, core), narrow: 2 (over x).
Axes of the slice: x: 2, y: 2, z: 4, core: 2. Of those that a mesh axis runs over, the one named last changes fastest.
Arguments:
- tokens: bfloat16 [64, 1024, 768], P('wide', 'narrow'), may hold values from -6 to 6
- cotangent: bfloat16 [64, 1024, 768], P('wide', 'narrow'), may hold values from -6 to 6
- conv_attn: bfloat16 [9, 768], P(None, 'wide'), may hold values from -2 to 2
- qkv_weight: bfloat16 [768, 2304], P('wide'), may hold values from -0.21875 to 0.21875
- out_weight: bfloat16 [768, 768], P('wide'), may hold values from -0.875 to 0.875
- up_weight: bfloat16 [768, 3072], P('wide'), may hold values from -0.21875 to 0.21875
- conv_ffn: bfloat16 [9, 3072], P(None, 'wide'), may hold values from -2 to 2
- down_weight: bfloat16 [3072, 768], P('wide'), may hold values from -0.109375 to 0.109375
- ada_weight: bfloat16 [768, 4608], P('wide'), may hold values from -0.21875 to 0.21875
- class_table: bfloat16 [1000, 768], P(None, 'wide'), may hold values from -6 to 6
- timesteps: int32 [64, 4], replicated, may hold values from 0 to 999
- labels: int32 [64, 4], replicated, may hold values from 0 to 999
- layout: int32 [64], replicated, may hold values from 0 to 2
- counts: int32 [64], replicated, may hold values from 0 to 1024, as said below
Outputs:
- output: bfloat16 [64, 1024, 768], P('wide', 'narrow')
- grad_tokens: bfloat16 [64, 1024, 768], P('wide', 'narrow')
- grad_conv_attn: float32 [9, 768], P(None, 'wide')
- grad_qkv_weight: float32 [768, 2304], P('wide')
- grad_out_weight: float32 [768, 768], P('wide')
- grad_up_weight: float32 [768, 3072], P('wide')
- grad_conv_ffn: float32 [9, 3072], P(None, 'wide')
- grad_down_weight: float32 [3072, 768], P('wide')
- grad_ada_weight: float32 [768, 4608], P('wide')
- grad_class_table: float32 [1000, 768], P(None, 'wide')
Inputs may be any that keep to these rules, and one draw needn't show every extreme that they name: Owner o holds the 4 canvas slots o * 4 to (o + 1) * 4 - 1, those with a nonzero count first. Owners o and o + 8 together hold exactly 4 canvases with nonzero counts, and some owner holds 4. Nonzero counts are 256 or more.
All inputs are finite; a program needn't handle non-finite values.
Results may differ from a plain program's by a relative error of at most 0.02.
The roundings to bfloat16 on the way count: a program that leaves them out, or rounds other values in their place, can miss the bound.
Values may be sent and summed in bfloat16 or wider, within the bound.
No kernel may reach another device: no remote copies, remote signals or barrier semaphores. Data moves between devices by JAX's collectives and lax.ppermute only.
A program may use at most 512 MiB of HBM per device.

v0:
```python
from functools import partial
import math

import jax
import jax.numpy as jnp
from jax import lax
from jax.sharding import PartitionSpec as P

HEADS = 12
HEAD_DIM = 64
GRID = 32
MICRO = 1


highest = lax.Precision.HIGHEST
norm_eps = 1e-06
masked_score = -1e30


def extended(block, sides, width):
    for axis, dim in sides:
        count = lax.axis_size(axis)
        forward = [(i, i + 1) for i in range(count - 1)]
        backward = [(target, source) for source, target in forward]
        low = lax.ppermute(
            lax.slice_in_dim(block, block.shape[dim] - width, None, axis=dim), axis, forward
        )
        high = lax.ppermute(lax.slice_in_dim(block, 0, width, axis=dim), axis, backward)
        block = jnp.concatenate([low, block, high], axis=dim)
    return block


def canvas_segments(layout_part, row_ids):
    row_grid = row_ids[None, :, None]
    col_grid = jnp.arange(GRID, dtype=jnp.int32)[None, None, :]
    quarter = 2 * (row_grid // (GRID // 2)) + col_grid // (GRID // 2)
    across = row_grid // (GRID // 4) + 0 * col_grid
    downward = col_grid // (GRID // 4) + 0 * row_grid
    chosen_layout = layout_part[:, None, None]
    return jnp.where(chosen_layout == 0, quarter, jnp.where(chosen_layout == 1, across, downward))


def depthwise(padded, taps, seg_rows):
    row_total = padded.shape[1] - 2
    side_pad = jnp.pad(padded, ((0, 0), (0, 0), (1, 1), (0, 0)))
    seg_pad = jnp.pad(seg_rows, ((0, 0), (0, 0), (1, 1)), constant_values=-1)
    centre = seg_rows[:, 1 : row_total + 1, :]
    total = jnp.zeros((padded.shape[0], row_total, GRID, padded.shape[3]), jnp.float32)
    for row_step in range(3):
        for col_step in range(3):
            nearby = side_pad[
                :, row_step : row_step + row_total, col_step : col_step + GRID, :
            ].astype(jnp.float32)
            same = seg_pad[:, row_step : row_step + row_total, col_step : col_step + GRID] == centre
            tap_row = taps[3 * row_step + col_step].astype(jnp.float32)
            total = total + jnp.where(same[..., None], nearby, 0.0) * tap_row
    return total


def tap_grads(padded, grads, seg_rows):
    row_total = padded.shape[1] - 2
    side_pad = jnp.pad(padded, ((0, 0), (0, 0), (1, 1), (0, 0)))
    seg_pad = jnp.pad(seg_rows, ((0, 0), (0, 0), (1, 1)), constant_values=-1)
    centre = seg_rows[:, 1 : row_total + 1, :]
    grads_float = grads.astype(jnp.float32)
    listed = []
    for row_step in range(3):
        for col_step in range(3):
            nearby = side_pad[
                :, row_step : row_step + row_total, col_step : col_step + GRID, :
            ].astype(jnp.float32)
            same = seg_pad[:, row_step : row_step + row_total, col_step : col_step + GRID] == centre
            listed.append(
                jnp.sum(jnp.where(same[..., None], nearby, 0.0) * grads_float, axis=(0, 1, 2))
            )
    return jnp.stack(listed)


def to_subgrids(values):
    batch_size = values.shape[0]
    row_total = values.shape[1]
    viewed = values.reshape(batch_size, row_total // 2, 2, GRID // 2, 2, HEADS, HEAD_DIM)
    reordered = viewed.transpose(0, 2, 4, 5, 1, 3, 6)
    return reordered.reshape(batch_size, 2, 2, HEADS, row_total // 2 * (GRID // 2), HEAD_DIM)


def from_subgrids(values, row_total):
    batch_size = values.shape[0]
    viewed = values.reshape(batch_size, 2, 2, HEADS, row_total // 2, GRID // 2, HEAD_DIM)
    reordered = viewed.transpose(0, 4, 1, 5, 2, 3, 6)
    return reordered.reshape(batch_size, row_total, GRID, HEADS * HEAD_DIM)


def seg_subgrids(segment):
    batch_size = segment.shape[0]
    row_total = segment.shape[1]
    viewed = segment.reshape(batch_size, row_total // 2, 2, GRID // 2, 2)
    return viewed.transpose(0, 2, 4, 1, 3).reshape(batch_size, 2, 2, row_total // 2 * (GRID // 2))


def pick_segment(table_rows, token_seg):
    picked = jnp.zeros(token_seg.shape + (table_rows.shape[2],), jnp.float32)
    for latent in range(4):
        picked = picked + jnp.where(
            (token_seg == latent)[..., None], table_rows[:, latent][:, None, :], 0.0
        )
    return picked


def layer_norm(values):
    centred = values - jnp.mean(values, axis=-1, keepdims=True)
    inverse = lax.rsqrt(jnp.mean(centred * centred, axis=-1, keepdims=True) + norm_eps)
    return (centred * inverse, inverse)


def norm_back(grad_normed, normed, inverse):
    return inverse * (
        grad_normed
        - jnp.mean(grad_normed, axis=-1, keepdims=True)
        - normed * jnp.mean(grad_normed * normed, axis=-1, keepdims=True)
    )


def body(
    tokens,
    cotangent,
    conv_attn,
    qkv_weight,
    out_weight,
    up_weight,
    conv_ffn,
    down_weight,
    ada_weight,
    class_table,
    timesteps,
    labels,
    layout,
    counts,
):
    gathered = (
        lax.all_gather(conv_attn, "wide", axis=1, tiled=True),
        lax.all_gather(qkv_weight, "wide", axis=0, tiled=True),
        lax.all_gather(out_weight, "wide", axis=0, tiled=True),
        lax.all_gather(up_weight, "wide", axis=0, tiled=True),
        lax.all_gather(conv_ffn, "wide", axis=1, tiled=True),
        lax.all_gather(down_weight, "wide", axis=0, tiled=True),
        lax.all_gather(ada_weight, "wide", axis=0, tiled=True),
        lax.all_gather(class_table, "wide", axis=1, tiled=True),
    )
    conv_one, qkv_full, out_full, up_full, conv_two, down_full, ada_full, table_full = gathered
    slot_count = tokens.shape[0]
    local_tokens = tokens.shape[1]
    model_width = tokens.shape[2]
    ffn_width = up_full.shape[1]
    row_count = local_tokens // GRID
    owner_index = lax.axis_index("wide")
    row_start = lax.axis_index("narrow") * row_count
    count_float = counts.astype(jnp.float32)
    scales = count_float * float(counts.shape[0]) / jnp.sum(count_float)
    positions = jnp.arange(slot_count, dtype=jnp.int32)
    work_index = owner_index * slot_count + positions
    work_count = tokens.shape[0]
    work_steps = timesteps[work_index]
    work_labels = labels[work_index]
    work_layout = layout[work_index]
    work_scale = scales[work_index]
    half_width = model_width // 2
    freqs = jnp.exp(-math.log(10000.0) * jnp.arange(half_width, dtype=jnp.float32) / half_width)
    angles = work_steps.astype(jnp.float32)[..., None] * freqs
    label_hot = (work_labels[..., None] == jnp.arange(table_full.shape[0], dtype=jnp.int32)).astype(
        jnp.bfloat16
    )
    embed = jnp.concatenate([jnp.cos(angles), jnp.sin(angles)], axis=-1) + jnp.einsum(
        "csk,kd->csd", label_hot, table_full, preferred_element_type=jnp.float32
    )
    activ, silu_back = jax.vjp(jax.nn.silu, embed)
    act_low = activ.astype(jnp.bfloat16)
    modulation = jnp.einsum("csd,de->cse", act_low, ada_full, preferred_element_type=jnp.float32)
    y_parts = []
    x_parts = []
    mod_parts = []
    grad_sums = None
    for block_start in range(0, work_count, MICRO):
        block_end = block_start + MICRO
        block_tokens = tokens[block_start:block_end]
        block_layout = work_layout[block_start:block_end]
        block_scale = work_scale[block_start:block_end]
        batch_size = block_tokens.shape[0]
        flat_rows = batch_size * local_tokens
        row_ids = row_start - 1 + jnp.arange(row_count + 2, dtype=jnp.int32)
        seg_rows = canvas_segments(block_layout, row_ids)
        centre = seg_rows[:, 1 : row_count + 1, :]
        token_seg = centre.reshape(batch_size, local_tokens)
        per_token = pick_segment(modulation[block_start:block_end], token_seg)
        shift_a, scale_a, gate_a, shift_b, scale_b, gate_b = jnp.split(per_token, 6, axis=-1)
        inputs = block_tokens.astype(jnp.float32)
        normed_a, inverse_a = layer_norm(inputs)
        hidden_in = (normed_a * (1.0 + scale_a) + shift_a).astype(jnp.bfloat16)
        hidden_pad = extended(
            hidden_in.reshape(batch_size, row_count, GRID, model_width), (("narrow", 1),), 1
        )
        mixed = depthwise(hidden_pad, conv_one, seg_rows).astype(jnp.bfloat16)
        mixed_flat = mixed.reshape(flat_rows, model_width)
        projected = jnp.dot(mixed_flat, qkv_full, preferred_element_type=jnp.float32).astype(
            jnp.bfloat16
        )
        projected = projected.reshape(batch_size, row_count, GRID, 3 * model_width)
        query = projected[..., :model_width]
        key_part = projected[..., model_width : 2 * model_width]
        value_part = projected[..., 2 * model_width :]
        full_keys = lax.all_gather(key_part, "narrow", axis=1, tiled=True)
        full_values = lax.all_gather(value_part, "narrow", axis=1, tiled=True)
        q_sub = to_subgrids(query)
        k_sub = to_subgrids(full_keys)
        v_sub = to_subgrids(full_values)
        seg_query = seg_subgrids(centre)
        seg_key = seg_subgrids(canvas_segments(block_layout, jnp.arange(GRID, dtype=jnp.int32)))
        allowed = seg_query[:, :, :, None, :, None] == seg_key[:, :, :, None, None, :]

        def score_block():
            raw = (
                jnp.einsum(
                    "cabhqd,cabhkd->cabhqk", q_sub, k_sub, preferred_element_type=jnp.float32
                )
                * 0.125
            )
            return jnp.where(allowed, raw, masked_score)

        masked = score_block()
        top = jnp.max(masked, axis=-1, keepdims=True)
        expo = jnp.exp(masked - top)
        total = jnp.sum(expo, axis=-1, keepdims=True)
        probs = expo / total
        log_total = top + jnp.log(total)
        probs_low = probs.astype(jnp.bfloat16)
        attended = jnp.einsum(
            "cabhqk,cabhkd->cabhqd", probs_low, v_sub, preferred_element_type=jnp.float32
        ).astype(jnp.bfloat16)
        attended_flat = from_subgrids(attended, row_count).reshape(flat_rows, model_width)
        branch_a = jnp.dot(attended_flat, out_full, preferred_element_type=jnp.float32).reshape(
            batch_size, local_tokens, model_width
        )
        middle = inputs + gate_a * branch_a
        normed_b, inverse_b = layer_norm(middle)
        ffn_in = (
            (normed_b * (1.0 + scale_b) + shift_b)
            .astype(jnp.bfloat16)
            .reshape(flat_rows, model_width)
        )
        upward = (
            jnp.dot(ffn_in, up_full, preferred_element_type=jnp.float32)
            .astype(jnp.bfloat16)
            .reshape(batch_size, row_count, GRID, ffn_width)
        )
        up_pad = extended(upward, (("narrow", 1),), 1)
        spread = depthwise(up_pad, conv_two, seg_rows)
        activated, gelu_back = jax.vjp(partial(jax.nn.gelu, approximate=True), spread)
        act_flat = activated.astype(jnp.bfloat16).reshape(flat_rows, ffn_width)
        branch_b = jnp.dot(act_flat, down_full, preferred_element_type=jnp.float32).reshape(
            batch_size, local_tokens, model_width
        )
        result = middle + gate_b * branch_b
        alive = (block_scale > 0.0)[:, None, None]
        y_block = jnp.where(alive, result, 0.0).astype(jnp.bfloat16)
        grad_out = cotangent[block_start:block_end].astype(jnp.float32) * block_scale[:, None, None]
        grad_gate_b = grad_out * branch_b
        grad_branch_b = (gate_b * grad_out).astype(jnp.bfloat16).reshape(flat_rows, model_width)
        grad_down = jnp.einsum(
            "tf,td->fd", act_flat, grad_branch_b, preferred_element_type=jnp.float32
        )
        grad_act = jnp.einsum(
            "td,fd->tf", grad_branch_b, down_full, preferred_element_type=jnp.float32
        ).reshape(batch_size, row_count, GRID, ffn_width)
        grad_spread = gelu_back(grad_act)[0].astype(jnp.bfloat16)
        spread_pad = extended(grad_spread, (("narrow", 1),), 1)
        grad_conv_two = tap_grads(up_pad, grad_spread, seg_rows)
        grad_up = (
            depthwise(spread_pad, conv_two[::-1], seg_rows)
            .astype(jnp.bfloat16)
            .reshape(flat_rows, ffn_width)
        )
        grad_up_weight = jnp.einsum(
            "td,tf->df", ffn_in, grad_up, preferred_element_type=jnp.float32
        )
        grad_ffn_in = jnp.einsum(
            "tf,df->td", grad_up, up_full, preferred_element_type=jnp.float32
        ).reshape(batch_size, local_tokens, model_width)
        grad_scale_b = grad_ffn_in * normed_b
        grad_middle = grad_out + norm_back(grad_ffn_in * (1.0 + scale_b), normed_b, inverse_b)
        grad_gate_a = grad_middle * branch_a
        grad_branch_a = (gate_a * grad_middle).astype(jnp.bfloat16).reshape(flat_rows, model_width)
        grad_out_weight = jnp.einsum(
            "td,te->de", attended_flat, grad_branch_a, preferred_element_type=jnp.float32
        )
        grad_attended = jnp.einsum(
            "te,de->td", grad_branch_a, out_full, preferred_element_type=jnp.float32
        ).astype(jnp.bfloat16)
        grad_sub = to_subgrids(grad_attended.reshape(batch_size, row_count, GRID, model_width))
        grad_probs = jnp.einsum(
            "cabhqd,cabhkd->cabhqk", grad_sub, v_sub, preferred_element_type=jnp.float32
        )
        probs_again = jnp.exp(score_block() - log_total)
        row_inner = jnp.sum(probs_again * grad_probs, axis=-1, keepdims=True)
        grad_scores = (probs_again * (grad_probs - row_inner)).astype(jnp.bfloat16)
        grad_query = (
            jnp.einsum(
                "cabhqk,cabhkd->cabhqd", grad_scores, k_sub, preferred_element_type=jnp.float32
            )
            * 0.125
        ).astype(jnp.bfloat16)
        grad_keys = (
            jnp.einsum(
                "cabhqk,cabhqd->cabhkd", grad_scores, q_sub, preferred_element_type=jnp.float32
            )
            * 0.125
        )
        grad_values = jnp.einsum(
            "cabhqk,cabhqd->cabhkd", probs_low, grad_sub, preferred_element_type=jnp.float32
        )
        key_sums = lax.psum_scatter(
            from_subgrids(grad_keys, GRID).astype(jnp.bfloat16),
            "narrow",
            scatter_dimension=1,
            tiled=True,
        )
        value_sums = lax.psum_scatter(
            from_subgrids(grad_values, GRID).astype(jnp.bfloat16),
            "narrow",
            scatter_dimension=1,
            tiled=True,
        )
        grad_projected = jnp.concatenate(
            [from_subgrids(grad_query, row_count), key_sums, value_sums], axis=-1
        ).reshape(flat_rows, 3 * model_width)
        grad_qkv_weight = jnp.einsum(
            "td,te->de", mixed_flat, grad_projected, preferred_element_type=jnp.float32
        )
        grad_mixed = (
            jnp.einsum("te,de->td", grad_projected, qkv_full, preferred_element_type=jnp.float32)
            .astype(jnp.bfloat16)
            .reshape(batch_size, row_count, GRID, model_width)
        )
        mixed_pad = extended(grad_mixed, (("narrow", 1),), 1)
        grad_conv_one = tap_grads(hidden_pad, grad_mixed, seg_rows)
        grad_hidden = depthwise(mixed_pad, conv_one[::-1], seg_rows).reshape(
            batch_size, local_tokens, model_width
        )
        grad_scale_a = grad_hidden * normed_a
        grad_inputs = grad_middle + norm_back(grad_hidden * (1.0 + scale_a), normed_a, inverse_a)
        x_block = grad_inputs.astype(jnp.bfloat16)
        grad_token_mod = jnp.concatenate(
            [grad_hidden, grad_scale_a, grad_gate_a, grad_ffn_in, grad_scale_b, grad_gate_b],
            axis=-1,
        )
        seg_hot = (token_seg[..., None] == jnp.arange(4, dtype=jnp.int32)).astype(jnp.float32)
        mod_grad = jnp.einsum("cts,cte->cse", seg_hot, grad_token_mod, precision=highest)
        y_block, x_block, mod_grad, block_grads = (
            y_block,
            x_block,
            mod_grad,
            (
                grad_conv_one,
                grad_qkv_weight,
                grad_out_weight,
                grad_up_weight,
                grad_conv_two,
                grad_down,
            ),
        )
        y_parts.append(y_block)
        x_parts.append(x_block)
        mod_parts.append(mod_grad)
        if grad_sums is None:
            grad_sums = block_grads
        else:
            grad_sums = tuple((summed + added for summed, added in zip(grad_sums, block_grads)))
    work_y = jnp.concatenate(y_parts, axis=0)
    work_x = jnp.concatenate(x_parts, axis=0)
    mod_all = jnp.concatenate(mod_parts, axis=0)
    grad_ada = jnp.einsum("csd,cse->de", act_low.astype(jnp.float32), mod_all, precision=highest)
    grad_activ = jnp.einsum("cse,de->csd", mod_all, ada_full.astype(jnp.float32), precision=highest)
    grad_embed = silu_back(grad_activ)[0]
    grad_table = jnp.einsum(
        "csk,csd->kd", label_hot.astype(jnp.float32), grad_embed, precision=highest
    )
    conv_sum, qkv_sum, out_sum, up_sum, conv_ffn_sum, down_sum = grad_sums
    wide_sums = (
        lax.psum_scatter(
            conv_sum.astype(jnp.bfloat16), "wide", scatter_dimension=1, tiled=True
        ).astype(jnp.float32),
        lax.psum_scatter(
            qkv_sum.astype(jnp.bfloat16), "wide", scatter_dimension=0, tiled=True
        ).astype(jnp.float32),
        lax.psum_scatter(
            out_sum.astype(jnp.bfloat16), "wide", scatter_dimension=0, tiled=True
        ).astype(jnp.float32),
        lax.psum_scatter(
            up_sum.astype(jnp.bfloat16), "wide", scatter_dimension=0, tiled=True
        ).astype(jnp.float32),
        lax.psum_scatter(
            conv_ffn_sum.astype(jnp.bfloat16), "wide", scatter_dimension=1, tiled=True
        ).astype(jnp.float32),
        lax.psum_scatter(
            down_sum.astype(jnp.bfloat16), "wide", scatter_dimension=0, tiled=True
        ).astype(jnp.float32),
        lax.psum_scatter(
            grad_ada.astype(jnp.bfloat16), "wide", scatter_dimension=0, tiled=True
        ).astype(jnp.float32),
        lax.psum_scatter(
            grad_table.astype(jnp.bfloat16), "wide", scatter_dimension=1, tiled=True
        ).astype(jnp.float32),
    )
    final = (
        lax.psum(wide_sums[0].astype(jnp.bfloat16), "narrow").astype(jnp.float32),
        lax.psum(wide_sums[1].astype(jnp.bfloat16), "narrow").astype(jnp.float32),
        lax.psum(wide_sums[2].astype(jnp.bfloat16), "narrow").astype(jnp.float32),
        lax.psum(wide_sums[3].astype(jnp.bfloat16), "narrow").astype(jnp.float32),
        lax.psum(wide_sums[4].astype(jnp.bfloat16), "narrow").astype(jnp.float32),
        lax.psum(wide_sums[5].astype(jnp.bfloat16), "narrow").astype(jnp.float32),
        lax.psum(wide_sums[6].astype(jnp.bfloat16), "narrow").astype(jnp.float32),
        lax.psum(wide_sums[7].astype(jnp.bfloat16), "narrow").astype(jnp.float32),
    )
    return (
        work_y,
        work_x,
        final[0],
        final[1],
        final[2],
        final[3],
        final[4],
        final[5],
        final[6],
        final[7],
    )


def solution(mesh):
    return jax.shard_map(
        body,
        mesh=mesh,
        in_specs=(
            P("wide", "narrow", None),
            P("wide", "narrow", None),
            P(None, "wide"),
            P("wide", None),
            P("wide", None),
            P("wide", None),
            P(None, "wide"),
            P("wide", None),
            P("wide", None),
            P(None, "wide"),
            P(),
            P(),
            P(),
            P(),
        ),
        out_specs=(
            P("wide", "narrow", None),
            P("wide", "narrow", None),
            P(None, "wide"),
            P("wide", None),
            P("wide", None),
            P("wide", None),
            P(None, "wide"),
            P("wide", None),
            P("wide", None),
            P(None, "wide"),
        ),
        check_vma=False,
    )
```

profile of v0, /device:TPU:0, one launch (start us, length us, event | category | flops | bytes accessed | tf_op | source)
XLA Modules:
  0.0 2079.0 jit_solution(638172698328290881)
XLA Ops:
  19.4 23.7 %all-gather = bf16[16,48,9]{1,2,0:T(8,128)(2,1)S(1)} all-gather(bf16[1,48,9]{1,2,0:T(8,128)(2,1)} %bitcast.1167), channel_id=1, replica_groups=mesh['wide'=16,'narrow'=2] {'wide'}, dimensions={0}, use_global_device_ids=true | all-gather | bytes 14688 | tf_op jit(solution)/shard_map/all_gather | solution.py:141
  54.7 65.9 %all-gather.19.cloned.1.call-done = bf16[768,4608]{1,0:T(8,128)(2,1)} async-done(((bf16[48,4608]{1,0:T(8,128)(2,1)}), bf16[768,4608]{1,0:T(8,128)(2,1)}) %all-gather.19.cloned.1.call-update) | async-done | bytes 7077904 | tf_op jit(solution)/shard_map/all_gather | solution.py:147
  145.3 23.0 %all-gather.21.cloned.1.call-done = bf16[768,2304]{1,0:T(8,128)(2,1)} async-done(((bf16[48,2304]{1,0:T(8,128)(2,1)}), bf16[768,2304]{1,0:T(8,128)(2,1)}) %all-gather.21.cloned.1.call-update) | async-done | bytes 3538960 | tf_op jit(solution)/shard_map/all_gather | solution.py:142
  181.8 19.8 all-gather.1
  258.7 12.1 all-gather.27.cloned.1.call-done
  280.7 44.8 %all-gather.29.cloned.1.call-done = bf16[768,3072]{1,0:T(8,128)(2,1)} async-done(((bf16[48,3072]{1,0:T(8,128)(2,1)}), bf16[768,3072]{1,0:T(8,128)(2,1)}) %all-gather.29.cloned.1.call-update) | async-done | bytes 4718608 | tf_op jit(solution)/shard_map/all_gather | solution.py:144
  346.9 14.8 multiply_convert_fusion.4
  361.7 18.1 all-gather.31.cloned.1.call-done
  379.8 21.5 %fusion.121 = (f32[3072]{0:T(1024)}, f32[3072]{0:T(1024)}, f32[3072]{0:T(1024)}, f32[3072]{0:T(1024)}, f32[3072]{0:T(1024)}, /*index=5*/f32[3072]{0:T(1024)}, f32[3072]{0:T(1024)}, bf16[1,16,32,3072]{3,2,1,0:T(8,128)(2,1)S(1)}) fusion(pred[16,32]{1,0:T(8,128)(4,1)S(1)} %copy-done.304, bf16[1,18,34,3072]{3,2,1,0:T(8,128)(2,1)} %copy-done.6, ...), kind=kOutput, calls=%fused_computation.189 | convolution fusion | flops 2491395072 | bytes 37051392 | tf_op jit(solution)/shard_map/td,fd->tf/dot_general | solution.py:271
  415.8 11.5 fusion.112
  463.7 8.0 multiply_reduce_fusion
  510.3 8.0 reduce-scatter.33.cloned.1.call-done
  518.3 8.2 fusion.325
  576.3 16.8 all-gather.23.cloned.1.call-done
  604.4 17.4 all-gather.25.cloned.1.call-done
  675.1 14.4 multiply_convert_fusion.7
  689.4 17.1 fusion.76
  717.6 11.5 fusion.67
  767.8 7.5 multiply_reduce_fusion.3
  817.9 8.9 reduce-scatter.21.cloned.1.call-done
  826.9 8.2 fusion.286
  880.3 16.7 all-gather.33.cloned.1.call-done
  908.2 17.5 all-gather.35.cloned.1.call-done
  978.9 14.4 multiply_convert_fusion.6
  993.3 17.1 fusion.91
  1021.5 11.5 fusion.82
  1071.7 7.5 multiply_reduce_fusion.2
  1102.4 7.3 select_add_fusion.1
  1122.0 8.7 reduce-scatter.25.cloned.1.call-done
  1130.8 8.4 fusion.299
  1184.9 16.3 all-gather.37.cloned.1.call-done
  1212.3 17.4 all-gather.39.cloned.1.call-done
  1284.0 13.9 multiply_convert_fusion.5
  1297.9 16.3 fusion.106
  1325.2 11.5 fusion.97
  1434.6 7.2 fusion.312
  1466.3 7.6 fusion.356
  1511.2 13.3 add_convert_fusion
  1539.7 13.2 add_convert_fusion.1
  1585.4 9.0 fusion.9
  1594.4 8.2 bitcast_convert_fusion
  1665.6 63.8 %reduce-scatter.41.cloned.1.call-done = bf16[48,3072]{1,0:T(8,128)(2,1)} async-done(((bf16[768,3072]{1,0:T(8,128)(2,1)}), bf16[48,3072]{1,0:T(8,128)(2,1)}) %reduce-scatter.41.cloned.1.call-update) | async-done | bytes 294928 | tf_op jit(solution)/shard_map/reduce_scatter | solution.py:397
  1729.4 71.3 %reduce-scatter.37.cloned.1.call-done = bf16[48,2304]{1,0:T(8,128)(2,1)} async-done(((bf16[768,2304]{1,0:T(8,128)(2,1)}), bf16[48,2304]{1,0:T(8,128)(2,1)}) %reduce-scatter.37.cloned.1.call-update) | async-done | bytes 221200 | tf_op jit(solution)/shard_map/reduce_scatter | solution.py:391
  1800.7 93.5 %reduce-scatter.45.cloned.1.call-done = bf16[48,4608]{1,0:T(8,128)(2,1)} async-done(((bf16[768,4608]{1,0:T(8,128)(2,1)}), bf16[48,4608]{1,0:T(8,128)(2,1)}) %reduce-scatter.45.cloned.1.call-update) | async-done | bytes 442384 | tf_op jit(solution)/shard_map/reduce_scatter | solution.py:406
  1894.2 60.2 %reduce-scatter.51.cloned.1.call-done = bf16[192,9]{1,0:T(8,128)(2,1)} async-done(((bf16[3072,9]{1,0:T(8,128)(2,1)}), bf16[192,9]{1,0:T(8,128)(2,1)}) %reduce-scatter.51.cloned.1.call-update) | async-done | bytes 3472
  1958.5 52.8 %reduce-scatter.49.cloned.1.call-done = bf16[48,9]{1,0:T(8,128)(2,1)} async-done(((bf16[768,9]{1,0:T(8,128)(2,1)}), bf16[48,9]{1,0:T(8,128)(2,1)}) %reduce-scatter.49.cloned.1.call-update) | async-done | bytes 880
  2012.1 8.1 all-reduce.20
  2024.3 38.2 %all-reduce.24.cloned.1.call-done = (bf16[48,2304]{1,0:T(8,128)(2,1)}, bf16[48,768]{1,0:T(8,128)(2,1)}, bf16[48,3072]{1,0:T(8,128)(2,1)}, bf16[192,768]{1,0:T(8,...) async-done(((bf16[48,2304]{1,0:T(8,128)(2,1)}, bf16[48,768]{1,0:T(8,128)(2,1)}, bf16[48,3072]{1,0:T(8,128)(2,1)}, bf16[192,768]{1,0:T(8,128)(2,1)}, ...) | async-done | bytes 1423120 | tf_op jit(solution)/shard_map/psum | solution.py:415
  (1381 shorter events, 1038.7 us)
Async XLA Ops:
  7.2 45.5 %all-gather.17.cloned.1.call-start = ((), (), s32[]{:S(2)}) async-start(), calls=%async_computation.16 | async-start | bytes 1671168 | tf_op jit(solution)/shard_map/all_gather | solution.py:148
  7.9 112.6 %all-gather.19.cloned.1.call-start = ((), (), s32[]{:S(2)}) async-start(), calls=%async_computation.17 | async-start | bytes 7520256 | tf_op jit(solution)/shard_map/all_gather | solution.py:147
  8.7 159.6 %all-gather.21.cloned.1.call-start = ((), (), s32[]{:S(2)}) async-start(), calls=%async_computation.18 | async-start | bytes 3760128 | tf_op jit(solution)/shard_map/all_gather | solution.py:142
  9.4 202.0 %all-gather.41.cloned.1.call-start = ((), (), s32[]{:S(2)}) async-start(), calls=%async_computation.28 | async-start | bytes 2359296 | tf_op jit(solution)/shard_map/all_gather | solution.py:211
  175.3 55.0 %all-gather.43.cloned.1.call-start = ((), (), s32[]{:S(2)}) async-start(), calls=%async_computation.29 | async-start | bytes 2359296 | tf_op jit(solution)/shard_map/all_gather | solution.py:212
  175.9 94.9 %all-gather.27.cloned.1.call-start = ((), (), s32[]{:S(2)}) async-start(), calls=%async_computation.21 | async-start | bytes 1253376 | tf_op jit(solution)/shard_map/all_gather | solution.py:143
  176.5 149.0 %all-gather.29.cloned.1.call-start = ((), (), s32[]{:S(2)}) async-start(), calls=%async_computation.22 | async-start | bytes 5013504 | tf_op jit(solution)/shard_map/all_gather | solution.py:144
  177.2 202.5 %all-gather.31.cloned.1.call-start = ((), (), s32[]{:S(2)}) async-start(), calls=%async_computation.23 | async-start | bytes 5013504 | tf_op jit(solution)/shard_map/all_gather | solution.py:146
  178.0 332.3 %reduce-scatter.35.cloned.1.call-start = ((), (), s32[]{:S(2)}) async-start(), calls=%async_computation.37 | async-start | bytes 2359296 | tf_op jit(solution)/shard_map/reduce_scatter | solution.py:326
  330.8 7.9 collective-permute-start.14
  334.2 8.7 collective-permute-start.15
  401.3 7.9 collective-permute-start.28
  404.7 8.7 collective-permute-start.29
  463.6 54.7 %reduce-scatter.33.cloned.1.call-start = ((), (), s32[]{:S(2)}) async-start(), calls=%async_computation.36 | async-start | bytes 2359296 | tf_op jit(solution)/shard_map/reduce_scatter | solution.py:320
  494.9 98.2 %all-gather.23.cloned.1.call-start = ((), (), s32[]{:S(2)}) async-start(), calls=%async_computation.19 | async-start | bytes 2359296 | tf_op jit(solution)/shard_map/all_gather | solution.py:211
  526.6 8.2 collective-permute-start.30
  565.5 56.2 %all-gather.25.cloned.1.call-start = ((), (), s32[]{:S(2)}) async-start(), calls=%async_computation.20 | async-start | bytes 2359296 | tf_op jit(solution)/shard_map/all_gather | solution.py:212
  566.1 251.8 %reduce-scatter.23.cloned.1.call-start = ((), (), s32[]{:S(2)}) async-start(), calls=%async_computation.31 | async-start | bytes 2359296 | tf_op jit(solution)/shard_map/reduce_scatter | solution.py:326
  662.5 6.5 collective-permute-start.2
  664.7 8.4 collective-permute-start.3
  706.6 8.9 collective-permute-start.16
  708.1 7.6 collective-permute-start.17
  767.7 59.0 %reduce-scatter.21.cloned.1.call-start = ((), (), s32[]{:S(2)}) async-start(), calls=%async_computation.30 | async-start | bytes 2359296 | tf_op jit(solution)/shard_map/reduce_scatter | solution.py:320
  798.5 98.6 %all-gather.33.cloned.1.call-start = ((), (), s32[]{:S(2)}) async-start(), calls=%async_computation.24 | async-start | bytes 2359296 | tf_op jit(solution)/shard_map/all_gather | solution.py:211
  869.4 56.3 %all-gather.35.cloned.1.call-start = ((), (), s32[]{:S(2)}) async-start(), calls=%async_computation.25 | async-start | bytes 2359296 | tf_op jit(solution)/shard_map/all_gather | solution.py:212
  870.0 252.0 %reduce-scatter.27.cloned.1.call-start = ((), (), s32[]{:S(2)}) async-start(), calls=%async_computation.33 | async-start | bytes 2359296 | tf_op jit(solution)/shard_map/reduce_scatter | solution.py:326
  968.6 8.4 collective-permute-start.7
  1010.5 9.1 collective-permute-start.20
  1011.9 7.6 collective-permute-start.21
  1071.6 59.1 %reduce-scatter.25.cloned.1.call-start = ((), (), s32[]{:S(2)}) async-start(), calls=%async_computation.32 | async-start | bytes 2359296 | tf_op jit(solution)/shard_map/reduce_scatter | solution.py:320
  1102.2 99.0 %all-gather.37.cloned.1.call-start = ((), (), s32[]{:S(2)}) async-start(), calls=%async_computation.26 | async-start | bytes 2359296 | tf_op jit(solution)/shard_map/all_gather | solution.py:211
  1173.5 56.3 %all-gather.39.cloned.1.call-start = ((), (), s32[]{:S(2)}) async-start(), calls=%async_computation.27 | async-start | bytes 2359296 | tf_op jit(solution)/shard_map/all_gather | solution.py:212
  1174.1 260.5 %reduce-scatter.31.cloned.1.call-start = ((), (), s32[]{:S(2)}) async-start(), calls=%async_computation.35 | async-start | bytes 2359296 | tf_op jit(solution)/shard_map/reduce_scatter | solution.py:326
  1271.4 6.5 collective-permute-start.10
  1273.6 8.4 collective-permute-start.11
  1314.2 8.8 collective-permute-start.24
  1315.7 7.6 collective-permute-start.25
  1369.1 65.5 %reduce-scatter.29.cloned.1.call-start = ((), (), s32[]{:S(2)}) async-start(), calls=%async_computation.34 | async-start | bytes 2359296 | tf_op jit(solution)/shard_map/reduce_scatter | solution.py:320
  1403.0 262.6 %reduce-scatter.39.cloned.1.call-start = ((), (), s32[]{:S(2)}) async-start(), calls=%async_computation.39 | async-start | bytes 1253376 | tf_op jit(solution)/shard_map/reduce_scatter | solution.py:394
  1441.8 8.1 collective-permute-start.26
  1449.8 215.7 %reduce-scatter.47.cloned.1.call-start = ((), (), s32[]{:S(2)}) async-start(), calls=%async_computation.43 | async-start | bytes 1671168 | tf_op jit(solution)/shard_map/reduce_scatter | solution.py:409
  1499.1 166.4 %reduce-scatter.43.cloned.1.call-start = ((), (), s32[]{:S(2)}) async-start(), calls=%async_computation.41 | async-start | bytes 5013504 | tf_op jit(solution)/shard_map/reduce_scatter | solution.py:403
  1524.4 205.0 %reduce-scatter.41.cloned.1.call-start = ((), (), s32[]{:S(2)}) async-start(), calls=%async_computation.40 | async-start | bytes 5013504 | tf_op jit(solution)/shard_map/reduce_scatter | solution.py:397
  1552.9 247.8 %reduce-scatter.37.cloned.1.call-start = ((), (), s32[]{:S(2)}) async-start(), calls=%async_computation.38 | async-start | bytes 3760128 | tf_op jit(solution)/shard_map/reduce_scatter | solution.py:391
  1594.4 299.8 %reduce-scatter.45.cloned.1.call-start = ((), (), s32[]{:S(2)}) async-start(), calls=%async_computation.42 | async-start | bytes 7520256 | tf_op jit(solution)/shard_map/reduce_scatter | solution.py:406
  1602.7 351.7 %reduce-scatter.51.cloned.1.call-start = ((), (), s32[]{:S(2)}) async-start(), calls=%async_computation.45 | async-start | bytes 835584
  1664.0 347.3 %reduce-scatter.49.cloned.1.call-start = ((), (), s32[]{:S(2)}) async-start(), calls=%async_computation.44 | async-start | bytes 208896
  1665.5 396.9 %all-reduce.24.cloned.1.call-start = ((), (), s32[]{:S(2)}) async-start(), calls=%async_computation.46 | async-start | bytes 2850816 | tf_op jit(solution)/shard_map/psum | solution.py:415
  (420 other events, 7012.7 us)
Sparse Core Ops, SparseCore 0:
  10.3 42.3 all-gather.16
  55.0 65.5 all-gather.18
  122.8 45.3 all-gather.20
  175.4 26.1 all-gather.40
  203.1 27.2 all-gather.42
  232.5 38.3 all-gather.26
  273.1 52.3 all-gather.28
  327.8 51.9 all-gather.30
  463.7 23.7 reduce-scatter.34
  495.0 23.2 reduce-scatter.32
  565.7 27.4 all-gather.22
  594.5 27.1 all-gather.24
  767.9 28.0 reduce-scatter.22
  798.6 28.1 reduce-scatter.20
  869.5 27.4 all-gather.32
  898.4 27.1 all-gather.34
  1071.7 28.2 reduce-scatter.26
  1102.3 28.3 reduce-scatter.24
  1173.6 27.4 all-gather.36
  1202.5 27.2 all-gather.38
  1369.2 28.1 reduce-scatter.30
  1403.1 28.1 reduce-scatter.28
  1449.9 60.1 reduce-scatter.38
  1513.6 58.4 reduce-scatter.46
  1576.5 74.5 reduce-scatter.42
  1654.8 74.5 reduce-scatter.40
  1733.6 67.0 reduce-scatter.36
  1805.2 88.9 reduce-scatter.44
  1898.3 56.0 reduce-scatter.50
  1958.7 52.5 reduce-scatter.48
  2014.2 48.2 all-reduce.23
where the time goes:
time: 2090 us; the launch traced here: 2080 us
  waiting for transfers between devices  747 us (36%)
  local copies, waits for them, and re-layouts  471 us (23%)
  matrix products  397 us (19%)
  other arithmetic  321 us (15%)
  starting transfers between devices  63.4 us (3%)
  blocking collectives  51.6 us (2%)
  between operations  28.5 us (1%)
    unnamed x33, waiting for transfers between devices  119 us
    reduce_scatter x1, waiting for transfers between devices, body(): lax.psum_scatter(grad_ada.astype(jnp.bfloat16), 'wide', scatter_dimension...  93.5 us
    dot_general x4, matrix products, body(): jnp.einsum('td,fd->tf', grad_branch_b, down_full, preferred_element_type=...  72.1 us
    reduce_scatter x1, waiting for transfers between devices, body(): lax.psum_scatter(qkv_sum.astype(jnp.bfloat16), 'wide', scatter_dimension=...  71.3 us
    convert_element_type x12, local copies, waits for them, and re-layouts, body(): from_subgrids(grad_keys, GRID).astype(jnp.bfloat16)  69.5 us
    convert_element_type x12, local copies, waits for them, and re-layouts, body(): from_subgrids(grad_values, GRID).astype(jnp.bfloat16)  67.5 us
    all_gather x1, waiting for transfers between devices, body(): lax.all_gather(ada_weight, 'wide', axis=0, tiled=True)  65.9 us
    reduce_scatter x1, waiting for transfers between devices, body(): lax.psum_scatter(up_sum.astype(jnp.bfloat16), 'wide', scatter_dimension=0...  63.8 us
  transfers between devices with their start and end apart: 63, of which 47 were waited for; matrix products, arithmetic and copies ran while one was open for 30% of the time, Pallas kernels for 0%

commit v1 on v0

v1 whole, which is shorter than its diff:
```python
from functools import partial
import math

import jax
import jax.numpy as jnp
import numpy as np
from jax import lax
from jax.experimental import pallas as pl
from jax.experimental.pallas import tpu as pltpu
from jax.sharding import PartitionSpec as P

HEAD_DIM = 64
GRID = 32
LATENT = 256
HALF = 2 * LATENT
PARTS = 2
ROWS = 128
GROUP = 256
VMEM_BYTES = 67000000

norm_eps = 1e-06
bf16 = jnp.bfloat16
f32 = jnp.float32


def dot(a, b):
    return lax.dot_general(a, b, (((1,), (0,)), ((), ())), preferred_element_type=f32)


def dot_nt(a, b):
    return lax.dot_general(a, b, (((1,), (1,)), ((), ())), preferred_element_type=f32)


def dot_tn(a, b):
    return lax.dot_general(a, b, (((0,), (0,)), ((), ())), preferred_element_type=f32)


def norm_parts(values):
    centred = values - jnp.mean(values, axis=-1, keepdims=True)
    inverse = lax.rsqrt(jnp.mean(centred * centred, axis=-1, keepdims=True) + norm_eps)
    return centred * inverse, inverse


def norm_back(grad_normed, normed, inverse):
    return inverse * (
        grad_normed
        - jnp.mean(grad_normed, axis=-1, keepdims=True)
        - normed * jnp.mean(grad_normed * normed, axis=-1, keepdims=True)
    )


def edges(narrow_grid):
    place = lax.broadcasted_iota(jnp.int32, (64, 128), 0)
    place = jnp.where(narrow_grid, place % 8, place % 16)
    return place == 0, place == jnp.where(narrow_grid, 7, 15)


def neighbours(blocks, narrow_grid, ends):
    first, last = ends
    gap = jnp.zeros((16, 128), blocks[0].dtype)

    def earlier(v):
        padded = jnp.concatenate([gap, v], 0)
        return jnp.where(narrow_grid, padded[8:72], padded[:64])

    def later(v):
        padded = jnp.concatenate([v, gap], 0)
        return jnp.where(narrow_grid, padded[8:72], padded[16:80])

    columns, moved = [], []
    for row_parity in range(2):
        even, odd = blocks[2 * row_parity], blocks[2 * row_parity + 1]
        before = jnp.where(first, 0.0, pltpu.roll(odd, 1, 0))
        after = jnp.where(last, 0.0, pltpu.roll(even, 63, 0))
        shift = later if row_parity == 0 else earlier
        b, e, o, a = [shift(v) for v in (before, even, odd, after)]
        columns.append(((before, even, odd), (even, odd, after)))
        moved.append(((b, e, o), (e, o, a)))
    found = []
    for row_parity in range(2):
        for parity in range(2):
            same, other, far = columns[row_parity][parity], columns[1 - row_parity][parity], moved[1 - row_parity][parity]
            found.append((*far, *same, *other) if row_parity == 0 else (*other, *same, *far))
    return found


def weighted(found, taps):
    total = found[0] * taps[0]
    for tap in range(1, 9):
        total = total + found[tap] * taps[tap]
    return total


def phase_rows(latent):
    return [slice(latent * LATENT + 64 * phase, latent * LATENT + 64 * phase + 64) for phase in range(4)]


def add_taps(store, which, lanes, found, grads):
    for tap in range(9):
        total = found[0][tap] * grads[0]
        for phase in range(1, 4):
            total = total + found[phase][tap] * grads[phase]
        store[which, 8 * tap : 8 * tap + 8, lanes] += jnp.sum(total.reshape(8, 8, total.shape[1]), axis=0)


def head_mask():
    rows = lax.broadcasted_iota(jnp.int32, (GROUP, GROUP), 0) // HEAD_DIM
    cols = lax.broadcasted_iota(jnp.int32, (GROUP, GROUP), 1) // HEAD_DIM
    return jnp.where(rows == cols, 1.0, 0.0).astype(bf16)


def spread_heads(values, mask):
    return jnp.concatenate([values] * 4, 0) * mask


def head_max(values):
    low = lax.broadcasted_iota(jnp.int32, values.shape, 1) < HEAD_DIM
    lower = jnp.max(jnp.where(low, values, -jnp.inf), axis=-1, keepdims=True)
    upper = jnp.max(jnp.where(low, -jnp.inf, values), axis=-1, keepdims=True)
    return jnp.where(low, lower, upper)


def row_block(step, size, start=0):
    return pl.ds(pl.multiple_of(start + step * size, size), size)


def arrange(base, meta, tok, far_tok, places, out):
    @pl.when(meta[pl.program_id(0) + base] > 0)
    def _():
        @pl.loop(0, HALF // ROWS)
        def _(step):
            rows = row_block(step, ROWS)
            source = lax.broadcasted_iota(jnp.int32, (ROWS, 3 * LATENT), 1)
            hot = jnp.where(places[0, rows, :] == source, 1.0, 0.0).astype(bf16)
            values = dot(hot[:, :HALF], tok[0]) + dot(hot[:, HALF:], far_tok[0])
            out[0, rows, :] = values.astype(bf16)


def put_back(result, spots, own, far):
    for step in range(3 * LATENT // ROWS):
        target = lax.broadcasted_iota(jnp.int32, (ROWS, HALF), 0) + step * ROWS
        hot = jnp.where(spots[0] == target, 1.0, 0.0).astype(bf16)
        values = dot(hot, result[0]).astype(bf16)
        if step * ROWS < HALF:
            own[0, step * ROWS : (step + 1) * ROWS, :] = values
        else:
            far[0, step * ROWS - HALF : (step + 1) * ROWS - HALF, :] = values


def place_back(meta, result, spots, own, far):
    @pl.when(meta[3] > 0)
    def _():
        put_back(result, spots, own, far)


def mix_tokens(base, taken, meta, *refs):
    if taken:
        x, other, mod, taps, x_o, mix_o, hidden = refs
    else:
        x, mod, taps, x_o, mix_o, hidden = refs
    unit = pl.program_id(0) + base

    @pl.when(meta[unit] > 0)
    def _():
        for latent in range(2):
            shift, scale = mod[0, latent, 0:1, :], 1.0 + mod[0, latent, 1:2, :]

            @pl.loop(0, LATENT // ROWS)
            def _(step):
                rows = row_block(step, ROWS, latent * LATENT)
                values = x[0, rows, :].astype(f32)
                if taken:
                    values = jnp.where(meta[0] > 0, values, other[0, rows, :].astype(f32))
                x_o[0, rows, :] = values.astype(bf16)
                normed, _ = norm_parts(values)
                hidden[rows, :] = (normed * scale + shift).astype(bf16).astype(f32)

        narrow_grid = meta[meta.shape[0] // 2 + unit] == 0
        ends = edges(narrow_grid)

        @pl.loop(0, x.shape[2] // 128)
        def _(step):
            lanes = row_block(step, 128)
            weights = [taps[0, tap : tap + 1, lanes] for tap in range(9)]
            for latent in range(2):
                found = neighbours([hidden[r, lanes] for r in phase_rows(latent)], narrow_grid, ends)
                for rows, near in zip(phase_rows(latent), found):
                    mix_o[0, rows, lanes] = weighted(near, weights).astype(bf16)


def attend(base, meta, x, mix, mod, weights_p, weights_q, qkv_o, prob_o, att_o, branch_o, mid_o, ffn_o):
    unit = pl.program_id(0) + base
    width = x.shape[2]
    groups = width // GROUP

    @pl.when(meta[unit] > 0)
    def _():
        @pl.loop(0, weights_p.shape[1] // 256)
        def _(step):
            lanes = row_block(step, 256)
            qkv_o[0, :, lanes] = dot(mix[0], weights_p[:, lanes]).astype(bf16)

        qkv_o[0, :, 3 * width - GROUP :] = dot(mix[0], weights_q[:, :GROUP]).astype(bf16)

        mask = head_mask()

        @pl.loop(0, HALF // 128)
        def _(step):
            chains = []
            for block in range(2):
                rows = row_block(step * 2 + block, 64)
                for group in range(groups):
                    at = GROUP * group
                    keys = spread_heads(qkv_o[0, rows, width + at : width + at + GROUP], mask)
                    chains.append((rows, group, dot_nt(qkv_o[0, rows, at : at + GROUP], keys) * 0.125))
            raised = [
                jnp.concatenate([jnp.exp(s[:, c : c + 128] - head_max(s[:, c : c + 128])) for c in (0, 128)], 1)
                for _, _, s in chains
            ]
            totals = [dot(e.astype(bf16), mask) for e in raised]
            for (rows, group, _), e, total in zip(chains, raised, totals):
                probs = (e / total).astype(bf16)
                at = GROUP * group
                values = spread_heads(qkv_o[0, rows, 2 * width + at : 2 * width + at + GROUP], mask)
                prob_o[0, rows, at : at + GROUP] = probs
                att_o[0, rows, at : at + GROUP] = dot(probs, values).astype(bf16)

        for latent in range(2):
            gate_a = mod[0, latent, 2:3, :]
            shift, scale = mod[0, latent, 3:4, :], 1.0 + mod[0, latent, 4:5, :]

            @pl.loop(0, LATENT // ROWS)
            def _(step):
                rows = row_block(step, ROWS, latent * LATENT)
                branch = dot(att_o[0, rows, :], weights_q[:, GROUP:])
                branch_o[0, rows, :] = branch.astype(bf16)
                middle = x[0, rows, :].astype(f32) + gate_a * branch
                mid_o[0, rows, :] = middle
                normed, _ = norm_parts(middle)
                ffn_o[0, rows, :] = (normed * scale + shift).astype(bf16)


def feed_forward(part, shard, taken, meta, *refs):
    if part == 0:
        if taken:
            cot, other, mod, ffn, up_w, down_w, taps, *refs = refs
        else:
            cot, mod, ffn, up_w, down_w, taps, *refs = refs
        gbb_o, bb_o, gf_o, up_o, down_o, dtap_o, *refs = refs
        gbb = gbb_o
    else:
        gbb, ffn, up_w, down_w, taps, bb_i, gf_i, mid, mod, spots, down_i, *refs = refs
        gf_o, y_o, own_o, far_o, grad_o, dtap_o, bb_o, *refs = refs
    ffn_t, gbb_t, acc_up, acc_down, *slots = refs
    unit = pl.program_id(0)
    width = ffn.shape[2]
    columns = taps.shape[2]
    items = columns // 256

    @pl.when(unit == 0)
    def _():
        acc_up[...] = jnp.zeros_like(acc_up)
        acc_down[...] = jnp.zeros_like(acc_down)
        dtap_o[...] = jnp.zeros_like(dtap_o)

    @pl.when(meta[unit] > 0)
    def _():
        if part == 0:
            for latent in range(2):
                gate, weight = mod[0, latent, 5:6, :], mod[0, latent, 6:7, :]

                @pl.loop(0, LATENT // 64)
                def _(step):
                    rows = row_block(step, 64, latent * LATENT)
                    grads = cot[0, rows, :].astype(f32)
                    if taken:
                        from_other = jnp.logical_and(unit == 2, meta[0] == 0)
                        grads = jnp.where(from_other, other[0, rows, :].astype(f32), grads)
                    gbb_o[0, rows, :] = (gate * (grads * weight)).astype(bf16)

        ffn_t[...] = ffn[0].T
        gbb_t[...] = gbb[0].T
        layout = meta[meta.shape[0] // 2 + unit]
        which = jnp.where(layout == 2, 1, 0)
        narrow_grid = layout == 0
        ends = edges(narrow_grid)
        uses = [slots[i::2] for i in range(2)]
        uses[1][2][...] = jnp.zeros_like(uses[1][2])
        uses[1][3][...] = jnp.zeros_like(uses[1][3])
        root = math.sqrt(2.0 / math.pi)

        @pl.loop(0, HALF // 128)
        def _(step):
            rows = row_block(step, 128)
            if part == 0:
                bb_o[0, rows, :] = jnp.zeros((128, width), f32)
                gf_o[0, rows, :] = jnp.zeros((128, width), f32)
            else:
                bb_o[0, rows, :] = bb_i[0, rows, :]
                gf_o[0, rows, :] = gf_i[0, rows, :]

        def project(item, use):
            upward, grad_act = use[0], use[1]
            here = row_block(item, 256)
            upward[...] = dot(ffn[0], up_w[:, here]).astype(bf16).astype(f32)
            grad_act[...] = dot_nt(gbb[0], down_w[here, :])

        def collect(item, use):
            act, grad_up = use[2], use[3]
            here = row_block(item, 256)
            bb_o[0] += dot(act[...], down_w[here, :])
            gf_o[0] += dot_nt(grad_up[...], up_w[:, here])
            acc_up[:, here] += dot(ffn_t[...], grad_up[...])
            acc_down[:, here] += dot(gbb_t[...], act[...])

        def convolve(item, use):
            upward, grad_act, act, grad_up = use
            for side in range(2):
                cols = slice(128 * side, 128 * side + 128)
                lanes = row_block(2 * item + side, 128)
                taken_taps = [taps[0, tap : tap + 1, lanes] for tap in range(9)]
                for latent in range(2):
                    rows = phase_rows(latent)
                    found = neighbours([upward[r, cols] for r in rows], narrow_grid, ends)
                    grads = []
                    for r, near in zip(rows, found):
                        spread = weighted(near, taken_taps)
                        square = spread * spread
                        bent = jnp.tanh(spread * (root + root * 0.044715 * square))
                        half = 0.5 + 0.5 * bent
                        act[r, cols] = (spread * half).astype(bf16)
                        slope = half + (0.5 * spread) * (1.0 - bent * bent) * (
                            root + 3.0 * root * 0.044715 * square
                        )
                        grads.append((grad_act[r, cols] * slope).astype(bf16).astype(f32))
                    add_taps(dtap_o, which, lanes, found, grads)
                    for r, near in zip(rows, neighbours(grads, narrow_grid, ends)):
                        grad_up[r, cols] = weighted(near, taken_taps[::-1]).astype(bf16)

        project(0, uses[0])

        @pl.loop(0, items // 2)
        def _(pair):
            for side in range(2):
                item = 2 * pair + side
                convolve(item, uses[side])
                project(jnp.minimum(item + 1, items - 1), uses[1 - side])
                collect(jnp.maximum(item - 1, 0), uses[1 - side])

        collect(items - 1, uses[1])

        if part == PARTS - 1:
            for latent in range(2):
                gate = mod[0, latent, 5:6, :]

                @pl.loop(0, LATENT // 64)
                def _(step):
                    rows = row_block(step, 64, latent * LATENT)
                    y_o[0, rows, :] = (mid[0, rows, :] + gate * bb_o[0, rows, :]).astype(bf16)

            put_back(y_o, spots, own_o, far_o)

    @pl.when(unit == pl.num_programs(0) - 1)
    def _():
        blocks = PARTS * columns // width
        if part == 0:
            up_o[...] = acc_up[...].astype(bf16)
            store, row_at, col_at = down_o, 0, 0
        else:
            grad_o[:, :columns] = acc_up[...].astype(bf16)
            grad_o[: width // 2, columns:] = down_i[...]
            store, row_at, col_at = grad_o, width // 2, columns
        for start in range(0, columns, width):
            turned_rows = acc_down[:, start : start + width].T
            for piece in range(width // shard):
                owner, block = divmod(start // shard + piece, blocks)
                rows = slice(row_at + owner * shard, row_at + owner * shard + shard)
                lanes = slice(col_at + block * width, col_at + block * width + width)
                store[rows, lanes] = turned_rows[piece * shard : piece * shard + shard].astype(bf16)


def backward_middle(taken, meta, *refs):
    if taken:
        cot, other, *refs = refs
    else:
        cot, *refs = refs
    bb, gf, mid, branch, att, mod, weights_q, grad_mid, grad_att, mod_o, dout_o, gba, acc_out = refs
    unit = pl.program_id(0)
    width = cot.shape[2]

    @pl.when(unit == 0)
    def _():
        acc_out[...] = jnp.zeros_like(acc_out)

    @pl.when(meta[unit] > 0)
    def _():
        mod_o[...] = jnp.zeros_like(mod_o)
        for latent in range(2):
            gate_a, scale_b = mod[0, latent, 2:3, :], 1.0 + mod[0, latent, 4:5, :]
            weight = mod[0, latent, 6:7, :]

            def tally(block, values):
                mod_o[0, latent, block : block + 1, :] += jnp.sum(values, axis=0, keepdims=True)

            @pl.loop(0, 4)
            def _(step):
                rows = row_block(step, 64, latent * LATENT)
                grads = cot[0, rows, :].astype(f32)
                if taken:
                    from_other = jnp.logical_and(unit == 2, meta[0] == 0)
                    grads = jnp.where(from_other, other[0, rows, :].astype(f32), grads)
                grad_out = grads * weight
                tally(3, grad_out * bb[0, rows, :])
                grad_ffn = gf[0, rows, :]
                normed, inverse = norm_parts(mid[0, rows, :])
                tally(1, grad_ffn)
                tally(2, grad_ffn * normed)
                total = grad_out + norm_back(grad_ffn * scale_b, normed, inverse)
                grad_mid[0, rows, :] = total
                tally(0, total * branch[0, rows, :].astype(f32))
                gba[rows, :] = (gate_a * total).astype(bf16)

        @pl.loop(0, width // 256)
        def _(step):
            lanes = row_block(step, 256)
            acc_out[:, lanes] += dot_tn(att[0], gba[:, lanes])
            grad_att[0, :, lanes] = dot_nt(gba[...], weights_q[lanes, GROUP:]).astype(bf16)

    @pl.when(unit == pl.num_programs(0) - 1)
    def _():
        dout_o[...] = acc_out[...].astype(bf16)


def backward_heads(meta, qkv, grad_att, prob, mix, dout, dqkv_o, grad_o, acc):
    unit = pl.program_id(0)
    width = grad_att.shape[2]

    @pl.when(unit == 0)
    def _():
        acc[...] = jnp.zeros_like(acc)

    @pl.when(meta[unit] > 0)
    def _():
        mask = head_mask()
        low = lax.broadcasted_iota(jnp.int32, (64, 128), 1) < HEAD_DIM

        @pl.loop(0, HALF // 128)
        def _(step):
            chains = []
            for block in range(2):
                rows = row_block(2 * step + block, 64)
                for at in range(0, width, GROUP):
                    grads = grad_att[0, rows, at : at + GROUP]
                    values = spread_heads(qkv[0, rows, 2 * width + at : 2 * width + at + GROUP], mask)
                    chains.append((rows, at, grads, dot_nt(grads, values), prob[0, rows, at : at + GROUP]))
            inners = []
            for _, _, _, grad_probs, probs in chains:
                product = probs.astype(f32) * grad_probs
                high = product.astype(bf16)
                rest = (product - high.astype(f32)).astype(bf16)
                inners.append(dot(high, mask) + dot(rest, mask))
            scores = [
                (probs.astype(f32) * (grad_probs - inner)).astype(bf16)
                for (_, _, _, grad_probs, probs), inner in zip(chains, inners)
            ]
            for (rows, at, grads, _, probs), grad_scores in zip(chains, scores):
                query = qkv[0, rows, at : at + GROUP]
                keys = spread_heads(qkv[0, rows, width + at : width + at + GROUP], mask)
                dqkv_o[0, rows, at : at + GROUP] = (dot(grad_scores, keys) * 0.125).astype(bf16)
                for pair in range(2):
                    lanes = slice(128 * pair, 128 * pair + 128)
                    both = dot_tn(grad_scores[:, lanes], query[:, lanes]) * 0.125
                    to = width + at + 128 * pair
                    dqkv_o[0, rows, to : to + 128] = jnp.where(low, both[:64], both[64:]).astype(bf16)
                    both = dot_tn(probs[:, lanes], grads[:, lanes])
                    to = 2 * width + at + 128 * pair
                    dqkv_o[0, rows, to : to + 128] = jnp.where(low, both[:64], both[64:]).astype(bf16)

        @pl.loop(0, 3 * width // 256)
        def _(step):
            lanes = row_block(step, 256)
            acc[:, lanes] += dot_tn(mix[0], dqkv_o[0, :, lanes])

    @pl.when(unit == pl.num_programs(0) - 1)
    def _():
        grad_o[:, : 3 * width] = acc[...].astype(bf16)
        grad_o[:, 3 * width :] = dout[...]


def backward_tokens(
    base, meta, dqkv, x, gm, mod, taps, spots, weights_p, weights_q,
    dx_o, own_o, far_o, mod_o, dtap_o, grad_mix, hidden, grad_hidden,
):
    unit = pl.program_id(0) + base
    width = x.shape[2]

    @pl.when(pl.program_id(0) == 0)
    def _():
        dtap_o[...] = jnp.zeros_like(dtap_o)

    @pl.when(meta[unit] > 0)
    def _():
        mod_o[...] = jnp.zeros_like(mod_o)

        @pl.loop(0, width // 256)
        def _(step):
            rows = row_block(step, 256)
            total = dot_nt(dqkv[0, :, : 3 * width - GROUP], weights_p[rows, :])
            total = total + dot_nt(dqkv[0, :, 3 * width - GROUP :], weights_q[rows, :GROUP])
            grad_mix[:, rows] = total.astype(bf16).astype(f32)

        for latent in range(2):
            shift, scale = mod[0, latent, 0:1, :], 1.0 + mod[0, latent, 1:2, :]

            @pl.loop(0, 4)
            def _(step):
                rows = row_block(step, 64, latent * LATENT)
                normed, _ = norm_parts(x[0, rows, :].astype(f32))
                hidden[rows, :] = (normed * scale + shift).astype(bf16).astype(f32)

        layout = meta[meta.shape[0] // 2 + unit]
        which = jnp.where(layout == 2, 1, 0)
        narrow_grid = layout == 0
        ends = edges(narrow_grid)

        @pl.loop(0, width // 128)
        def _(step):
            lanes = row_block(step, 128)
            weights = [taps[0, tap : tap + 1, lanes] for tap in range(9)]
            for latent in range(2):
                rows = phase_rows(latent)
                grads = [grad_mix[r, lanes] for r in rows]
                found = neighbours([hidden[r, lanes] for r in rows], narrow_grid, ends)
                add_taps(dtap_o, which, lanes, found, grads)
                for r, near in zip(rows, neighbours(grads, narrow_grid, ends)):
                    grad_hidden[r, lanes] = weighted(near, weights[::-1])

        for latent in range(2):
            scale = 1.0 + mod[0, latent, 1:2, :]

            def tally(block, values):
                mod_o[0, latent, block : block + 1, :] += jnp.sum(values, axis=0, keepdims=True)

            @pl.loop(0, 4)
            def _(step):
                rows = row_block(step, 64, latent * LATENT)
                normed, inverse = norm_parts(x[0, rows, :].astype(f32))
                grads = grad_hidden[rows, :]
                tally(0, grads)
                tally(1, grads * normed)
                total = gm[0, rows, :] + norm_back(grads * scale, normed, inverse)
                dx_o[0, rows, :] = total.astype(bf16)

        put_back(dx_o, spots, own_o, far_o)


def source_places(layouts, half):
    p = jnp.arange(HALF, dtype=jnp.int32)
    latent, q = p // LATENT, p % 64
    row_parity, column_parity = (p // 128) % 2, (p // 64) % 2
    square = (2 * (q // 8) + row_parity) * GRID + 16 * latent + 2 * (q % 8) + column_parity
    low_row, wide_col = 2 * (q // 16) + row_parity, 2 * (q % 16) + column_parity
    across = (8 * latent + low_row) * GRID + wide_col
    column = 8 * latent + low_row
    own = (wide_col - 16 * half) * GRID + 16 * half + column
    other = HALF + (wide_col - 16 * (1 - half)) * 16 + column
    downward = jnp.where(wide_col // 16 == half, own, other)
    kind = layouts[:, None]
    return jnp.where(kind == 0, square, jnp.where(kind == 1, across, downward))


def turned(taps):
    return taps.reshape(taps.shape[:-2] + (3, 3, taps.shape[-1])).swapaxes(-3, -2).reshape(taps.shape)


def tap_sum(parts):
    summed = parts.reshape(2, 9, 8, -1).sum(2)
    return summed[0] + turned(summed[1])


def bit_of(index, bit):
    return (index // bit) % 2


def swapped(values, bit):
    count = lax.axis_size("wide")
    return lax.ppermute(values, "wide", [(i, i ^ bit) for i in range(count)])


def bits_of(count):
    return [1 << b for b in range(count.bit_length() - 1)]


def ordered(values, other, bit):
    low = bit_of(lax.axis_index("wide"), bit) == 0
    return jnp.where(low, values, other), jnp.where(low, other, values)


def gathered_rows(values, crosswise):
    count = lax.axis_size("wide")
    far_bits = bits_of(count)[2:]

    def direct(v):
        found = {0: v}
        for mask in range(4, count, 4):
            found[mask] = swapped(v, mask)
        for bit in far_bits:
            found = {
                mask: jnp.stack(ordered(found[mask], found[mask | bit], bit), 0)
                for mask in found if not mask & bit
            }
        return found[0].reshape((count // 4,) + v.shape)

    if crosswise:
        near = direct(jnp.stack(ordered(values, swapped(values, 2), 2)))
    else:
        far = direct(values)
        near = jnp.stack(ordered(far, swapped(far, 2), 2), 1)
    full = jnp.stack(ordered(near, swapped(near, 1), 1), 2)
    return full.reshape(count * values.shape[0], values.shape[1])


def gathered_everywhere(values):
    lane, count = lax.axis_index("narrow"), lax.axis_size("narrow")
    if count == 2:
        other = lax.ppermute(values, "narrow", [(0, 1), (1, 0)])
        values = jnp.where(lane == 0, jnp.stack([values, other]), jnp.stack([other, values]))
    else:
        values = lax.all_gather(values, "narrow", axis=0)
    values = values[None]
    for bit in reversed(bits_of(lax.axis_size("wide"))):
        values = jnp.stack(ordered(values, swapped(values, bit), bit), 1)
        values = values.reshape((-1,) + values.shape[2:])
    return values


def after(value, *earlier):
    return lax.optimization_barrier((value, *earlier))[0]


def narrow_sum(values):
    count = lax.axis_size("narrow")
    if count == 2:
        other = lax.ppermute(values, "narrow", [(0, 1), (1, 0)])
        return values.astype(f32) + other.astype(f32)
    return lax.psum(values, "narrow").astype(f32)


def body(
    tokens, cotangent, conv_attn, qkv_weight, out_weight, up_weight, conv_ffn, down_weight,
    ada_weight, class_table, timesteps, labels, layout, counts,
):
    slots, local_tokens, D = tokens.shape
    owners, narrow = lax.axis_size("wide"), lax.axis_size("narrow")
    owner, lane = lax.axis_index("wide"), lax.axis_index("narrow")
    shard = D // owners
    half = lane % 2
    spread = narrow // 2
    balanced = narrow == 2 and slots == 4
    units = 3 if balanced else slots // spread
    hidden_width = up_weight.shape[1]
    columns = hidden_width // PARTS

    loads = (counts > 0).astype(jnp.int32).reshape(owners, slots)

    def all_units(values):
        values = values.reshape((owners, slots) + values.shape[1:])
        if balanced:
            idle = (loads.sum(1) == 0).reshape((owners,) + (1,) * (values.ndim - 2))
            other = jnp.roll(values[:, 3], owners // 2, axis=0)
            return jnp.stack([values[:, 0], values[:, 1], jnp.where(idle, other, values[:, 2])], 1)
        return values

    def my_units(values):
        values = lax.dynamic_index_in_dim(all_units(values), owner, 0, keepdims=False)
        if balanced:
            return values
        values = values.reshape((units, spread) + values.shape[1:])
        return lax.dynamic_index_in_dim(values, lane // 2, 1, keepdims=False)

    def latent_rows(values):
        values = all_units(values)
        if balanced:
            return values.reshape(owners, units, 2, 2).transpose(0, 2, 1, 3).reshape(-1)
        return values.reshape(owners, units, spread, 2, 2).transpose(0, 2, 3, 1, 4).reshape(-1)

    count_float = counts.astype(f32)
    scales = count_float * float(counts.shape[0]) / jnp.sum(count_float)
    my_layout, my_scale = my_units(layout), my_units(scales)
    active = my_units(counts) > 0
    meta = jnp.concatenate([active.astype(jnp.int32), my_layout])
    places = source_places(my_layout, half)

    half_width = D // 2
    my_columns = owner * shard + jnp.arange(shard, dtype=jnp.int32)
    freqs = jnp.exp(-math.log(10000.0) * (my_columns % half_width).astype(f32) / half_width)
    angles = latent_rows(timesteps)[:, None].astype(f32) * freqs
    label_hot = (latent_rows(labels)[:, None] == jnp.arange(class_table.shape[0], dtype=jnp.int32)).astype(bf16)
    embed = jnp.where(my_columns < half_width, jnp.cos(angles), jnp.sin(angles)) + dot(label_hot, class_table)
    activ, silu_back = jax.vjp(jax.nn.silu, embed)
    act_low = activ.astype(bf16)
    mine = lax.dynamic_index_in_dim(act_low.reshape(owners, narrow, units * 2, shard), lane, 1, keepdims=False)
    partial_mod = dot(mine.reshape(-1, shard), ada_weight).astype(bf16).reshape(owners, units * 2, -1)
    both_taps = jnp.concatenate([conv_attn, conv_ffn], 1).reshape(-1)
    tap_size = both_taps.shape[0]
    tap_lanes = -(-tap_size // (units * 2 * 128)) * 128
    both_taps = jnp.pad(both_taps, (0, units * 2 * tap_lanes - tap_size)).reshape(1, units * 2, tap_lanes)
    sent = jnp.concatenate([partial_mod, jnp.broadcast_to(both_taps, (owners, units * 2, tap_lanes))], 2)
    arrived = lax.all_to_all(sent, "wide", 0, 0, tiled=True)
    modulation = jnp.sum(arrived[:, :, : 6 * D].astype(f32), axis=0).reshape(units, 2, 6, D)
    both_taps = arrived[:, :, 6 * D :].reshape(owners, -1)[:, :tap_size].reshape(owners, 9, -1).astype(f32)
    conv_one = both_taps[:, :, :shard].swapaxes(0, 1).reshape(9, D)
    conv_two = both_taps[:, :, shard:].swapaxes(0, 1).reshape(9, hidden_width)
    weight_row = jnp.broadcast_to(my_scale[:, None, None, None], (units, 2, 1, D))
    mod = jnp.concatenate([modulation, weight_row], 2)

    split = 3 * D - GROUP
    weights_p = gathered_rows(qkv_weight[:, :split], False)
    weights_q = gathered_rows(jnp.concatenate([qkv_weight[:, split:], out_weight], 1), True)
    up_full = lax.all_gather(up_weight, "wide", axis=0, tiled=True)
    down_full = lax.all_gather(down_weight, "wide", axis=0, tiled=True)

    def unit_taps(taps):
        return jnp.where((my_layout == 2)[:, None, None], turned(taps), taps)

    taps_one, taps_two = unit_taps(conv_one), unit_taps(conv_two)

    params = pltpu.CompilerParams(vmem_limit_bytes=VMEM_BYTES, dimension_semantics=("arbitrary",))
    any_space = pl.BlockSpec(memory_space=pl.ANY)

    def per_unit(*shape, base=0):
        return pl.BlockSpec((1,) + shape, lambda i, meta: (i + base,) + (0,) * len(shape))

    def whole(*shape):
        return pl.BlockSpec(shape, lambda i, meta: (0,) * len(shape), pipeline_mode=pl.Buffered(1))

    def struct(*shape, kind=bf16):
        return jax.ShapeDtypeStruct(shape, kind)

    def call(kernel, name, count, flags, ins, in_specs, outs, out_specs, scratch=(), flops=0, before=()):
        aliases = {1 + len(ins) + i: i for i in range(len(before))}
        extra = len(before)

        def run(meta, *refs):
            kept = refs[: len(ins)] + refs[len(ins) + extra :]
            kernel(meta, *kept)

        return pl.pallas_call(
            run,
            grid_spec=pltpu.PrefetchScalarGridSpec(
                num_scalar_prefetch=1, grid=(count,), in_specs=list(in_specs) + [any_space] * extra,
                out_specs=out_specs, scratch_shapes=list(scratch),
            ),
            out_shape=outs,
            input_output_aliases=aliases,
            compiler_params=params,
            cost_estimate=pl.CostEstimate(flops=int(flops * count), bytes_accessed=int(8e6 * count), transcendentals=0),
            name=name,
        )(flags, *ins, *before)

    tokens_shape = (HALF, D)

    def arranged(base, count, tok, far, far_base, where, flags):
        return call(
            partial(arrange, base), "arrange", count, flags, [tok, far, where[:, :, None]],
            [per_unit(*tokens_shape, base=base), per_unit(LATENT, D, base=far_base), per_unit(HALF, 1, base=base)],
            struct(count, *tokens_shape), per_unit(*tokens_shape), flops=2e9,
        )

    if balanced:
        own_layout = lax.dynamic_slice_in_dim(layout, owner * slots, slots)
        own_active = lax.dynamic_slice_in_dim(counts, owner * slots, slots) > 0
        own_places = source_places(own_layout, half)
        own_flags = jnp.concatenate([own_active.astype(jnp.int32), own_layout])
        swap = [(0, 1), (1, 0)]
        partner = [(i, (i + owners // 2) % owners) for i in range(owners)]

        def for_other_half(first, count):
            parts = [v.reshape(slots, 16, GRID, D)[first : first + count] for v in (tokens, cotangent)]
            parts = [lax.dynamic_slice_in_dim(v, 16 * (1 - half), 16, axis=2) for v in parts]
            return lax.ppermute(jnp.concatenate(parts, 0).reshape(-1, LATENT, D), "narrow", swap)

        far_last, far_first = for_other_half(3, 1), for_other_half(0, 3)
        own_tok, own_cot = [v.reshape(slots, HALF, D) for v in (tokens, cotangent)]
        x_last = arranged(3, 1, own_tok, far_last, 0, own_places, own_flags)
        x_other = lax.ppermute(x_last, "wide", partner)
        cot_last = arranged(3, 1, own_cot, far_last, 1, own_places, own_flags)
        cot_other = lax.ppermute(cot_last, "wide", partner)
        x_own = arranged(0, 3, own_tok, far_first, 0, own_places, own_flags)
        cot_own = arranged(0, 3, own_cot, far_first, 3, own_places, own_flags)
        cots, cot_specs = [cot_own, cot_other], [per_unit(*tokens_shape), whole(1, *tokens_shape)]
    else:

        def to_units(values):
            full = lax.all_gather(values, "narrow", axis=1, tiled=True)
            full = full.reshape(units, spread, 2, 16, GRID, D)
            full = lax.dynamic_index_in_dim(full, lane // 2, 1, keepdims=False)
            here = lax.dynamic_index_in_dim(full, half, 1, keepdims=False)
            far = lax.dynamic_index_in_dim(full, 1 - half, 1, keepdims=False)
            far = lax.dynamic_slice_in_dim(far, 16 * half, 16, axis=2)
            return arranged(0, units, here.reshape(units, HALF, D), far.reshape(units, LATENT, D), 0, places, meta)

        x_own = to_units(tokens)
        cot_own = to_units(cotangent)
        cots, cot_specs = [cot_own], [per_unit(*tokens_shape)]

    unit_values = struct(units, *tokens_shape)
    unit_floats = struct(units, *tokens_shape, kind=f32)

    def mix_call(base, count, taken, before):
        spec = per_unit(*tokens_shape, base=base)
        ins, specs = [x_own], [spec]
        if taken:
            ins, specs = ins + [x_other], specs + [whole(1, *tokens_shape)]
        return call(
            partial(mix_tokens, base, taken), "mix_tokens", count, meta, ins + [mod, taps_one],
            specs + [per_unit(2, 7, D, base=base), per_unit(9, D, base=base)],
            [unit_values, unit_values], [spec, spec], [pltpu.VMEM(tokens_shape, f32)], 3e9, before,
        )

    def attend_call(base, count, before):
        spec = per_unit(*tokens_shape, base=base)
        return call(
            partial(attend, base), "attend", count, meta, [x, mixed, mod, weights_p, weights_q],
            [spec, spec, per_unit(2, 7, D, base=base), whole(D, split), whole(D, GROUP + D)],
            [struct(units, HALF, 3 * D), unit_values, unit_values, unit_values, unit_floats, unit_values],
            [per_unit(HALF, 3 * D, base=base)] + [spec] * 5, (), 8e9, before,
        )

    if balanced:
        x, mixed = mix_call(0, 2, False, ())
        front = attend_call(0, 2, ())
        x, mixed = mix_call(2, 1, True, (x, mixed))
        front = attend_call(2, 1, front)
    else:
        x, mixed = mix_call(0, units, False, ())
        front = attend_call(0, units, ())
    projected, probs, attended, branch, middle, ffn_in = front

    slot_pair = [pltpu.VMEM((HALF, 256), kind) for kind in (f32, f32, f32, f32, bf16, bf16, bf16, bf16)]
    work = [pltpu.VMEM((D, HALF), bf16), pltpu.VMEM((D, HALF), bf16)]
    work += [pltpu.VMEM((D, columns), f32), pltpu.VMEM((D, columns), f32)]
    unit_spec = per_unit(*tokens_shape)
    tap_grad, tap_spec = struct(2, 72, columns, kind=f32), whole(2, 72, columns)
    spots = places[:, None, :]

    def of_part(part):
        specs = [
            pl.BlockSpec((D, columns), lambda i, meta: (0, part), pipeline_mode=pl.Buffered(1)),
            pl.BlockSpec((columns, D), lambda i, meta: (part, 0), pipeline_mode=pl.Buffered(1)),
            pl.BlockSpec((1, 9, columns), lambda i, meta: (i, 0, part)),
        ]
        return [up_full, down_full, taps_two], specs

    ins, specs = of_part(0)
    gbb, branch_b, grad_ffn, up_grad, down_grad, ffn_taps_0 = call(
        partial(feed_forward, 0, shard, balanced), "feed_forward", units, meta, cots + [mod, ffn_in] + ins,
        cot_specs + [per_unit(2, 7, D), unit_spec] + specs,
        [unit_values, unit_floats, unit_floats, struct(D, columns), struct(D // 2, hidden_width), tap_grad],
        [unit_spec, unit_spec, unit_spec, whole(D, columns), whole(D // 2, hidden_width), tap_spec],
        work + slot_pair, 16e9,
    )

    def owner_sum(values):
        return lax.psum_scatter(values, "wide", scatter_dimension=0, tiled=True)

    sums_up = owner_sum(up_grad)
    ins, specs = of_part(1)
    grad_ffn, y_units, y_own, y_far, ffn_grad, ffn_taps_1, branch_b = call(
        partial(feed_forward, 1, shard, balanced), "feed_forward", units, meta,
        [gbb, ffn_in] + ins + [branch_b, grad_ffn, middle, mod, spots, down_grad],
        [unit_spec, unit_spec] + specs
        + [unit_spec, unit_spec, unit_spec, per_unit(2, 7, D), per_unit(1, HALF), whole(D // 2, hidden_width)],
        [unit_floats, unit_values, unit_values, struct(units, LATENT, D), struct(D, columns + hidden_width),
         tap_grad, unit_floats],
        [unit_spec, unit_spec, unit_spec, per_unit(LATENT, D), whole(D, columns + hidden_width), tap_spec, unit_spec],
        work + slot_pair, 17e9,
    )
    grad_ffn, sums_up = lax.optimization_barrier((grad_ffn, sums_up))
    sums_ffn = owner_sum(ffn_grad)

    grad_mid, grad_att, mod_late, out_grad = call(
        partial(backward_middle, balanced), "backward_middle", units, meta,
        cots + [branch_b, grad_ffn, middle, branch, attended, mod, weights_q],
        cot_specs + [unit_spec] * 5 + [per_unit(2, 7, D), whole(D, GROUP + D)],
        [unit_floats, unit_values, struct(units, 2, 4, D, kind=f32), struct(D, D)],
        [unit_spec, unit_spec, per_unit(2, 4, D), whole(D, D)],
        [pltpu.VMEM(tokens_shape, bf16), pltpu.VMEM((D, D), f32)], 4e9,
    )
    head_grads, attn_grad = call(
        backward_heads, "backward_heads", units, meta, [projected, grad_att, probs, mixed, out_grad],
        [per_unit(HALF, 3 * D), unit_spec, unit_spec, unit_spec, whole(D, D)],
        [struct(units, HALF, 3 * D), struct(D, 4 * D)], [per_unit(HALF, 3 * D), whole(D, 4 * D)],
        [pltpu.VMEM((D, 3 * D), f32)], 12e9,
    )

    def tokens_call(base, count, before):
        spec = per_unit(*tokens_shape, base=base)
        return call(
            partial(backward_tokens, base), "backward_tokens", count, meta,
            [head_grads, x, grad_mid, mod, taps_one, spots, weights_p, weights_q],
            [per_unit(HALF, 3 * D, base=base), spec, spec, per_unit(2, 7, D, base=base), per_unit(9, D, base=base), per_unit(1, HALF, base=base),
             whole(D, split), whole(D, GROUP + D)],
            [unit_values, unit_values, struct(units, LATENT, D), struct(units, 2, 2, D, kind=f32),
             struct(2, 72, D, kind=f32)],
            [spec, spec, per_unit(LATENT, D, base=base), per_unit(2, 2, D, base=base), whole(2, 72, D)],
            [pltpu.VMEM(tokens_shape, f32)] * 3, 6e9, before,
        )

    def finished(pieces):
        pairs = []
        for own, far in pieces:
            count = own.shape[0]
            far = lax.ppermute(far, "narrow", swap).reshape(count, 16, 16, D)
            empty = jnp.zeros_like(far)
            side = jnp.where(half == 0, jnp.concatenate([empty, far], 2), jnp.concatenate([far, empty], 2))
            pairs.append(own.reshape(count, 16, GRID, D) + side)
        total = jnp.concatenate(pairs, 0)
        return jnp.where(own_active[:, None, None, None], total, 0.0).reshape(slots, local_tokens, D)

    def returned(values, later):
        back = lax.ppermute(values, "wide", partner)
        return call(
            place_back, "place_back", 1, after(own_flags, later), [back, own_places[3:, None, :]],
            [unit_spec, per_unit(1, HALF)], [struct(1, *tokens_shape), struct(1, LATENT, D)],
            [unit_spec, per_unit(LATENT, D)], (), 2e9,
        )

    def rows_back(own, far):
        own = jnp.where(active[:, None, None], own, 0.0).reshape(units, 1, 16, GRID, D)
        far = jnp.where(active[:, None, None], far, 0.0).reshape(units, 1, 16, 16, D)
        full = lax.dynamic_update_slice_in_dim(jnp.zeros((units, 2, 16, GRID, D), bf16), own, half, 1)
        other = lax.dynamic_update_slice_in_dim(jnp.zeros((units, 1, 16, GRID, D), bf16), far, 16 * half, 3)
        full = lax.dynamic_update_slice_in_dim(full, other, 1 - half, 1).reshape(units, 1, 2 * HALF, D)
        full = lax.dynamic_update_slice_in_dim(jnp.zeros((units, spread, 2 * HALF, D), bf16), full, lane // 2, 1)
        return lax.psum_scatter(full.reshape(slots, 2 * HALF, D), "narrow", scatter_dimension=1, tiled=True)

    if balanced:
        dx_units, dx_own, dx_far, mod_early, taps_a = tokens_call(2, 1, ())
        y_back = returned(y_units[2:], dx_units)
        dx_last = dx_units[2:]
        head_grads, sums_ffn = lax.optimization_barrier((head_grads, sums_ffn))
        attn_sums = owner_sum(after(attn_grad, sums_ffn))
        _, dx_own, dx_far, mod_early, taps_b = tokens_call(0, 2, (dx_units, dx_own, dx_far, mod_early))
        x_back = returned(dx_last, mod_early)
        work_y = finished([(y_own, y_far), y_back])
        work_x = finished([(dx_own, dx_far), x_back])
        conv_one_grad = tap_sum(taps_a) + tap_sum(taps_b)
    else:
        work_y = rows_back(y_own, y_far)
        dx_units, dx_own, dx_far, mod_early, taps_a = tokens_call(0, units, ())
        attn_sums = owner_sum(after(attn_grad, sums_ffn))
        work_x = rows_back(dx_own, dx_far)
        conv_one_grad = tap_sum(taps_a)

    attn_final = narrow_sum(attn_sums)
    final_qkv, final_out = attn_final[:, : 3 * D], attn_final[:, 3 * D :]
    ffn_final = narrow_sum(sums_ffn)
    final_up = jnp.concatenate([narrow_sum(sums_up), ffn_final[:, :columns]], 1)
    final_down = ffn_final[:, columns:].reshape(shard, -1, D).swapaxes(0, 1).reshape(-1, D)
    conv_two_grad = jnp.concatenate([tap_sum(ffn_taps_0), tap_sum(ffn_taps_1)], 1)
    conv_grads = jnp.concatenate(
        [conv_one_grad.reshape(9, owners, shard), conv_two_grad.reshape(9, owners, -1)], 2
    ).swapaxes(0, 1)
    conv_grads = jnp.broadcast_to(conv_grads[:, None], (owners, narrow) + conv_grads.shape[1:])
    conv_grads = conv_grads.reshape((owners * narrow,) + conv_grads.shape[2:])
    conv_sums = jnp.sum(lax.all_to_all(conv_grads, ("wide", "narrow"), 0, 0, tiled=True), axis=0)

    mod_grads = jnp.concatenate([mod_early, mod_late], 2)
    mod_grads = jnp.where(active[:, None, None, None], mod_grads, 0.0).astype(bf16)
    mod_all = gathered_everywhere(mod_grads.reshape(units * 2, 6 * D)).reshape(-1, 6 * D)
    grad_ada = dot_tn(act_low, mod_all)
    grad_embed = silu_back(dot_nt(mod_all, ada_weight))[0]
    grad_table = dot_tn(label_hot, grad_embed.astype(bf16))
    return (
        work_y, work_x, conv_sums[:, :shard], final_qkv, final_out, final_up,
        conv_sums[:, shard:], final_down, grad_ada, grad_table,
    )


def solution(mesh):
    rows = P("wide", None)
    columns = P(None, "wide")
    canvases = P("wide", "narrow", None)
    return jax.shard_map(
        body,
        mesh=mesh,
        in_specs=(canvases, canvases, columns, rows, rows, rows, columns, rows, rows, columns, P(), P(), P(), P()),
        out_specs=(canvases, canvases, columns, rows, rows, rows, columns, rows, rows, columns),
        check_vma=False,
    )
```

time: 2090 us -> 613 us (0.29)
  waiting for transfers between devices: 747 us -> 132 us
  local copies, waits for them, and re-layouts: 471 us -> 45.9 us
  matrix products: 397 us -> 4.28 us
  Pallas kernels: 0 us -> 308 us
  other arithmetic: 321 us -> 66.5 us
  blocking collectives: 51.6 us -> 0 us
  starting transfers between devices: 63.4 us -> 34.3 us
    dot_general x81 -> x4, matrix products: 397 us -> 4.28 us  [the longest x2 2.92 us: dot_tn(): lax.dot_general(a, b, (((0,), (0,)), ((), ())), preferred_element_type=f32)]
    pallas_call x0 -> x16, Pallas kernels: none -> 308 us  [call(): pl.pallas_call(run, grid_spec=pltpu.PrefetchScalarGridSpec(num_scalar_pre...]
    all_gather x14 -> x2, waiting for transfers between devices: 275 us -> 0.02 us  [the longest x1 0.02 us: body(): down_full = lax.all_gather(down_weight, 'wide', axis=0, tiled=True)]
    reduce_scatter x14 -> x3, waiting for transfers between devices: 254 us -> 0.02 us  [owner_sum(): return lax.psum_scatter(values, 'wide', scatter_dimension=0, tiled=True)]
    convert_element_type x38 -> x4, other arithmetic: 161 us -> 0.1 us  [the longest x1 0.08 us: body(): jnp.where(active[:, None, None, None], mod_grads, 0.0).astype(bf16)]
    convert_element_type x32 -> x4, local copies, waits for them, and re-layouts: 157 us -> 0.57 us  [the longest x2 0.27 us: body(): angles = latent_rows(timesteps)[:, None].astype(f32) * freqs]
    unnamed x33 -> x5, waiting for transfers between devices: 119 us -> 1.43 us
    transpose x28 -> x13, local copies, waits for them, and re-layouts: 86.7 us -> 4.61 us  [the longest x6 3.22 us: turned(): taps.reshape(taps.shape[:-2] + (3, 3, taps.shape[-1])).swapaxes(-3, -2)]
  transfers between devices with their start and end apart: 63 -> 35, of which waited for: 47 -> 13; matrix products, arithmetic and copies ran while one was open for 30% -> 18% of each run, Pallas kernels for 0% -> 41%
where the time goes in v1:
time: 613 us; the launch traced here: 606 us
  Pallas kernels  308 us (50%)
  waiting for transfers between devices  132 us (22%)
  other arithmetic  66.5 us (11%)
  local copies, waits for them, and re-layouts  45.9 us (7%)
  starting transfers between devices  34.3 us (6%)
  between operations  15.3 us (2%)
    pallas_call x16, Pallas kernels, call(): pl.pallas_call(run, grid_spec=pltpu.PrefetchScalarGridSpec(num_scalar_pre...  308 us
    ppermute x14, waiting for transfers between devices, swapped(): return lax.ppermute(values, 'wide', [(i, i ^ bit) for i in range(count)])  73.5 us
    ppermute x1, waiting for transfers between devices, body(): x_other = lax.ppermute(x_last, 'wide', partner)  28.7 us
    ppermute x4, waiting for transfers between devices, finished(): far = lax.ppermute(far, 'narrow', swap).reshape(count, 16, 16, D)  23.5 us
    ppermute x14, starting transfers between devices, swapped(): return lax.ppermute(values, 'wide', [(i, i ^ bit) for i in range(count)])  12.7 us
  transfers between devices with their start and end apart: 35, of which 13 were waited for; matrix products, arithmetic and copies ran while one was open for 18% of the time, Pallas kernels for 41%

profile of v1, /device:TPU:0, one launch (start us, length us, event | category | flops | bytes accessed | tf_op | source)
XLA Modules:
  0.0 606.4 jit_solution(6322381090066401137)
XLA Ops:
  8.9 5.1 collective-permute-start.6
  16.3 1.7 collective-permute-start.9
  25.4 5.0 all-to-all-start
  33.2 1.9 copy-done.4
  41.0 2.0 select_select_fusion.refs_2_
  48.3 3.7 collective-permute-start.12
  53.1 2.8 collective-permute-done.5
  58.1 15.1 %collective-permute-done.12 = bf16[2,48,1024]{2,1,0:T(8,128)(2,1)S(1)} collective-permute-done((bf16[2,48,1024]{2,1,0:T(8,128)(2,1)S(1)}, bf16[2,48,1024]{2,1,0:T(8,128)(2,1)S(1)}, u32[]{:S(2)}, u32[]{:S(2)}) %collective-permute-start.12) | collective-permute-done | bytes 196640 | tf_op jit(solution)/shard_map/ppermute | solution.py:587
  74.4 29.0 %collective-permute-done.11 = bf16[2,48,1024]{2,1,0:T(8,128)(2,1)S(1)} collective-permute-done((bf16[2,48,1024]{2,1,0:T(8,128)(2,1)S(1)}, bf16[2,48,1024]{2,1,0:T(8,128)(2,1)S(1)}, u32[]{:S(2)}, u32[]{:S(2)}) %collective-permute-start.11) | collective-permute-done | bytes 196640 | tf_op jit(solution)/shard_map/ppermute | solution.py:587
  104.6 4.4 arrange.5
  109.0 4.5 arrange.7
  126.8 7.4 %arrange.6.refs_0_ = bf16[3,512,768]{2,1,0:T(8,128)(2,1)} custom-call(s32[8]{0:T(128)} %pad_add_fusion.3.meta, bf16[4,512,768]{2,1,0:T(8,128)(2,1)} %refs_0_.7, bf16[6,256,768]{2,1,0:T(8,128)(2,1)} %collective-permute-done.refs_1_, s32[4,512,1]{2,1,0:T(8,128)} %select_select_fusion.refs_2_), custom_call_target="tpu_custom_call" | custom-call | flops 6000000000 | bytes 24000000 | tf_op jit(solution)/shard_map/arrange/pallas_call | solution.py:748
  134.2 7.5 %mix_tokens.2 = (bf16[3,512,768]{2,1,0:T(8,128)(2,1)}, bf16[3,512,768]{2,1,0:T(8,128)(2,1)}) custom-call(s32[6]{0:T(128)} %pad_add_fusion.2.meta, bf16[3,512,768]{2,1,0:T(8,128)(2,1)} %arrange.6.refs_0_, f32[3,2,7,768]{3,2,1,0:T(8,128)} %pad_maximum_fusion.17.refs_1_.refs_2_.refs_8_.refs_7_.refs_3_, f32[3,9,768]{2,1,0:T(8,128)} %broadcast_select_fusion.9.refs_2_.refs_3_.refs_4_), custom_call_target="tpu_custom_call" | custom-call | flops 6000000000 | bytes 16000000 | tf_op jit(solution)/shard_map/mix_tokens/pallas_call | solution.py:748
  141.7 7.4 %arrange.4.refs_0_ = bf16[3,512,768]{2,1,0:T(8,128)(2,1)} custom-call(s32[8]{0:T(128)} %pad_add_fusion.3.meta, bf16[4,512,768]{2,1,0:T(8,128)(2,1)} %refs_0_.5, bf16[6,256,768]{2,1,0:T(8,128)(2,1)} %collective-permute-done.refs_1_, s32[4,512,1]{2,1,0:T(8,128)} %select_select_fusion.refs_2_), custom_call_target="tpu_custom_call" | custom-call | flops 6000000000 | bytes 24000000 | tf_op jit(solution)/shard_map/arrange/pallas_call | solution.py:748
  149.2 2.0 select_bitcast_fusion.1
  151.2 2.0 pad_maximum_fusion
  153.2 24.2 %attend.2 = (bf16[3,512,2304]{2,1,0:T(8,128)(2,1)}, bf16[3,512,768]{2,1,0:T(8,128)(2,1)}, bf16[3,512,768]{2,1,0:T(8,128)(2,1)}, bf16[3,512,768]{2,1,0:T(8,128)(2...) custom-call(s32[6]{0:T(128)} %pad_add_fusion.2.meta, bf16[3,512,768]{2,1,0:T(8,128)(2,1)} %get-tuple-element.65.refs_4_.refs_0_, ...), custom_call_target="tpu_custom_call" | custom-call | flops 16000000000 | bytes 16000000 | tf_op jit(solution)/shard_map/attend/pallas_call | solution.py:748
  177.4 28.7 %collective-permute-done.3.refs_1_ = bf16[1,512,768]{2,1,0:T(8,128)(2,1)} collective-permute-done((bf16[1,512,768]{2,1,0:T(8,128)(2,1)}, bf16[1,512,768]{2,1,0:T(8,128)(2,1)}, u32[]{:S(2)}, u32[]{:S(2)}) %collective-permute-start.3) | collective-permute-done | bytes 786464 | tf_op jit(solution)/shard_map/ppermute | solution.py:786
  206.1 5.5 mix_tokens.3
  211.6 15.3 %attend.3 = (bf16[3,512,2304]{2,1,0:T(8,128)(2,1)}, bf16[3,512,768]{2,1,0:T(8,128)(2,1)}, bf16[3,512,768]{2,1,0:T(8,128)(2,1)}, bf16[3,512,768]{2,1,0:T(8,128)(2...) custom-call(s32[6]{0:T(128)} %pad_add_fusion.2.meta, ...), custom_call_target="tpu_custom_call", output_to_operand_aliasing={{0}: (6, {}), {1}: (7, {}), {2}: (8, {}), {3}: (9, {}), {4}... | custom-call | flops 8000000000 | bytes 8000000 | tf_op jit(solution)/shard_map/attend/pallas_call | solution.py:748
  226.9 60.5 %feed_forward.2 = (bf16[3,512,768]{2,1,0:T(8,128)(2,1)}, f32[3,512,768]{2,1,0:T(8,128)}, f32[3,512,768]{2,1,0:T(8,128)}, bf16[768,1536]{1,0:T(8,128)(2,1)}, bf16...) custom-call(s32[6]{0:T(128)} %pad_add_fusion.2.meta, bf16[3,512,768]{2,1,0:T(8,128)(2,1)} %arrange.4.refs_0_, ...), custom_call_target="tpu_custom_call" | custom-call | flops 48000000000 | bytes 24000000 | tf_op jit(solution)/shard_map/feed_forward/pallas_call | solution.py:748
  287.9 67.4 %feed_forward.3 = (f32[3,512,768]{2,1,0:T(8,128)}, bf16[3,512,768]{2,1,0:T(8,128)(2,1)}, bf16[3,512,768]{2,1,0:T(8,128)(2,1)}, bf16[3,256,768]{2,1,0:T(8,128)(2,...) custom-call(s32[6]{0:T(128)} %pad_add_fusion.2.meta, ...), custom_call_target="tpu_custom_call" | custom-call | flops 51000000512 | bytes 24000000 | tf_op jit(solution)/shard_map/feed_forward/pallas_call | solution.py:748
  357.3 1.9 fusion.37.refs_1_
  376.5 2.1 slice.233
  381.7 5.4 collective-permute-done.14
  387.2 2.2 select_add_fusion.1
  389.3 21.4 %backward_middle.1 = (f32[3,512,768]{2,1,0:T(8,128)}, bf16[3,512,768]{2,1,0:T(8,128)(2,1)}, f32[3,2,4,768]{3,2,1,0:T(4,128)}, bf16[768,768]{1,0:T(8,128)(2,1)}) custom-call(s32[6]{0:T(128)} %pad_add_fusion.2.meta, bf16[3,512,768]{2,1,0:T(8,128)(2,1)} %arrange.4.refs_0_, bf16[1,512,768]{2,1,0:T(8,128)(2,1)} %collective-permute-done.2.refs_1_, ...), custom_call_target="tpu_custom_call" | custom-call | flops 12000000000 | bytes 24000000 | tf_op jit(solution)/shard_map/backward_middle/pallas_call | solution.py:748
  410.8 32.2 %backward_heads.1 = (bf16[3,512,2304]{2,1,0:T(8,128)(2,1)}, bf16[768,3072]{1,0:T(8,128)(2,1)}) custom-call(s32[6]{0:T(128)} %pad_add_fusion.2.meta, bf16[3,512,2304]{2,1,0:T(8,128)(2,1)} %get-tuple-element.83.refs_0_, bf16[3,512,768]{2,1,0:T(8,128)(2,1)} %get-tuple-element.90.refs_1_, bf16[3,512,768]{2,1,0:T(8,128)(2,1)} %get-tuple-element.91.refs_2_, ...), custom_call_target="tpu_custom_call" | custom-call | flops 35999997952 | bytes 24000000 | tf_op jit(solution)/shard_map/backward_heads/pallas_call | solution.py:748
  443.0 16.2 %backward_tokens.2 = (bf16[3,512,768]{2,1,0:T(8,128)(2,1)}, bf16[3,512,768]{2,1,0:T(8,128)(2,1)}, bf16[3,256,768]{2,1,0:T(8,128)(2,1)}, f32[3,2,2,768]{3,2,1,0:T(2,128)}, f32[2,72,768]{2,1,0:T(8,128)}) custom-call(s32[6]{0:T(128)} %pad_add_fusion.2.meta, bf16[3,512,2304]{2,1,0:T(8,128)(2,1)} %get-tuple-element.101.refs_0_, ...), custom_call_target="tpu_custom_call" | custom-call | flops 6000000000 | bytes 8000000 | tf_op jit(solution)/shard_map/backward_tokens/pallas_call | solution.py:748
  459.1 2.1 slice.235
  465.4 3.6 place_back.2
  469.5 1.7 convert_add_fusion.2
  471.2 7.2 %collective-permute-done.16 = bf16[1,256,768]{2,1,0:T(8,128)(2,1)S(1)} collective-permute-done((bf16[1,256,768]{2,1,0:T(8,128)(2,1)}, bf16[1,256,768]{2,1,0:T(8,128)(2,1)S(1)}, u32[]{:S(2)}, u32[]{:S(2)}) %collective-permute-start.16) | collective-permute-done | bytes 393248 | tf_op jit(solution)/shard_map/ppermute | solution.py:914
  478.4 2.3 select_add_fusion.3
  481.3 26.4 %backward_tokens.3 = (bf16[3,512,768]{2,1,0:T(8,128)(2,1)}, bf16[3,512,768]{2,1,0:T(8,128)(2,1)}, bf16[3,256,768]{2,1,0:T(8,128)(2,1)}, f32[3,2,2,768]{3,2,1,0:T(2,128)}, f32[2,72,768]{2,1,0:T(8,128)}) custom-call(s32[6]{0:T(128)} %pad_add_fusion.2.meta, ...), custom_call_target="tpu_custom_call", output_to_operand_aliasing={{0}: (9, {}), {1}: (10, {}), {2}: (11, {}), {3}: (12, {})} | custom-call | flops 12000000000 | bytes 16000000 | tf_op jit(solution)/shard_map/backward_tokens/pallas_call | solution.py:748
  514.5 9.9 %collective-permute-done.24 = bf16[1,2,6,4608]{3,2,1,0:T(8,128)(2,1)S(1)} collective-permute-done((bf16[1,2,6,4608]{3,2,1,0:T(8,128)(2,1)S(1)}, bf16[1,2,6,4608]{3,2,1,0:T(8,128)(2,1)S(1)}, u32[]{:S(2)}, u32[]{:S(2)}) %collective-permute-start.24) | collective-permute-done | bytes 110624 | tf_op jit(solution)/shard_map/ppermute | solution.py:587
  527.0 3.4 all-to-all-start.1
  530.4 3.8 place_back.3
  536.2 8.4 %collective-permute-done.25 = bf16[2,2,6,4608]{3,2,1,0:T(8,128)(2,1)} collective-permute-done((bf16[2,2,6,4608]{3,2,1,0:T(8,128)(2,1)}, bf16[2,2,6,4608]{3,2,1,0:T(8,128)(2,1)}, u32[]{:S(2)}, u32[]{:S(2)}) %collective-permute-start.25) | collective-permute-done | bytes 221216 | tf_op jit(solution)/shard_map/ppermute | solution.py:587
  546.3 3.8 collective-permute-done.19
  551.6 8.3 %collective-permute-done.26 = bf16[4,2,6,4608]{3,1,2,0:T(2,128)(2,1)S(1)} collective-permute-done((bf16[4,2,6,4608]{3,1,2,0:T(2,128)(2,1)S(1)}, bf16[4,2,6,4608]{3,1,2,0:T(2,128)(2,1)S(1)}, u32[]{:S(2)}, u32[]{:S(2)}) %collective-permute-start.26) | collective-permute-done | bytes 442400 | tf_op jit(solution)/shard_map/ppermute | solution.py:587
  567.1 7.1 %collective-permute-done.17 = bf16[3,256,768]{2,1,0:T(8,128)(2,1)} collective-permute-done((bf16[3,256,768]{2,1,0:T(8,128)(2,1)}, bf16[3,256,768]{2,1,0:T(8,128)(2,1)}, u32[]{:S(2)}, u32[]{:S(2)}) %collective-permute-start.17) | collective-permute-done | bytes 1179680 | tf_op jit(solution)/shard_map/ppermute | solution.py:914
  574.1 3.3 select_add_fusion
  577.5 3.1 maximum_select_fusion.1
  580.6 2.7 fusion
  583.3 2.5 pad_maximum_fusion.2
  587.4 2.7 reshape_reshape.11
  594.6 3.5 collective-permute-done.20
  (325 shorter events, 100.8 us)
Async XLA Ops:
  7.2 10.9 %slice-start = ((bf16[4,512,768]{2,1,0:T(8,128)(2,1)}), bf16[1,512,768]{2,1,0:T(8,128)(2,1)S(1)}, s32[]{:S(2)}) async-start(bf16[4,512,768]{2,1,0:T(8,128)(2,1)} %refs_0_.7), calls=%async_computation.10 | async-start | bytes 1572864 | tf_op jit(solution)/shard_map/slice | solution.py:779
  7.2 10.9 %slice-start.2 = ((bf16[4,512,768]{2,1,0:T(8,128)(2,1)}), bf16[1,512,768]{2,1,0:T(8,128)(2,1)S(1)}, s32[]{:S(2)}) async-start(bf16[4,512,768]{2,1,0:T(8,128)(2,1)} %refs_0_.5), calls=%async_computation.12 | async-start | bytes 1572864 | tf_op jit(solution)/shard_map/slice | solution.py:779
  7.2 219.7 %all-gather.3.cloned.1.call-start = ((), (), s32[]{:S(2)}) async-start(), calls=%async_computation.5 | async-start | bytes 5013504 | tf_op jit(solution)/shard_map/all_gather | solution.py:720
  8.9 44.1 %collective-permute-start.6 = (bf16[48,2048]{1,0:T(8,128)(2,1)S(1)}, bf16[48,2048]{1,0:T(8,128)(2,1)}, u32[]{:S(2)}, u32[]{:S(2)}) collective-permute-start(bf16[48,2048]{1,0:T(8,128)(2,1)S(1)} %slice.230), channel_id=1, source_target_pairs={{0,24},{2,26},{4,28},{6,30},{8,16},{10,18},{12,20},{14,22},{16,8},... | collective-permute-start | bytes 589832 | tf_op jit(solution)/shard_map/ppermute | solution.py:587
  14.0 42.0 %collective-permute-start.5 = (bf16[48,2048]{1,0:T(8,128)(2,1)S(1)}, bf16[48,2048]{1,0:T(8,128)(2,1)}, u32[]{:S(2)}, u32[]{:S(2)}) collective-permute-start(bf16[48,2048]{1,0:T(8,128)(2,1)S(1)} %slice.230), channel_id=1, source_target_pairs={{0,16},{2,18},{4,20},{6,22},{8,24},{10,26},{12,28},{14,30},{16,0},... | collective-permute-start | bytes 589832 | tf_op jit(solution)/shard_map/ppermute | solution.py:587
  14.0 34.3 %collective-permute-start.4 = (bf16[48,2048]{1,0:T(8,128)(2,1)S(1)}, bf16[48,2048]{1,0:T(8,128)(2,1)}, u32[]{:S(2)}, u32[]{:S(2)}) collective-permute-start(bf16[48,2048]{1,0:T(8,128)(2,1)S(1)} %slice.230), channel_id=1, source_target_pairs={{0,8},{2,10},{4,12},{6,14},{8,0},{10,2},{12,4},{14,6},{16,24},{18,... | collective-permute-start | bytes 589832 | tf_op jit(solution)/shard_map/ppermute | solution.py:587
  16.3 30.5 %collective-permute-start.9 = (bf16[48,1024]{1,0:T(8,128)(2,1)S(1)}, bf16[48,1024]{1,0:T(8,128)(2,1)}, u32[]{:S(2)}, u32[]{:S(2)}) collective-permute-start(bf16[48,1024]{1,0:T(8,128)(2,1)S(1)} %pad_maximum_fusion.19), channel_id=1, source_target_pairs={{0,4},{2,6},{4,0},{6,2},{8,12},{10,14},{12,8},{14,10},{16,20},{18,... | collective-permute-start | bytes 294920 | tf_op jit(solution)/shard_map/ppermute | solution.py:587
  18.2 86.3 %collective-permute-start.1 = (bf16[2,256,768]{2,1,0:T(8,128)(2,1)S(1)}, bf16[2,256,768]{2,1,0:T(8,128)(2,1)}, u32[]{:S(2)}, u32[]{:S(2)}) collective-permute-start(bf16[2,256,768]{2,1,0:T(8,128)(2,1)S(1)} %bitcast.176), channel_id=1, source_target_pairs={{0,1},{1,0},{2,3},{3,2},{4,5},{5,4},{6,7},{7,6},{8,9},{9,8},{10,11... | collective-permute-start | bytes 2359304 | tf_op jit(solution)/shard_map/ppermute | solution.py:781
  24.1 7.9 %copy-start.36 = (s32[64]{0:T(128)S(1)}, s32[64]{0:T(128)}, u32[]{:S(2)}) copy-start(s32[64]{0:T(128)} %param.26) | copy-start | bytes 772
  25.4 95.3 %all-to-all-start = ((bf16[16,6,4992]{2,1,0:T(8,128)(2,1)}), bf16[16,6,4992]{2,1,0:T(8,128)(2,1)}, u32[]{:S(2)}, u32[]{:S(2)}) async-start(bf16[16,6,4992]{2,1,0:T(8,128)(2,1)} %pad_maximum_fusion.5), calls=%async_computation | async-start | bytes 2555904 | tf_op jit(solution)/shard_map/all_to_all | solution.py:709
  30.4 196.5 %all-gather.5.cloned.1.call-start = ((), (), s32[]{:S(2)}) async-start(), calls=%async_computation.6 | async-start | bytes 5013504 | tf_op jit(solution)/shard_map/all_gather | solution.py:721
  31.2 358.1 %reduce-scatter.4.cloned.1.call-start = ((), (), s32[]{:S(2)}) async-start(), calls=%async_computation.7 | async-start | bytes 2506752 | tf_op jit(solution)/shard_map/reduce_scatter | solution.py:865
  31.9 9.1 %copy-start.22 = (s32[512]{0:T(512)}, s32[512]{0:T(512)S(1)}, u32[]{:S(2)}) copy-start(s32[512]{0:T(512)S(1)} %multiply_add_fusion) | copy-start | bytes 6148
  35.1 7.9 %slice-start.1 = ((bf16[4,512,768]{2,1,0:T(8,128)(2,1)}), bf16[3,512,768]{2,1,0:T(8,128)(2,1)S(1)}, s32[]{:S(2)}) async-start(bf16[4,512,768]{2,1,0:T(8,128)(2,1)} %refs_0_.7), calls=%async_computation.11 | async-start | bytes 4718592 | tf_op jit(solution)/shard_map/slice | solution.py:779
  38.5 6.0 copy-start.24
  44.5 7.5 %copy-start.12 = (bf16[48,2304]{1,0:T(8,128)(2,1)S(1)}, bf16[48,2304]{1,0:T(8,128)(2,1)}, u32[]{:S(2)}) copy-start(bf16[48,2304]{1,0:T(8,128)(2,1)} %param.17) | copy-start | bytes 663556
  46.8 80.0 %collective-permute-start = (bf16[6,256,768]{2,1,0:T(8,128)(2,1)}, bf16[6,256,768]{2,1,0:T(8,128)(2,1)}, u32[]{:S(2)}, u32[]{:S(2)}) collective-permute-start(bf16[6,256,768]{2,1,0:T(8,128)(2,1)} %bitcast.3), channel_id=1, source_target_pairs={{0,1},{1,0},{2,3},{3,2},{4,5},{5,4},{6,7},{7,6},{8,9},{9,8},{10,11... | collective-permute-start | bytes 7077896 | tf_op jit(solution)/shard_map/ppermute | solution.py:781
  48.3 24.9 %collective-permute-start.12 = (bf16[2,48,1024]{2,1,0:T(8,128)(2,1)S(1)}, bf16[2,48,1024]{2,1,0:T(8,128)(2,1)S(1)}, u32[]{:S(2)}, u32[]{:S(2)}) collective-permute-start(bf16[2,48,1024]{2,1,0:T(8,128)(2,1)S(1)} %pad_maximum_fusion.16), channel_id=1, source_target_pairs={{0,24},{2,26},{4,28},{6,30},{8,16},{10,18},{12,20},{14,22},{16,8},... | collective-permute-start | bytes 589832 | tf_op jit(solution)/shard_map/ppermute | solution.py:587
  53.0 50.4 %collective-permute-start.11 = (bf16[2,48,1024]{2,1,0:T(8,128)(2,1)S(1)}, bf16[2,48,1024]{2,1,0:T(8,128)(2,1)S(1)}, u32[]{:S(2)}, u32[]{:S(2)}) collective-permute-start(bf16[2,48,1024]{2,1,0:T(8,128)(2,1)S(1)} %pad_maximum_fusion.16), channel_id=1, source_target_pairs={{0,16},{2,18},{4,20},{6,22},{8,24},{10,26},{12,28},{14,30},{16,0},... | collective-permute-start | bytes 589832 | tf_op jit(solution)/shard_map/ppermute | solution.py:587
  56.0 47.5 %collective-permute-start.10 = (bf16[2,48,1024]{2,1,0:T(8,128)(2,1)S(1)}, bf16[2,48,1024]{2,1,0:T(8,128)(2,1)S(1)}, u32[]{:S(2)}, u32[]{:S(2)}) collective-permute-start(bf16[2,48,1024]{2,1,0:T(8,128)(2,1)S(1)} %pad_maximum_fusion.16), channel_id=1, source_target_pairs={{0,8},{2,10},{4,12},{6,14},{8,0},{10,2},{12,4},{14,6},{16,24},{18,... | collective-permute-start | bytes 589832 | tf_op jit(solution)/shard_map/ppermute | solution.py:587
  73.2 41.7 %collective-permute-start.7 = (bf16[4,48,2048]{2,1,0:T(8,128)(2,1)}, bf16[4,48,2048]{2,1,0:T(8,128)(2,1)}, u32[]{:S(2)}, u32[]{:S(2)}) collective-permute-start(bf16[4,48,2048]{2,1,0:T(8,128)(2,1)} %bitcast.17), channel_id=1, source_target_pairs={{0,4},{2,6},{4,0},{6,2},{8,12},{10,14},{12,8},{14,10},{16,20},{18,... | collective-permute-start | bytes 2359304 | tf_op jit(solution)/shard_map/ppermute | solution.py:587
  104.6 13.3 %collective-permute-start.13 = (bf16[4,2,48,1024]{3,2,1,0:T(8,128)(2,1)}, bf16[4,2,48,1024]{3,2,1,0:T(8,128)(2,1)}, u32[]{:S(2)}, u32[]{:S(2)}) collective-permute-start(bf16[4,2,48,1024]{3,2,1,0:T(8,128)(2,1)} %bitcast.31), channel_id=1, source_target_pairs={{0,2},{2,0},{4,6},{6,4},{8,10},{10,8},{12,14},{14,12},{16,18},{18,... | collective-permute-start | bytes 2359304 | tf_op jit(solution)/shard_map/ppermute | solution.py:587
  109.0 117.9 %collective-permute-start.2 = (bf16[1,512,768]{2,1,0:T(8,128)(2,1)}, bf16[1,512,768]{2,1,0:T(8,128)(2,1)}, u32[]{:S(2)}, u32[]{:S(2)}) collective-permute-start(bf16[1,512,768]{2,1,0:T(8,128)(2,1)} %arrange.5), channel_id=1, source_target_pairs={{0,16},{2,18},{4,20},{6,22},{8,24},{10,26},{12,28},{14,30},{16,0},... | collective-permute-start | bytes 2359304 | tf_op jit(solution)/shard_map/ppermute | solution.py:788
  113.5 92.6 %collective-permute-start.3 = (bf16[1,512,768]{2,1,0:T(8,128)(2,1)}, bf16[1,512,768]{2,1,0:T(8,128)(2,1)}, u32[]{:S(2)}, u32[]{:S(2)}) collective-permute-start(bf16[1,512,768]{2,1,0:T(8,128)(2,1)} %arrange.7), channel_id=1, source_target_pairs={{0,16},{2,18},{4,20},{6,22},{8,24},{10,26},{12,28},{14,30},{16,0},... | collective-permute-start | bytes 2359304 | tf_op jit(solution)/shard_map/ppermute | solution.py:786
  117.9 31.3 %collective-permute-start.8 = (bf16[4,2,48,2048]{3,2,1,0:T(8,128)(2,1)}, bf16[4,2,48,2048]{3,2,1,0:T(8,128)(2,1)}, u32[]{:S(2)}, u32[]{:S(2)}) collective-permute-start(bf16[4,2,48,2048]{3,2,1,0:T(8,128)(2,1)} %pad_maximum_fusion.3), channel_id=1, source_target_pairs={{0,2},{2,0},{4,6},{6,4},{8,10},{10,8},{12,14},{14,12},{16,18},{18,... | collective-permute-start | bytes 4718600 | tf_op jit(solution)/shard_map/ppermute | solution.py:587
  287.5 193.2 %reduce-scatter.6.cloned.1.call-start = ((), (), s32[]{:S(2)}) async-start(), calls=%async_computation.8 | async-start | bytes 7520256 | tf_op jit(solution)/shard_map/reduce_scatter | solution.py:865
  355.4 234.7 %reduce-scatter.8.cloned.1.call-start = ((), (), s32[]{:S(2)}) async-start(), calls=%async_computation.9 | async-start | bytes 5013504 | tf_op jit(solution)/shard_map/reduce_scatter | solution.py:865
  359.2 28.0 %collective-permute-start.14 = (bf16[3,256,768]{2,1,0:T(8,128)(2,1)}, bf16[3,256,768]{2,1,0:T(8,128)(2,1)S(1)}, u32[]{:S(2)}, u32[]{:S(2)}) collective-permute-start(bf16[3,256,768]{2,1,0:T(8,128)(2,1)} %get-tuple-element.82), channel_id=1, source_target_pairs={{0,1},{1,0},{2,3},{3,2},{4,5},{5,4},{6,7},{7,6},{8,9},{9,8},{10,11... | collective-permute-start | bytes 3538952 | tf_op jit(solution)/shard_map/ppermute | solution.py:914
  361.5 25.6 %copy-start.5 = (bf16[3,512,768]{2,1,0:T(8,128)(2,1)S(1)}, bf16[3,512,768]{2,1,0:T(8,128)(2,1)}, u32[]{:S(2)}) copy-start(bf16[3,512,768]{2,1,0:T(8,128)(2,1)} %get-tuple-element.81) | copy-start | bytes 7077892
  378.6 86.7 %collective-permute-start.15 = (bf16[1,512,768]{2,1,0:T(8,128)(2,1)}, bf16[1,512,768]{2,1,0:T(8,128)(2,1)}, u32[]{:S(2)}, u32[]{:S(2)}) collective-permute-start(bf16[1,512,768]{2,1,0:T(8,128)(2,1)} %slice.233), channel_id=1, source_target_pairs={{0,16},{2,18},{4,20},{6,22},{8,24},{10,26},{12,28},{14,30},{16,0},... | collective-permute-start | bytes 2359304 | tf_op jit(solution)/shard_map/ppermute | solution.py:922
  461.2 8.3 %collective-permute-start.21 = (bf16[48,1536]{1,0:T(8,128)(2,1)}, bf16[48,1536]{1,0:T(8,128)(2,1)}, u32[]{:S(2)}, u32[]{:S(2)}) collective-permute-start(bf16[48,1536]{1,0:T(8,128)(2,1)} %reduce-scatter.4.cloned.1.call-done), channel_id=1, source_target_pairs={{0,1},{1,0},{2,3},{3,2},{4,5},{5,4},{6,7},{7,6},{8,9},{9,8},{10,11... | collective-permute-start | bytes 442376 | tf_op jit(solution)/shard_map/ppermute | solution.py:644
  469.0 9.4 %collective-permute-start.16 = (bf16[1,256,768]{2,1,0:T(8,128)(2,1)}, bf16[1,256,768]{2,1,0:T(8,128)(2,1)S(1)}, u32[]{:S(2)}, u32[]{:S(2)}) collective-permute-start(bf16[1,256,768]{2,1,0:T(8,128)(2,1)} %get-tuple-element.99), channel_id=1, source_target_pairs={{0,1},{1,0},{2,3},{3,2},{4,5},{5,4},{6,7},{7,6},{8,9},{9,8},{10,11... | collective-permute-start | bytes 1179656 | tf_op jit(solution)/shard_map/ppermute | solution.py:914
  469.5 60.9 %collective-permute-start.18 = (bf16[1,512,768]{2,1,0:T(8,128)(2,1)}, bf16[1,512,768]{2,1,0:T(8,128)(2,1)}, u32[]{:S(2)}, u32[]{:S(2)}) collective-permute-start(bf16[1,512,768]{2,1,0:T(8,128)(2,1)} %slice.235), channel_id=1, source_target_pairs={{0,16},{2,18},{4,20},{6,22},{8,24},{10,26},{12,28},{14,30},{16,0},... | collective-permute-start | bytes 2359304 | tf_op jit(solution)/shard_map/ppermute | solution.py:922
  480.7 69.7 %collective-permute-start.22 = (bf16[48,4608]{1,0:T(8,128)(2,1)}, bf16[48,4608]{1,0:T(8,128)(2,1)}, u32[]{:S(2)}, u32[]{:S(2)}) collective-permute-start(bf16[48,4608]{1,0:T(8,128)(2,1)} %reduce-scatter.6.cloned.1.call-done), channel_id=1, source_target_pairs={{0,1},{1,0},{2,3},{3,2},{4,5},{5,4},{6,7},{7,6},{8,9},{9,8},{10,11... | collective-permute-start | bytes 1327112 | tf_op jit(solution)/shard_map/ppermute | solution.py:644
  507.6 18.2 %copy-start.16 = (f32[9,8,192]{2,1,0:T(8,128)S(1)}, f32[9,8,192]{2,1,0:T(8,128)}, u32[]{:S(2)}) copy-start(f32[9,8,192]{2,1,0:T(8,128)} %add.382) | copy-start | bytes 165892
  507.7 18.2 %copy-start.17 = (f32[9,8,192]{2,1,0:T(8,128)S(1)}, f32[9,8,192]{2,1,0:T(8,128)}, u32[]{:S(2)}) copy-start(f32[9,8,192]{2,1,0:T(8,128)} %add.381) | copy-start | bytes 165892
  509.0 4.4 collective-permute-start.23
  513.5 10.9 %collective-permute-start.24 = (bf16[1,2,6,4608]{3,2,1,0:T(8,128)(2,1)S(1)}, bf16[1,2,6,4608]{3,2,1,0:T(8,128)(2,1)S(1)}, u32[]{:S(2)}, u32[]{:S(2)}) collective-permute-start(bf16[1,2,6,4608]{3,2,1,0:T(8,128)(2,1)S(1)} %maximum_select_fusion.2), channel_id=1, source_target_pairs={{0,16},{2,18},{4,20},{6,22},{8,24},{10,26},{12,28},{14,30},{16,0},... | collective-permute-start | bytes 331784 | tf_op jit(solution)/shard_map/ppermute | solution.py:587
  525.9 18.7 %collective-permute-start.25 = (bf16[2,2,6,4608]{3,2,1,0:T(8,128)(2,1)}, bf16[2,2,6,4608]{3,2,1,0:T(8,128)(2,1)}, u32[]{:S(2)}, u32[]{:S(2)}) collective-permute-start(bf16[2,2,6,4608]{3,2,1,0:T(8,128)(2,1)} %maximum_bitcast_fusion), channel_id=1, source_target_pairs={{0,8},{2,10},{4,12},{6,14},{8,0},{10,2},{12,4},{14,6},{16,24},{18,... | collective-permute-start | bytes 663560 | tf_op jit(solution)/shard_map/ppermute | solution.py:587
  527.0 37.7 %all-to-all-start.1 = ((f32[32,9,240]{2,1,0:T(8,128)}), f32[32,9,240]{2,1,0:T(8,128)}, u32[]{:S(2)}, u32[]{:S(2)}) async-start(f32[32,9,240]{2,1,0:T(8,128)} %bitcast.60), calls=%async_computation.3 | async-start | bytes 1048576 | tf_op jit(solution)/shard_map/all_to_all | solution.py:967
  534.2 16.0 %copy-start.13 = (bf16[1,512,768]{2,1,0:T(8,128)(2,1)S(1)}, bf16[1,512,768]{2,1,0:T(8,128)(2,1)}, u32[]{:S(2)}) copy-start(bf16[1,512,768]{2,1,0:T(8,128)(2,1)} %get-tuple-element.109) | copy-start | bytes 2359300
  534.2 15.9 %collective-permute-start.19 = (bf16[1,256,768]{2,1,0:T(8,128)(2,1)}, bf16[1,256,768]{2,1,0:T(8,128)(2,1)S(1)}, u32[]{:S(2)}, u32[]{:S(2)}) collective-permute-start(bf16[1,256,768]{2,1,0:T(8,128)(2,1)} %get-tuple-element.110), channel_id=1, source_target_pairs={{0,1},{1,0},{2,3},{3,2},{4,5},{5,4},{6,7},{7,6},{8,9},{9,8},{10,11... | collective-permute-start | bytes 1179656 | tf_op jit(solution)/shard_map/ppermute | solution.py:914
  535.9 38.3 %collective-permute-start.17 = (bf16[3,256,768]{2,1,0:T(8,128)(2,1)}, bf16[3,256,768]{2,1,0:T(8,128)(2,1)}, u32[]{:S(2)}, u32[]{:S(2)}) collective-permute-start(bf16[3,256,768]{2,1,0:T(8,128)(2,1)} %get-tuple-element.106), channel_id=1, source_target_pairs={{0,1},{1,0},{2,3},{3,2},{4,5},{5,4},{6,7},{7,6},{8,9},{9,8},{10,11... | collective-permute-start | bytes 3538952 | tf_op jit(solution)/shard_map/ppermute | solution.py:914
  546.2 13.6 %collective-permute-start.26 = (bf16[4,2,6,4608]{3,1,2,0:T(2,128)(2,1)S(1)}, bf16[4,2,6,4608]{3,1,2,0:T(2,128)(2,1)S(1)}, u32[]{:S(2)}, u32[]{:S(2)}) collective-permute-start(bf16[4,2,6,4608]{3,1,2,0:T(2,128)(2,1)S(1)} %bitcast.174), channel_id=1, source_target_pairs={{0,4},{2,6},{4,0},{6,2},{8,12},{10,14},{12,8},{14,10},{16,20},{18,... | collective-permute-start | bytes 1327112 | tf_op jit(solution)/shard_map/ppermute | solution.py:587
  551.5 11.0 %copy-start.10 = (f32[48,1536]{1,0:T(8,128)S(1)}, f32[48,1536]{1,0:T(8,128)}, u32[]{:S(2)}) copy-start(f32[48,1536]{1,0:T(8,128)} %convert_add_fusion.2) | copy-start | bytes 884740
  562.5 18.1 %collective-permute-start.27 = (bf16[8,2,6,4608]{3,1,2,0:T(2,128)(2,1)S(1)}, bf16[8,2,6,4608]{3,1,2,0:T(2,128)(2,1)}, u32[]{:S(2)}, u32[]{:S(2)}) collective-permute-start(bf16[8,2,6,4608]{3,1,2,0:T(2,128)(2,1)S(1)} %bitcast.167), channel_id=1, source_target_pairs={{0,2},{2,0},{4,6},{6,4},{8,10},{10,8},{12,14},{14,12},{16,18},{18,... | collective-permute-start | bytes 2654216 | tf_op jit(solution)/shard_map/ppermute | solution.py:587
  590.2 7.9 %collective-permute-start.20 = (bf16[48,3072]{1,0:T(8,128)(2,1)}, bf16[48,3072]{1,0:T(8,128)(2,1)S(1)}, u32[]{:S(2)}, u32[]{:S(2)}) collective-permute-start(bf16[48,3072]{1,0:T(8,128)(2,1)} %reduce-scatter.8.cloned.1.call-done), channel_id=1, source_target_pairs={{0,1},{1,0},{2,3},{3,2},{4,5},{5,4},{6,7},{7,6},{8,9},{9,8},{10,11... | collective-permute-start | bytes 884744 | tf_op jit(solution)/shard_map/ppermute | solution.py:644
  591.6 6.5 %copy-start.18 = (bf16[48,3072]{1,0:T(8,128)(2,1)S(1)}, bf16[48,3072]{1,0:T(8,128)(2,1)}, u32[]{:S(2)}) copy-start(bf16[48,3072]{1,0:T(8,128)(2,1)} %reduce-scatter.8.cloned.1.call-done) | copy-start | bytes 884740
  (32 other events, 92.8 us)
Sparse Core Ops, SparseCore 0:
  10.3 82.2 all-gather.2
  94.9 99.9 all-gather.4
  287.6 63.8 reduce-scatter.3
  355.9 105.4 reduce-scatter.5
  481.4 81.6 reduce-scatter.7

commit v2 on v1

--- a/solution.py
+++ b/solution.py
@@ -103,6 +103,13 @@
         store[which, 8 * tap : 8 * tap + 8, lanes] += jnp.sum(total.reshape(8, 8, total.shape[1]), axis=0)
 
 
+def finish_taps(store, out):
+    for tap in range(9):
+        other = 3 * (tap % 3) + tap // 3
+        total = store[0, 8 * tap : 8 * tap + 8, :] + store[1, 8 * other : 8 * other + 8, :]
+        out[tap : tap + 1, :] = jnp.sum(total, axis=0, keepdims=True)
+
+
 def head_mask():
     rows = lax.broadcasted_iota(jnp.int32, (GROUP, GROUP), 0) // HEAD_DIM
     cols = lax.broadcasted_iota(jnp.int32, (GROUP, GROUP), 1) // HEAD_DIM
@@ -188,19 +195,17 @@
                     mix_o[0, rows, lanes] = weighted(near, weights).astype(bf16)
 
 
-def attend(base, meta, x, mix, mod, weights_p, weights_q, qkv_o, prob_o, att_o, branch_o, mid_o, ffn_o):
+def attend(base, meta, x, mix, mod, weights, qkv_o, prob_o, att_o, branch_o, mid_o, ffn_o):
     unit = pl.program_id(0) + base
     width = x.shape[2]
     groups = width // GROUP
 
     @pl.when(meta[unit] > 0)
     def _():
-        @pl.loop(0, weights_p.shape[1] // 256)
+        @pl.loop(0, 3 * width // 256)
         def _(step):
             lanes = row_block(step, 256)
-            qkv_o[0, :, lanes] = dot(mix[0], weights_p[:, lanes]).astype(bf16)
-
-        qkv_o[0, :, 3 * width - GROUP :] = dot(mix[0], weights_q[:, :GROUP]).astype(bf16)
+            qkv_o[0, :, lanes] = dot(mix[0], weights[:, lanes]).astype(bf16)
 
         mask = head_mask()
 
@@ -232,7 +237,7 @@
             @pl.loop(0, LATENT // ROWS)
             def _(step):
                 rows = row_block(step, ROWS, latent * LATENT)
-                branch = dot(att_o[0, rows, :], weights_q[:, GROUP:])
+                branch = dot(att_o[0, rows, :], weights[:, 3 * width :])
                 branch_o[0, rows, :] = branch.astype(bf16)
                 middle = x[0, rows, :].astype(f32) + gate_a * branch
                 mid_o[0, rows, :] = middle
@@ -240,28 +245,29 @@
                 ffn_o[0, rows, :] = (normed * scale + shift).astype(bf16)
 
 
-def feed_forward(part, shard, taken, meta, *refs):
+def feed_forward(part, taken, meta, *refs):
     if part == 0:
         if taken:
-            cot, other, mod, ffn, up_w, down_w, taps, *refs = refs
+            cot, other, mod, ffn, weights, taps, *refs = refs
         else:
-            cot, mod, ffn, up_w, down_w, taps, *refs = refs
-        gbb_o, bb_o, gf_o, up_o, down_o, dtap_o, *refs = refs
+            cot, mod, ffn, weights, taps, *refs = refs
+        gbb_o, bb_o, gf_o, grad_o, tap_o, *refs = refs
         gbb = gbb_o
     else:
-        gbb, ffn, up_w, down_w, taps, bb_i, gf_i, mid, mod, spots, down_i, *refs = refs
-        gf_o, y_o, own_o, far_o, grad_o, dtap_o, bb_o, *refs = refs
-    ffn_t, gbb_t, acc_up, acc_down, *slots = refs
+        gbb, ffn, weights, taps, bb_i, gf_i, mid, mod, spots, tap_i, *refs = refs
+        gf_o, y_o, own_o, far_o, grad_o, tap_o, bb_o, *refs = refs
+    ffn_t, gbb_t, acc_up, acc_down, dtap, *slots = refs
     unit = pl.program_id(0)
     width = ffn.shape[2]
     columns = taps.shape[2]
     items = columns // 256
+    per_block = width // 256
 
     @pl.when(unit == 0)
     def _():
         acc_up[...] = jnp.zeros_like(acc_up)
         acc_down[...] = jnp.zeros_like(acc_down)
-        dtap_o[...] = jnp.zeros_like(dtap_o)
+        dtap[...] = jnp.zeros_like(dtap)
 
     @pl.when(meta[unit] > 0)
     def _():
@@ -299,17 +305,22 @@
                 bb_o[0, rows, :] = bb_i[0, rows, :]
                 gf_o[0, rows, :] = gf_i[0, rows, :]
 
+        def down_rows(item):
+            block = item // per_block
+            return row_block(item - block * per_block, 256), row_block(block, width, columns)
+
         def project(item, use):
             upward, grad_act = use[0], use[1]
-            here = row_block(item, 256)
-            upward[...] = dot(ffn[0], up_w[:, here]).astype(bf16).astype(f32)
-            grad_act[...] = dot_nt(gbb[0], down_w[here, :])
+            rows, lanes = down_rows(item)
+            upward[...] = dot(ffn[0], weights[:, row_block(item, 256)]).astype(bf16).astype(f32)
+            grad_act[...] = dot_nt(gbb[0], weights[rows, lanes])
 
         def collect(item, use):
             act, grad_up = use[2], use[3]
+            rows, lanes = down_rows(item)
             here = row_block(item, 256)
-            bb_o[0] += dot(act[...], down_w[here, :])
-            gf_o[0] += dot_nt(grad_up[...], up_w[:, here])
+            bb_o[0] += dot(act[...], weights[rows, lanes])
+            gf_o[0] += dot_nt(grad_up[...], weights[:, here])
             acc_up[:, here] += dot(ffn_t[...], grad_up[...])
             acc_down[:, here] += dot(gbb_t[...], act[...])
 
@@ -333,7 +344,7 @@
                             root + 3.0 * root * 0.044715 * square
                         )
                         grads.append((grad_act[r, cols] * slope).astype(bf16).astype(f32))
-                    add_taps(dtap_o, which, lanes, found, grads)
+                    add_taps(dtap, which, lanes, found, grads)
                     for r, near in zip(rows, neighbours(grads, narrow_grid, ends)):
                         grad_up[r, cols] = weighted(near, taken_taps[::-1]).astype(bf16)
 
@@ -362,21 +373,14 @@
 
     @pl.when(unit == pl.num_programs(0) - 1)
     def _():
-        blocks = PARTS * columns // width
-        if part == 0:
-            up_o[...] = acc_up[...].astype(bf16)
-            store, row_at, col_at = down_o, 0, 0
-        else:
-            grad_o[:, :columns] = acc_up[...].astype(bf16)
-            grad_o[: width // 2, columns:] = down_i[...]
-            store, row_at, col_at = grad_o, width // 2, columns
-        for start in range(0, columns, width):
-            turned_rows = acc_down[:, start : start + width].T
-            for piece in range(width // shard):
-                owner, block = divmod(start // shard + piece, blocks)
-                rows = slice(row_at + owner * shard, row_at + owner * shard + shard)
-                lanes = slice(col_at + block * width, col_at + block * width + width)
-                store[rows, lanes] = turned_rows[piece * shard : piece * shard + shard].astype(bf16)
+        finish_taps(dtap, tap_o)
+        if part == PARTS - 1:
+            rows = [t[:, at : at + width] for t in (tap_i, tap_o) for at in range(0, columns, width)]
+            rows.append(jnp.zeros((128 - 9 * len(rows), width), f32))
+            grad_o[:, 2 * columns :] = jnp.concatenate(rows, 0).T.astype(bf16)
+        grad_o[:, :columns] = acc_up[...].astype(bf16)
+        for at in range(0, columns, width):
+            grad_o[:, columns + at : columns + at + width] = acc_down[:, at : at + width].astype(bf16).T
 
 
 def backward_middle(taken, meta, *refs):
@@ -384,7 +388,7 @@
         cot, other, *refs = refs
     else:
         cot, *refs = refs
-    bb, gf, mid, branch, att, mod, weights_q, grad_mid, grad_att, mod_o, dout_o, gba, acc_out = refs
+    bb, gf, mid, branch, att, mod, out_w, grad_mid, grad_att, mod_o, dout_o, gba, acc_out = refs
     unit = pl.program_id(0)
     width = cot.shape[2]
 
@@ -424,7 +428,7 @@
         def _(step):
             lanes = row_block(step, 256)
             acc_out[:, lanes] += dot_tn(att[0], gba[:, lanes])
-            grad_att[0, :, lanes] = dot_nt(gba[...], weights_q[lanes, GROUP:]).astype(bf16)
+            grad_att[0, :, lanes] = dot_nt(gba[...], out_w[lanes, :]).astype(bf16)
 
     @pl.when(unit == pl.num_programs(0) - 1)
     def _():
@@ -488,15 +492,15 @@
 
 
 def backward_tokens(
-    base, meta, dqkv, x, gm, mod, taps, spots, weights_p, weights_q,
-    dx_o, own_o, far_o, mod_o, dtap_o, grad_mix, hidden, grad_hidden,
+    base, meta, dqkv, x, gm, mod, taps, spots, qkv_w,
+    dx_o, own_o, far_o, mod_o, tap_o, grad_mix, hidden, grad_hidden, dtap,
 ):
     unit = pl.program_id(0) + base
     width = x.shape[2]
 
     @pl.when(pl.program_id(0) == 0)
     def _():
-        dtap_o[...] = jnp.zeros_like(dtap_o)
+        dtap[...] = jnp.zeros_like(dtap)
 
     @pl.when(meta[unit] > 0)
     def _():
@@ -505,9 +509,7 @@
         @pl.loop(0, width // 256)
         def _(step):
             rows = row_block(step, 256)
-            total = dot_nt(dqkv[0, :, : 3 * width - GROUP], weights_p[rows, :])
-            total = total + dot_nt(dqkv[0, :, 3 * width - GROUP :], weights_q[rows, :GROUP])
-            grad_mix[:, rows] = total.astype(bf16).astype(f32)
+            grad_mix[:, rows] = dot_nt(dqkv[0], qkv_w[rows, :]).astype(bf16).astype(f32)
 
         for latent in range(2):
             shift, scale = mod[0, latent, 0:1, :], 1.0 + mod[0, latent, 1:2, :]
@@ -531,7 +533,7 @@
                 rows = phase_rows(latent)
                 grads = [grad_mix[r, lanes] for r in rows]
                 found = neighbours([hidden[r, lanes] for r in rows], narrow_grid, ends)
-                add_taps(dtap_o, which, lanes, found, grads)
+                add_taps(dtap, which, lanes, found, grads)
                 for r, near in zip(rows, neighbours(grads, narrow_grid, ends)):
                     grad_hidden[r, lanes] = weighted(near, weights[::-1])
 
@@ -552,6 +554,10 @@
                 dx_o[0, rows, :] = total.astype(bf16)
 
         put_back(dx_o, spots, own_o, far_o)
+
+    @pl.when(pl.program_id(0) == pl.num_programs(0) - 1)
+    def _():
+        finish_taps(dtap, tap_o)
 
 
 def source_places(layouts, half):
@@ -573,11 +579,6 @@
     return taps.reshape(taps.shape[:-2] + (3, 3, taps.shape[-1])).swapaxes(-3, -2).reshape(taps.shape)
 
 
-def tap_sum(parts):
-    summed = parts.reshape(2, 9, 8, -1).sum(2)
-    return summed[0] + turned(summed[1])
-
-
 def bit_of(index, bit):
     return (index // bit) % 2
 
@@ -596,31 +597,25 @@
     return jnp.where(low, values, other), jnp.where(low, other, values)
 
 
-def gathered_rows(values, crosswise):
+def gathered_far(values):
     count = lax.axis_size("wide")
-    far_bits = bits_of(count)[2:]
-
-    def direct(v):
-        found = {0: v}
-        for mask in range(4, count, 4):
-            found[mask] = swapped(v, mask)
-        for bit in far_bits:
-            found = {
-                mask: jnp.stack(ordered(found[mask], found[mask | bit], bit), 0)
-                for mask in found if not mask & bit
-            }
-        return found[0].reshape((count // 4,) + v.shape)
-
-    if crosswise:
-        near = direct(jnp.stack(ordered(values, swapped(values, 2), 2)))
-    else:
-        far = direct(values)
-        near = jnp.stack(ordered(far, swapped(far, 2), 2), 1)
-    full = jnp.stack(ordered(near, swapped(near, 1), 1), 2)
-    return full.reshape(count * values.shape[0], values.shape[1])
-
-
-def gathered_everywhere(values):
+    found = {0: values}
+    for mask in range(4, count, 4):
+        found[mask] = swapped(values, mask)
+    for bit in bits_of(count)[2:]:
+        found = {
+            mask: jnp.stack(ordered(found[mask], found[mask | bit], bit), 0) for mask in found if not mask & bit
+        }
+    return found[0].reshape((count // 4,) + values.shape)
+
+
+def gathered_near(values, bit, axis, *waits):
+    other = swapped(values, bit)
+    values, *waits = joined(values, *waits)
+    return jnp.stack(ordered(values, other, bit), axis), *waits
+
+
+def gathered_everywhere(values, wait):
     lane, count = lax.axis_index("narrow"), lax.axis_size("narrow")
     if count == 2:
         other = lax.ppermute(values, "narrow", [(0, 1), (1, 0)])
@@ -629,9 +624,15 @@
         values = lax.all_gather(values, "narrow", axis=0)
     values = values[None]
     for bit in reversed(bits_of(lax.axis_size("wide"))):
+        if bit == 2:
+            values = after(values, wait)
         values = jnp.stack(ordered(values, swapped(values, bit), bit), 1)
         values = values.reshape((-1,) + values.shape[2:])
     return values
+
+
+def joined(*values):
+    return lax.optimization_barrier(values)
 
 
 def after(value, *earlier):
@@ -660,6 +661,7 @@
     units = 3 if balanced else slots // spread
     hidden_width = up_weight.shape[1]
     columns = hidden_width // PARTS
+    per_part = columns // D
 
     loads = (counts > 0).astype(jnp.int32).reshape(owners, slots)
 
@@ -678,11 +680,16 @@
         values = values.reshape((units, spread) + values.shape[1:])
         return lax.dynamic_index_in_dim(values, lane // 2, 1, keepdims=False)
 
+    rows_here = units * 2
+
     def latent_rows(values):
         values = all_units(values)
         if balanced:
-            return values.reshape(owners, units, 2, 2).transpose(0, 2, 1, 3).reshape(-1)
-        return values.reshape(owners, units, spread, 2, 2).transpose(0, 2, 3, 1, 4).reshape(-1)
+            values = values.reshape(owners, units, 2, 2).transpose(0, 2, 1, 3)
+        else:
+            values = values.reshape(owners, units, spread, 2, 2).transpose(0, 2, 3, 1, 4)
+        values = values.reshape(owners, narrow, rows_here)
+        return jnp.pad(values, ((0, 0), (0, 0), (0, 2)), constant_values=-1).reshape(-1)
 
     count_float = counts.astype(f32)
     scales = count_float * float(counts.shape[0]) / jnp.sum(count_float)
@@ -698,9 +705,11 @@
     label_hot = (latent_rows(labels)[:, None] == jnp.arange(class_table.shape[0], dtype=jnp.int32)).astype(bf16)
     embed = jnp.where(my_columns < half_width, jnp.cos(angles), jnp.sin(angles)) + dot(label_hot, class_table)
     activ, silu_back = jax.vjp(jax.nn.silu, embed)
-    act_low = activ.astype(bf16)
-    mine = lax.dynamic_index_in_dim(act_low.reshape(owners, narrow, units * 2, shard), lane, 1, keepdims=False)
-    partial_mod = dot(mine.reshape(-1, shard), ada_weight).astype(bf16).reshape(owners, units * 2, -1)
+    real_row = (latent_rows(labels) >= 0)[:, None]
+    act_low = jnp.where(real_row, activ, 0.0).astype(bf16)
+    mine = act_low.reshape(owners, narrow, rows_here + 2, shard)[:, :, :rows_here]
+    mine = lax.dynamic_index_in_dim(mine, lane, 1, keepdims=False)
+    partial_mod = dot(mine.reshape(-1, shard), ada_weight).astype(bf16).reshape(owners, rows_here, -1)
     both_taps = jnp.concatenate([conv_attn, conv_ffn], 1).reshape(-1)
     tap_size = both_taps.shape[0]
     tap_lanes = -(-tap_size // (units * 2 * 128)) * 128
@@ -710,20 +719,25 @@
     modulation = jnp.sum(arrived[:, :, : 6 * D].astype(f32), axis=0).reshape(units, 2, 6, D)
     both_taps = arrived[:, :, 6 * D :].reshape(owners, -1)[:, :tap_size].reshape(owners, 9, -1).astype(f32)
     conv_one = both_taps[:, :, :shard].swapaxes(0, 1).reshape(9, D)
-    conv_two = both_taps[:, :, shard:].swapaxes(0, 1).reshape(9, hidden_width)
+    conv_two = both_taps[:, :, shard:].reshape(owners, 9, PARTS, per_part, shard).transpose(2, 1, 3, 0, 4)
+    conv_two = conv_two.reshape(PARTS, 9, columns)
     weight_row = jnp.broadcast_to(my_scale[:, None, None, None], (units, 2, 1, D))
     mod = jnp.concatenate([modulation, weight_row], 2)
 
-    split = 3 * D - GROUP
-    weights_p = gathered_rows(qkv_weight[:, :split], False)
-    weights_q = gathered_rows(jnp.concatenate([qkv_weight[:, split:], out_weight], 1), True)
-    up_full = lax.all_gather(up_weight, "wide", axis=0, tiled=True)
-    down_full = lax.all_gather(down_weight, "wide", axis=0, tiled=True)
+    attn_far = gathered_far(jnp.concatenate([qkv_weight, out_weight], 1))
+    up_parts = up_weight.reshape(shard, owners, PARTS, per_part, shard).transpose(2, 0, 3, 1, 4)
+    up_parts = up_parts.reshape(PARTS, shard, columns)
+    down_parts = down_weight.reshape(PARTS, per_part, shard, D).swapaxes(1, 2).reshape(PARTS, shard, columns)
+    ffn_parts = jnp.concatenate([up_parts, down_parts], 2)
+
+    def all_rows(values):
+        return lax.all_gather(values, "wide", axis=0, tiled=True)
+
 
     def unit_taps(taps):
         return jnp.where((my_layout == 2)[:, None, None], turned(taps), taps)
 
-    taps_one, taps_two = unit_taps(conv_one), unit_taps(conv_two)
+    taps_one = unit_taps(conv_one)
 
     params = pltpu.CompilerParams(vmem_limit_bytes=VMEM_BYTES, dimension_semantics=("arbitrary",))
     any_space = pl.BlockSpec(memory_space=pl.ANY)
@@ -754,7 +768,7 @@
             out_shape=outs,
             input_output_aliases=aliases,
             compiler_params=params,
-            cost_estimate=pl.CostEstimate(flops=int(flops * count), bytes_accessed=int(8e6 * count), transcendentals=0),
+            cost_estimate=pl.CostEstimate(flops=int(flops * count * 0.25), bytes_accessed=int(1e6 * count), transcendentals=0),
             name=name,
         )(flags, *ins, *before)
 
@@ -775,20 +789,17 @@
         swap = [(0, 1), (1, 0)]
         partner = [(i, (i + owners // 2) % owners) for i in range(owners)]
 
-        def for_other_half(first, count):
-            parts = [v.reshape(slots, 16, GRID, D)[first : first + count] for v in (tokens, cotangent)]
-            parts = [lax.dynamic_slice_in_dim(v, 16 * (1 - half), 16, axis=2) for v in parts]
-            return lax.ppermute(jnp.concatenate(parts, 0).reshape(-1, LATENT, D), "narrow", swap)
-
-        far_last, far_first = for_other_half(3, 1), for_other_half(0, 3)
+        def for_other_half(values, first, count):
+            part = values.reshape(slots, 16, GRID, D)[first : first + count]
+            part = lax.dynamic_slice_in_dim(part, 16 * (1 - half), 16, axis=2)
+            return lax.ppermute(part.reshape(-1, LATENT, D), "narrow", swap)
+
         own_tok, own_cot = [v.reshape(slots, HALF, D) for v in (tokens, cotangent)]
-        x_last = arranged(3, 1, own_tok, far_last, 0, own_places, own_flags)
+        x_last = arranged(3, 1, own_tok, for_other_half(tokens, 3, 1), 0, own_places, own_flags)
+        attn_far, x_last, cot_far_last = joined(attn_far, x_last, for_other_half(cotangent, 3, 1))
         x_other = lax.ppermute(x_last, "wide", partner)
-        cot_last = arranged(3, 1, own_cot, far_last, 1, own_places, own_flags)
-        cot_other = lax.ppermute(cot_last, "wide", partner)
-        x_own = arranged(0, 3, own_tok, far_first, 0, own_places, own_flags)
-        cot_own = arranged(0, 3, own_cot, far_first, 3, own_places, own_flags)
-        cots, cot_specs = [cot_own, cot_other], [per_unit(*tokens_shape), whole(1, *tokens_shape)]
+        x_own = arranged(0, 3, own_tok, for_other_half(tokens, 0, 3), 0, own_places, own_flags)
+        cot_far = for_other_half(after(cotangent, attn_far), 0, 3)
     else:
 
         def to_units(values):
@@ -802,6 +813,7 @@
 
         x_own = to_units(tokens)
         cot_own = to_units(cotangent)
+        ffn_first = all_rows(after(ffn_parts[0], attn_far))
         cots, cot_specs = [cot_own], [per_unit(*tokens_shape)]
 
     unit_values = struct(units, *tokens_shape)
@@ -821,68 +833,72 @@
     def attend_call(base, count, before):
         spec = per_unit(*tokens_shape, base=base)
         return call(
-            partial(attend, base), "attend", count, meta, [x, mixed, mod, weights_p, weights_q],
-            [spec, spec, per_unit(2, 7, D, base=base), whole(D, split), whole(D, GROUP + D)],
+            partial(attend, base), "attend", count, meta, [x, mixed, mod, attn_full],
+            [spec, spec, per_unit(2, 7, D, base=base), whole(D, 4 * D)],
             [struct(units, HALF, 3 * D), unit_values, unit_values, unit_values, unit_floats, unit_values],
             [per_unit(HALF, 3 * D, base=base)] + [spec] * 5, (), 8e9, before,
         )
 
     if balanced:
         x, mixed = mix_call(0, 2, False, ())
+        attn_near, mixed, x_other, cot_far = gathered_near(attn_far, 2, 1, mixed, x_other, cot_far)
+        cot_own = arranged(0, 3, own_cot, cot_far, 0, own_places, own_flags)
+        ffn_first = all_rows(after(ffn_parts[0], attn_near))
+        cot_last = arranged(3, 1, own_cot, cot_far_last, 0, own_places, after(own_flags, attn_near))
+        cot_other = lax.ppermute(cot_last, "wide", partner)
+        attn_full, cot_own = gathered_near(attn_near, 1, 2, cot_own)
+        attn_full = attn_full.reshape(D, 4 * D)
         front = attend_call(0, 2, ())
+        ffn_second = all_rows(after(ffn_parts[1], attn_full))
         x, mixed = mix_call(2, 1, True, (x, mixed))
         front = attend_call(2, 1, front)
+        cots, cot_specs = [cot_own, cot_other], [per_unit(*tokens_shape), whole(1, *tokens_shape)]
     else:
         x, mixed = mix_call(0, units, False, ())
+        (attn_near,) = gathered_near(attn_far, 2, 1)
+        (attn_full,) = gathered_near(attn_near, 1, 2)
+        attn_full = attn_full.reshape(D, 4 * D)
         front = attend_call(0, units, ())
+        ffn_second = all_rows(after(ffn_parts[1], attn_full))
     projected, probs, attended, branch, middle, ffn_in = front
 
     slot_pair = [pltpu.VMEM((HALF, 256), kind) for kind in (f32, f32, f32, f32, bf16, bf16, bf16, bf16)]
     work = [pltpu.VMEM((D, HALF), bf16), pltpu.VMEM((D, HALF), bf16)]
-    work += [pltpu.VMEM((D, columns), f32), pltpu.VMEM((D, columns), f32)]
+    work += [pltpu.VMEM((D, columns), f32), pltpu.VMEM((D, columns), f32), pltpu.VMEM((2, 72, columns), f32)]
     unit_spec = per_unit(*tokens_shape)
-    tap_grad, tap_spec = struct(2, 72, columns, kind=f32), whole(2, 72, columns)
+    tap_grad, tap_spec = struct(9, columns, kind=f32), whole(9, columns)
+    weight_grad, weight_spec = struct(D, 2 * columns), whole(D, 2 * columns)
     spots = places[:, None, :]
-
-    def of_part(part):
-        specs = [
-            pl.BlockSpec((D, columns), lambda i, meta: (0, part), pipeline_mode=pl.Buffered(1)),
-            pl.BlockSpec((columns, D), lambda i, meta: (part, 0), pipeline_mode=pl.Buffered(1)),
-            pl.BlockSpec((1, 9, columns), lambda i, meta: (i, 0, part)),
-        ]
-        return [up_full, down_full, taps_two], specs
-
-    ins, specs = of_part(0)
-    gbb, branch_b, grad_ffn, up_grad, down_grad, ffn_taps_0 = call(
-        partial(feed_forward, 0, shard, balanced), "feed_forward", units, meta, cots + [mod, ffn_in] + ins,
-        cot_specs + [per_unit(2, 7, D), unit_spec] + specs,
-        [unit_values, unit_floats, unit_floats, struct(D, columns), struct(D // 2, hidden_width), tap_grad],
-        [unit_spec, unit_spec, unit_spec, whole(D, columns), whole(D // 2, hidden_width), tap_spec],
-        work + slot_pair, 16e9,
+    gbb, branch_b, grad_ffn, ffn_grad_0, ffn_taps_0 = call(
+        partial(feed_forward, 0, balanced), "feed_forward", units, meta,
+        cots + [mod, ffn_in, ffn_first, unit_taps(conv_two[0])],
+        cot_specs + [per_unit(2, 7, D), unit_spec, weight_spec, per_unit(9, columns)],
+        [unit_values, unit_floats, unit_floats, weight_grad, tap_grad],
+        [unit_spec, unit_spec, unit_spec, weight_spec, tap_spec], work + slot_pair, 16e9,
     )
 
     def owner_sum(values):
         return lax.psum_scatter(values, "wide", scatter_dimension=0, tiled=True)
 
-    sums_up = owner_sum(up_grad)
-    ins, specs = of_part(1)
-    grad_ffn, y_units, y_own, y_far, ffn_grad, ffn_taps_1, branch_b = call(
-        partial(feed_forward, 1, shard, balanced), "feed_forward", units, meta,
-        [gbb, ffn_in] + ins + [branch_b, grad_ffn, middle, mod, spots, down_grad],
-        [unit_spec, unit_spec] + specs
-        + [unit_spec, unit_spec, unit_spec, per_unit(2, 7, D), per_unit(1, HALF), whole(D // 2, hidden_width)],
-        [unit_floats, unit_values, unit_values, struct(units, LATENT, D), struct(D, columns + hidden_width),
-         tap_grad, unit_floats],
-        [unit_spec, unit_spec, unit_spec, per_unit(LATENT, D), whole(D, columns + hidden_width), tap_spec, unit_spec],
+    sums_0 = owner_sum(ffn_grad_0)
+    grad_ffn, y_units, y_own, y_far, ffn_grad_1, ffn_taps_1, branch_b = call(
+        partial(feed_forward, 1, balanced), "feed_forward", units, meta,
+        [gbb, ffn_in, ffn_second, unit_taps(conv_two[1]), branch_b, grad_ffn, middle, mod, spots, ffn_taps_0],
+        [unit_spec, unit_spec, weight_spec, per_unit(9, columns), unit_spec, unit_spec, unit_spec,
+         per_unit(2, 7, D), per_unit(1, HALF), tap_spec],
+        [unit_floats, unit_values, unit_values, struct(units, LATENT, D), struct(D, 2 * columns + 128), tap_grad,
+         unit_floats],
+        [unit_spec, unit_spec, unit_spec, per_unit(LATENT, D), whole(D, 2 * columns + 128), tap_spec, unit_spec],
         work + slot_pair, 17e9,
     )
-    grad_ffn, sums_up = lax.optimization_barrier((grad_ffn, sums_up))
-    sums_ffn = owner_sum(ffn_grad)
+    sums_1 = owner_sum(after(ffn_grad_1, sums_0))
+    grad_ffn = after(grad_ffn, sums_0)
 
     grad_mid, grad_att, mod_late, out_grad = call(
         partial(backward_middle, balanced), "backward_middle", units, meta,
-        cots + [branch_b, grad_ffn, middle, branch, attended, mod, weights_q],
-        cot_specs + [unit_spec] * 5 + [per_unit(2, 7, D), whole(D, GROUP + D)],
+        cots + [branch_b, grad_ffn, middle, branch, attended, mod, attn_full],
+        cot_specs + [unit_spec] * 5 + [per_unit(2, 7, D),
+         pl.BlockSpec((D, D), lambda i, meta: (0, 3), pipeline_mode=pl.Buffered(1))],
         [unit_floats, unit_values, struct(units, 2, 4, D, kind=f32), struct(D, D)],
         [unit_spec, unit_spec, per_unit(2, 4, D), whole(D, D)],
         [pltpu.VMEM(tokens_shape, bf16), pltpu.VMEM((D, D), f32)], 4e9,
@@ -893,35 +909,35 @@
         [struct(units, HALF, 3 * D), struct(D, 4 * D)], [per_unit(HALF, 3 * D), whole(D, 4 * D)],
         [pltpu.VMEM((D, 3 * D), f32)], 12e9,
     )
+    attn_sums = owner_sum(after(attn_grad, sums_1))
 
     def tokens_call(base, count, before):
         spec = per_unit(*tokens_shape, base=base)
         return call(
             partial(backward_tokens, base), "backward_tokens", count, meta,
-            [head_grads, x, grad_mid, mod, taps_one, spots, weights_p, weights_q],
+            [head_grads, x, grad_mid, mod, taps_one, spots, attn_full],
             [per_unit(HALF, 3 * D, base=base), spec, spec, per_unit(2, 7, D, base=base), per_unit(9, D, base=base), per_unit(1, HALF, base=base),
-             whole(D, split), whole(D, GROUP + D)],
+             whole(D, 3 * D)],
             [unit_values, unit_values, struct(units, LATENT, D), struct(units, 2, 2, D, kind=f32),
-             struct(2, 72, D, kind=f32)],
-            [spec, spec, per_unit(LATENT, D, base=base), per_unit(2, 2, D, base=base), whole(2, 72, D)],
-            [pltpu.VMEM(tokens_shape, f32)] * 3, 6e9, before,
+             struct(9, D, kind=f32)],
+            [spec, spec, per_unit(LATENT, D, base=base), per_unit(2, 2, D, base=base), whole(9, D)],
+            [pltpu.VMEM(tokens_shape, f32)] * 3 + [pltpu.VMEM((2, 72, D), f32)], 6e9, before,
         )
 
     def finished(pieces):
         pairs = []
         for own, far in pieces:
             count = own.shape[0]
-            far = lax.ppermute(far, "narrow", swap).reshape(count, 16, 16, D)
+            far = far.reshape(count, 16, 16, D)
             empty = jnp.zeros_like(far)
             side = jnp.where(half == 0, jnp.concatenate([empty, far], 2), jnp.concatenate([far, empty], 2))
             pairs.append(own.reshape(count, 16, GRID, D) + side)
         total = jnp.concatenate(pairs, 0)
         return jnp.where(own_active[:, None, None, None], total, 0.0).reshape(slots, local_tokens, D)
 
-    def returned(values, later):
-        back = lax.ppermute(values, "wide", partner)
+    def placed(back):
         return call(
-            place_back, "place_back", 1, after(own_flags, later), [back, own_places[3:, None, :]],
+            place_back, "place_back", 1, own_flags, [back, own_places[3:, None, :]],
             [unit_spec, per_unit(1, HALF)], [struct(1, *tokens_shape), struct(1, LATENT, D)],
             [unit_spec, per_unit(LATENT, D)], (), 2e9,
         )
@@ -936,45 +952,50 @@
         return lax.psum_scatter(full.reshape(slots, 2 * HALF, D), "narrow", scatter_dimension=1, tiled=True)
 
     if balanced:
+        y_back = lax.ppermute(y_units[2:], "wide", partner)
+        y_far = lax.ppermute(y_far, "narrow", swap)
+        head_grads, y_back, y_far = lax.optimization_barrier((head_grads, y_back, y_far))
+        y_last, y_last_far = placed(y_back)
         dx_units, dx_own, dx_far, mod_early, taps_a = tokens_call(2, 1, ())
-        y_back = returned(y_units[2:], dx_units)
-        dx_last = dx_units[2:]
-        head_grads, sums_ffn = lax.optimization_barrier((head_grads, sums_ffn))
-        attn_sums = owner_sum(after(attn_grad, sums_ffn))
+        x_back = lax.ppermute(dx_units[2:], "wide", partner)
+        y_last_far = lax.ppermute(y_last_far, "narrow", swap)
+        work_y = finished([(y_own, y_far), (y_last, y_last_far)])
+        head_grads, sums_1, work_y = lax.optimization_barrier((head_grads, sums_1, work_y))
         _, dx_own, dx_far, mod_early, taps_b = tokens_call(0, 2, (dx_units, dx_own, dx_far, mod_early))
-        x_back = returned(dx_last, mod_early)
-        work_y = finished([(y_own, y_far), y_back])
-        work_x = finished([(dx_own, dx_far), x_back])
-        conv_one_grad = tap_sum(taps_a) + tap_sum(taps_b)
+        mod_early, x_back, dx_far = lax.optimization_barrier((mod_early, x_back, dx_far))
+        x_last, x_last_far = placed(x_back)
+        dx_far, x_last_far = [lax.ppermute(v, "narrow", swap) for v in (dx_far, x_last_far)]
+        work_x = finished([(dx_own, dx_far), (x_last, x_last_far)])
+        conv_one_grad = taps_a + taps_b
     else:
         work_y = rows_back(y_own, y_far)
         dx_units, dx_own, dx_far, mod_early, taps_a = tokens_call(0, units, ())
-        attn_sums = owner_sum(after(attn_grad, sums_ffn))
         work_x = rows_back(dx_own, dx_far)
-        conv_one_grad = tap_sum(taps_a)
+        conv_one_grad = taps_a
 
     attn_final = narrow_sum(attn_sums)
     final_qkv, final_out = attn_final[:, : 3 * D], attn_final[:, 3 * D :]
-    ffn_final = narrow_sum(sums_ffn)
-    final_up = jnp.concatenate([narrow_sum(sums_up), ffn_final[:, :columns]], 1)
-    final_down = ffn_final[:, columns:].reshape(shard, -1, D).swapaxes(0, 1).reshape(-1, D)
-    conv_two_grad = jnp.concatenate([tap_sum(ffn_taps_0), tap_sum(ffn_taps_1)], 1)
-    conv_grads = jnp.concatenate(
-        [conv_one_grad.reshape(9, owners, shard), conv_two_grad.reshape(9, owners, -1)], 2
-    ).swapaxes(0, 1)
-    conv_grads = jnp.broadcast_to(conv_grads[:, None], (owners, narrow) + conv_grads.shape[1:])
-    conv_grads = conv_grads.reshape((owners * narrow,) + conv_grads.shape[2:])
-    conv_sums = jnp.sum(lax.all_to_all(conv_grads, ("wide", "narrow"), 0, 0, tiled=True), axis=0)
+    second = narrow_sum(sums_1)
+    ffn_final = jnp.stack([narrow_sum(sums_0), second[:, : 2 * columns]])
+    final_up = ffn_final[:, :, :columns].reshape(PARTS, shard, per_part, owners, shard)
+    final_up = final_up.transpose(1, 3, 0, 2, 4).reshape(shard, hidden_width)
+    final_down = ffn_final[:, :, columns:].reshape(PARTS, shard, per_part, D).swapaxes(1, 2).reshape(-1, D)
+    final_taps = second[:, 2 * columns : 2 * columns + 9 * PARTS * per_part].reshape(shard, PARTS, per_part, 9)
+    final_taps = final_taps.transpose(3, 1, 2, 0).reshape(9, -1)
 
     mod_grads = jnp.concatenate([mod_early, mod_late], 2)
-    mod_grads = jnp.where(active[:, None, None, None], mod_grads, 0.0).astype(bf16)
-    mod_all = gathered_everywhere(mod_grads.reshape(units * 2, 6 * D)).reshape(-1, 6 * D)
+    mod_grads = jnp.where(active[:, None, None, None], mod_grads, 0.0).astype(bf16).reshape(rows_here, 6 * D)
+    tap_rows = jnp.pad(conv_one_grad.astype(bf16).reshape(-1), (0, 3 * D)).reshape(2, 6 * D)
+    gathered = gathered_everywhere(jnp.concatenate([mod_grads, tap_rows], 0), attn_sums)
+    conv_one_sum = gathered[:, :, rows_here:].astype(f32).sum((0, 1)).reshape(-1)[: 9 * D].reshape(9, D)
+    conv_one_sum = lax.dynamic_slice_in_dim(conv_one_sum, owner * shard, shard, axis=1)
+    mod_all = gathered.reshape(-1, 6 * D)
     grad_ada = dot_tn(act_low, mod_all)
-    grad_embed = silu_back(dot_nt(mod_all, ada_weight))[0]
+    grad_embed = jnp.where(real_row, silu_back(dot_nt(mod_all, ada_weight))[0], 0.0)
     grad_table = dot_tn(label_hot, grad_embed.astype(bf16))
     return (
-        work_y, work_x, conv_sums[:, :shard], final_qkv, final_out, final_up,
-        conv_sums[:, shard:], final_down, grad_ada, grad_table,
+        work_y, work_x, conv_one_sum, final_qkv, final_out, final_up,
+        final_taps, final_down, grad_ada, grad_table,
     )
 
 

time: 613 us -> 546 us (0.89)
  waiting for transfers between devices: 132 us -> 82.4 us
  other arithmetic: 66.5 us -> 47.6 us
    ppermute x14 -> x9, waiting for transfers between devices: 73.5 us -> 24.6 us  [swapped(): return lax.ppermute(values, 'wide', [(i, i ^ bit) for i in range(count)])]
    reduce_scatter x3, waiting for transfers between devices: 0.02 us -> 26.4 us  [owner_sum(): return lax.psum_scatter(values, 'wide', scatter_dimension=0, tiled=True)]
    ppermute x1, waiting for transfers between devices: 28.7 us -> 6.74 us  [body(): x_other = lax.ppermute(x_last, 'wide', partner)]
    ppermute x8 -> x10, waiting for transfers between devices: 23.5 us -> 8.36 us  [the longest x4 8.34 us: for_other_half(): return lax.ppermute(part.reshape(-1, LATENT, D), 'narrow', swap)]
    reshape x3 -> x15, local copies, waits for them, and re-layouts: 0.43 us -> 11 us  [the longest x1 3.16 us: body(): final_up = final_up.transpose(1, 3, 0, 2, 4).reshape(shard, hidden_width)]
    ppermute x1, waiting for transfers between devices: 0.01 us -> 7.9 us  [body(): cot_other = lax.ppermute(cot_last, 'wide', partner)]
    ppermute x1, starting transfers between devices: 1.42 us -> 8.38 us  [body(): x_other = lax.ppermute(x_last, 'wide', partner)]
    ppermute x14 -> x9, starting transfers between devices: 12.7 us -> 7.03 us  [swapped(): return lax.ppermute(values, 'wide', [(i, i ^ bit) for i in range(count)])]
  transfers between devices with their start and end apart: 35 -> 31, of which waited for: 13 -> 10; matrix products, arithmetic and copies ran while one was open for 18% -> 15% of each run, Pallas kernels for 41% -> 57%
where the time goes in v2:
time: 546 us; the launch traced here: 536 us
  Pallas kernels  308 us (56%)
  waiting for transfers between devices  82.4 us (15%)
  other arithmetic  47.6 us (9%)
  local copies, waits for them, and re-layouts  42 us (8%)
  starting transfers between devices  36.3 us (7%)
  between operations  15.2 us (3%)
    pallas_call x16, Pallas kernels, call(): pl.pallas_call(run, grid_spec=pltpu.PrefetchScalarGridSpec(num_scalar_pre...  308 us
    reduce_scatter x3, waiting for transfers between devices, owner_sum(): return lax.psum_scatter(values, 'wide', scatter_dimension=0, tiled=True)  26.4 us
    ppermute x9, waiting for transfers between devices, swapped(): return lax.ppermute(values, 'wide', [(i, i ^ bit) for i in range(count)])  24.6 us
  transfers between devices with their start and end apart: 31, of which 10 were waited for; matrix products, arithmetic and copies ran while one was open for 15% of the time, Pallas kernels for 57%

profile of v2, /device:TPU:0, one launch (start us, length us, event | category | flops | bytes accessed | tf_op | source)
XLA Modules:
  0.0 535.9 jit_solution(11522413200833422481)
XLA Ops:
  7.2 1.8 constant_dynamic-update-slice_fusion.1
  10.5 4.0 collective-permute-start.2
  25.2 5.3 all-to-all-start
  35.6 1.7 reshape.723
  38.7 2.1 reshape.724
  50.9 4.3 arrange.5
  55.6 8.4 %collective-permute-start.6 = (bf16[1,512,768]{2,1,0:T(8,128)(2,1)}, bf16[1,512,768]{2,1,0:T(8,128)(2,1)}, u32[]{:S(2)}, u32[]{:S(2)}) collective-permute-start(bf16[1,512,768]{2,1,0:T(8,128)(2,1)} %arrange.5), channel_id=1, source_target_pairs={{0,16},{2,18},{4,20},{6,22},{8,24},{10,26},{12,28},{14,30},{16,0},... | collective-permute-start | bytes 2359304 | tf_op jit(solution)/shard_map/ppermute | solution.py:800
  66.7 8.3 %collective-permute-done.refs_1_ = bf16[3,256,768]{2,1,0:T(8,128)(2,1)} collective-permute-done((bf16[3,256,768]{2,1,0:T(8,128)(2,1)}, bf16[3,256,768]{2,1,0:T(8,128)(2,1)}, u32[]{:S(2)}, u32[]{:S(2)}) %collective-permute-start) | collective-permute-done | bytes 1179680 | tf_op jit(solution)/shard_map/ppermute | solution.py:795
  75.0 7.4 %arrange.4.refs_0_ = bf16[3,512,768]{2,1,0:T(8,128)(2,1)} custom-call(s32[8]{0:T(128)} %pad_add_fusion.3.meta, bf16[4,512,768]{2,1,0:T(8,128)(2,1)} %refs_0_.5, bf16[3,256,768]{2,1,0:T(8,128)(2,1)} %collective-permute-done.refs_1_, s32[4,512,1]{2,1,0:T(8,128)} %select_select_fusion.refs_2_), custom_call_target="tpu_custom_call" | custom-call | flops 1500000000 | bytes 3000000 | tf_op jit(solution)/shard_map/arrange/pallas_call | solution.py:762
  87.7 7.5 %mix_tokens.2 = (bf16[3,512,768]{2,1,0:T(8,128)(2,1)}, bf16[3,512,768]{2,1,0:T(8,128)(2,1)}) custom-call(s32[6]{0:T(128)} %pad_add_fusion.2.meta, bf16[3,512,768]{2,1,0:T(8,128)(2,1)} %arrange.4.refs_0_, f32[3,2,7,768]{3,2,1,0:T(8,128)} %pad_maximum_fusion.10.refs_1_.refs_2_.refs_7_.refs_3_, f32[3,9,768]{2,1,0:T(8,128)} %broadcast_select_fusion.4.refs_2_.refs_3_.refs_4_), custom_call_target="tpu_custom_call" | custom-call | flops 1500000000 | bytes 2000000 | tf_op jit(solution)/shard_map/mix_tokens/pallas_call | solution.py:762
  95.2 6.7 %collective-permute-done.6.refs_1_ = bf16[1,512,768]{2,1,0:T(8,128)(2,1)} collective-permute-done((bf16[1,512,768]{2,1,0:T(8,128)(2,1)}, bf16[1,512,768]{2,1,0:T(8,128)(2,1)}, u32[]{:S(2)}, u32[]{:S(2)}) %collective-permute-start.6) | collective-permute-done | bytes 786464 | tf_op jit(solution)/shard_map/ppermute | solution.py:800
  101.9 1.8 select_bitcast_fusion.5
  103.7 1.6 pad_maximum_fusion.1
  105.5 7.4 %arrange.6.refs_0_ = bf16[3,512,768]{2,1,0:T(8,128)(2,1)} custom-call(s32[8]{0:T(128)} %pad_add_fusion.3.meta, bf16[4,512,768]{2,1,0:T(8,128)(2,1)} %refs_0_.7, bf16[3,256,768]{2,1,0:T(8,128)(2,1)} %collective-permute-done.7.refs_1_, s32[4,512,1]{2,1,0:T(8,128)} %select_select_fusion.refs_2_), custom_call_target="tpu_custom_call" | custom-call | flops 1500000000 | bytes 3000000 | tf_op jit(solution)/shard_map/arrange/pallas_call | solution.py:762
  112.9 2.9 select_bitcast_fusion.1
  115.8 2.6 pad_maximum_fusion
  122.8 4.3 arrange.7
  127.2 2.0 broadcast_select_fusion.2
  129.1 24.3 %attend.2 = (bf16[3,512,2304]{2,1,0:T(8,128)(2,1)}, bf16[3,512,768]{2,1,0:T(8,128)(2,1)}, bf16[3,512,768]{2,1,0:T(8,128)(2,1)}, bf16[3,512,768]{2,1,0:T(8,128)(2...) custom-call(s32[6]{0:T(128)} %pad_add_fusion.2.meta, bf16[3,512,768]{2,1,0:T(8,128)(2,1)} %get-tuple-element.87.refs_4_.refs_0_, ...), custom_call_target="tpu_custom_call" | custom-call | flops 4000000000 | bytes 2000000 | tf_op jit(solution)/shard_map/attend/pallas_call | solution.py:762
  153.5 5.5 %mix_tokens.3 = (bf16[3,512,768]{2,1,0:T(8,128)(2,1)}, bf16[3,512,768]{2,1,0:T(8,128)(2,1)}) custom-call(s32[6]{0:T(128)} %pad_add_fusion.2.meta, bf16[3,512,768]{2,1,0:T(8,128)(2,1)} %arrange.4.refs_0_, bf16[1,512,768]{2,1,0:T(8,128)(2,1)} %collective-permute-done.6.refs_1_, ...), custom_call_target="tpu_custom_call", output_to_operand_aliasing={{0}: (5, {}), {1}: (6, {})} | custom-call | flops 750000000 | bytes 1000000 | tf_op jit(solution)/shard_map/mix_tokens/pallas_call | solution.py:762
  158.9 15.2 %attend.3 = (bf16[3,512,2304]{2,1,0:T(8,128)(2,1)}, bf16[3,512,768]{2,1,0:T(8,128)(2,1)}, bf16[3,512,768]{2,1,0:T(8,128)(2,1)}, bf16[3,512,768]{2,1,0:T(8,128)(2...) custom-call(s32[6]{0:T(128)} %pad_add_fusion.2.meta, ...), custom_call_target="tpu_custom_call", output_to_operand_aliasing={{0}: (5, {}), {1}: (6, {}), {2}: (7, {}), {3}: (8, {}), {4}... | custom-call | flops 2000000000 | bytes 1000000 | tf_op jit(solution)/shard_map/attend/pallas_call | solution.py:762
  174.1 7.9 %collective-permute-done.10.refs_1_ = bf16[1,512,768]{2,1,0:T(8,128)(2,1)} collective-permute-done((bf16[1,512,768]{2,1,0:T(8,128)(2,1)}, bf16[1,512,768]{2,1,0:T(8,128)(2,1)}, u32[]{:S(2)}, u32[]{:S(2)}) %collective-permute-start.10) | collective-permute-done | bytes 786464 | tf_op jit(solution)/shard_map/ppermute | solution.py:848
  182.0 61.4 %feed_forward.2 = (bf16[3,512,768]{2,1,0:T(8,128)(2,1)}, f32[3,512,768]{2,1,0:T(8,128)}, f32[3,512,768]{2,1,0:T(8,128)}, bf16[768,3072]{1,0:T(8,128)(2,1)}, f32[9,1536]{1,0:T(8,128)}) custom-call(s32[6]{0:T(128)} %pad_add_fusion.2.meta, bf16[3,512,768]{2,1,0:T(8,128)(2,1)} %arrange.6.refs_0_, bf16[1,512,768]{2,1,0:T(8,128)(2,1)} %collective-permute-done.10.refs_1_, ...), custom_call_target="tpu_custom_call" | custom-call | flops 12000000000 | bytes 3000000 | tf_op jit(solution)/shard_map/feed_forward/pallas_call | solution.py:762
  244.8 67.0 %feed_forward.3 = (f32[3,512,768]{2,1,0:T(8,128)}, bf16[3,512,768]{2,1,0:T(8,128)(2,1)}, bf16[3,512,768]{2,1,0:T(8,128)(2,1)}, bf16[3,256,768]{2,1,0:T(8,128)(2,...) custom-call(s32[6]{0:T(128)} %pad_add_fusion.2.meta, ...), custom_call_target="tpu_custom_call" | custom-call | flops 12750000128 | bytes 3000000 | tf_op jit(solution)/shard_map/feed_forward/pallas_call | solution.py:762
  311.8 7.2 %reduce-scatter.4.cloned.1.call-done = bf16[48,3072]{1,0:T(8,128)(2,1)} async-done(((bf16[768,3072]{1,0:T(8,128)(2,1)}), bf16[48,3072]{1,0:T(8,128)(2,1)}) %reduce-scatter.4.cloned.1.call-update) | async-done | bytes 294928 | tf_op jit(solution)/shard_map/reduce_scatter | solution.py:881
  321.8 1.9 fusion.38.refs_1_
  323.9 2.1 slice.238
  327.4 22.0 %backward_middle.1 = (f32[3,512,768]{2,1,0:T(8,128)}, bf16[3,512,768]{2,1,0:T(8,128)(2,1)}, f32[3,2,4,768]{3,2,1,0:T(4,128)}, bf16[768,768]{1,0:T(8,128)(2,1)}) custom-call(s32[6]{0:T(128)} %pad_add_fusion.2.meta, bf16[3,512,768]{2,1,0:T(8,128)(2,1)} %arrange.6.refs_0_, bf16[1,512,768]{2,1,0:T(8,128)(2,1)} %collective-permute-done.10.refs_1_, ...), custom_call_target="tpu_custom_call" | custom-call | flops 3000000000 | bytes 3000000 | tf_op jit(solution)/shard_map/backward_middle/pallas_call | solution.py:762
  349.3 32.7 %backward_heads.1 = (bf16[3,512,2304]{2,1,0:T(8,128)(2,1)}, bf16[768,3072]{1,0:T(8,128)(2,1)}) custom-call(s32[6]{0:T(128)} %pad_add_fusion.2.meta, bf16[3,512,2304]{2,1,0:T(8,128)(2,1)} %get-tuple-element.100.refs_0_, bf16[3,512,768]{2,1,0:T(8,128)(2,1)} %get-tuple-element.118.refs_1_, bf16[3,512,768]{2,1,0:T(8,128)(2,1)} %get-tuple-element.119.refs_2_, ...), custom_call_target="tpu_custom_call" | custom-call | flops 8999999488 | bytes 3000000 | tf_op jit(solution)/shard_map/backward_heads/pallas_call | solution.py:762
  382.0 3.6 place_back.2
  386.2 15.7 %backward_tokens.2 = (bf16[3,512,768]{2,1,0:T(8,128)(2,1)}, bf16[3,512,768]{2,1,0:T(8,128)(2,1)}, bf16[3,256,768]{2,1,0:T(8,128)(2,1)}, f32[3,2,2,768]{3,2,1,0:T(2,128)}, f32[9,768]{1,0:T(8,128)}) custom-call(s32[6]{0:T(128)} %pad_add_fusion.2.meta, bf16[3,512,2304]{2,1,0:T(8,128)(2,1)} %get-tuple-element.133.refs_0_, ...), custom_call_target="tpu_custom_call" | custom-call | flops 1500000000 | bytes 1000000 | tf_op jit(solution)/shard_map/backward_tokens/pallas_call | solution.py:762
  401.8 2.1 slice.240
  405.5 3.2 select_add_fusion.1
  410.1 2.1 maximum_select_fusion
  412.2 25.6 %backward_tokens.3 = (bf16[3,512,768]{2,1,0:T(8,128)(2,1)}, bf16[3,512,768]{2,1,0:T(8,128)(2,1)}, bf16[3,256,768]{2,1,0:T(8,128)(2,1)}, f32[3,2,2,768]{3,2,1,0:T(2,128)}, f32[9,768]{1,0:T(8,128)}) custom-call(s32[6]{0:T(128)} %pad_add_fusion.2.meta, ...), custom_call_target="tpu_custom_call", output_to_operand_aliasing={{0}: (8, {}), {1}: (9, {}), {2}: (10, {}), {3}: (11, {})} | custom-call | flops 3000000000 | bytes 2000000 | tf_op jit(solution)/shard_map/backward_tokens/pallas_call | solution.py:762
  440.4 3.8 collective-permute-done.17
  444.9 1.9 add_bitcast_fusion
  447.4 3.8 place_back.3
  453.2 5.2 collective-permute-done.18
  460.8 13.0 %collective-permute-done.19 = bf16[2,2,8,4608]{3,2,1,0:T(8,128)(2,1)S(1)} collective-permute-done((bf16[2,2,8,4608]{3,2,1,0:T(8,128)(2,1)S(1)}, bf16[2,2,8,4608]{3,2,1,0:T(8,128)(2,1)S(1)}, u32[]{:S(2)}, u32[]{:S(2)}) %collective-permute-start.19) | collective-permute-done | bytes 294944 | tf_op jit(solution)/shard_map/ppermute | solution.py:588
  474.8 19.2 %reduce-scatter.8.cloned.1.call-done = bf16[48,3072]{1,0:T(8,128)(2,1)} async-done(((bf16[768,3072]{1,0:T(8,128)(2,1)}), bf16[48,3072]{1,0:T(8,128)(2,1)}) %reduce-scatter.8.cloned.1.call-update) | async-done | bytes 294928 | tf_op jit(solution)/shard_map/reduce_scatter | solution.py:881
  498.6 3.2 reshape.745
  502.0 6.4 %collective-permute-done.20 = bf16[4,2,8,4608]{3,2,1,0:T(8,128)(2,1)} collective-permute-done((bf16[4,2,8,4608]{3,2,1,0:T(8,128)(2,1)}, bf16[4,2,8,4608]{3,2,1,0:T(8,128)(2,1)}, u32[]{:S(2)}, u32[]{:S(2)}) %collective-permute-start.20) | collective-permute-done | bytes 589856 | tf_op jit(solution)/shard_map/ppermute | solution.py:588
  511.4 2.5 select_add_fusion
  513.9 1.6 collective-permute-start.22
  515.4 2.1 maximum_select_fusion.1
  517.5 4.5 collective-permute-done.22
  526.5 1.8 fusion
  (286 shorter events, 72.3 us)
Async XLA Ops:
  7.2 9.0 %slice-start = ((bf16[4,512,768]{2,1,0:T(8,128)(2,1)}), bf16[1,512,768]{2,1,0:T(8,128)(2,1)S(1)}, s32[]{:S(2)}) async-start(bf16[4,512,768]{2,1,0:T(8,128)(2,1)} %refs_0_.5), calls=%async_computation.9 | async-start | bytes 1572864 | tf_op jit(solution)/shard_map/slice | solution.py:793
  7.2 11.2 %slice-start.2 = ((bf16[4,512,768]{2,1,0:T(8,128)(2,1)}), bf16[1,512,768]{2,1,0:T(8,128)(2,1)S(1)}, s32[]{:S(2)}) async-start(bf16[4,512,768]{2,1,0:T(8,128)(2,1)} %refs_0_.7), calls=%async_computation.11 | async-start | bytes 1572864 | tf_op jit(solution)/shard_map/slice | solution.py:793
  10.5 38.0 %collective-permute-start.2 = (bf16[48,3072]{1,0:T(8,128)(2,1)}, bf16[48,3072]{1,0:T(8,128)(2,1)}, u32[]{:S(2)}, u32[]{:S(2)}) collective-permute-start(bf16[48,3072]{1,0:T(8,128)(2,1)} %constant_dynamic-update-slice_fusion), channel_id=1, source_target_pairs={{0,16},{2,18},{4,20},{6,22},{8,24},{10,26},{12,28},{14,30},{16,0},... | collective-permute-start | bytes 884744 | tf_op jit(solution)/shard_map/ppermute | solution.py:588
  14.5 34.0 %collective-permute-start.3 = (bf16[48,3072]{1,0:T(8,128)(2,1)}, bf16[48,3072]{1,0:T(8,128)(2,1)}, u32[]{:S(2)}, u32[]{:S(2)}) collective-permute-start(bf16[48,3072]{1,0:T(8,128)(2,1)} %constant_dynamic-update-slice_fusion), channel_id=1, source_target_pairs={{0,24},{2,26},{4,28},{6,30},{8,16},{10,18},{12,20},{14,22},{16,8},... | collective-permute-start | bytes 884744 | tf_op jit(solution)/shard_map/ppermute | solution.py:588
  15.9 30.0 %collective-permute-start.1 = (bf16[48,3072]{1,0:T(8,128)(2,1)}, bf16[48,3072]{1,0:T(8,128)(2,1)}, u32[]{:S(2)}, u32[]{:S(2)}) collective-permute-start(bf16[48,3072]{1,0:T(8,128)(2,1)} %constant_dynamic-update-slice_fusion), channel_id=1, source_target_pairs={{0,8},{2,10},{4,12},{6,14},{8,0},{10,2},{12,4},{14,6},{16,24},{18,... | collective-permute-start | bytes 884744 | tf_op jit(solution)/shard_map/ppermute | solution.py:588
  16.1 3.7 copy-start.21
  16.1 3.9 copy-start.16
  16.1 3.9 copy-start.17
  16.1 4.1 copy-start.18
  16.1 4.3 copy-start.19
  16.1 5.4 %copy-start.29 = (bf16[1000,48]{0,1:T(8,128)(2,1)S(1)}, bf16[1000,48]{0,1:T(8,128)(2,1)}, u32[]{:S(2)}) copy-start(bf16[1000,48]{0,1:T(8,128)(2,1)} %param.23) | copy-start | bytes 288004
  16.1 7.1 %copy-start.2 = (bf16[48,4608]{1,0:T(8,128)(2,1)S(1)}, bf16[48,4608]{1,0:T(8,128)(2,1)}, u32[]{:S(2)}) copy-start(bf16[48,4608]{1,0:T(8,128)(2,1)} %param.22) | copy-start | bytes 1327108
  16.9 34.0 %collective-permute-start.4 = (bf16[1,256,768]{2,1,0:T(8,128)(2,1)}, bf16[1,256,768]{2,1,0:T(8,128)(2,1)}, u32[]{:S(2)}, u32[]{:S(2)}) collective-permute-start(bf16[1,256,768]{2,1,0:T(8,128)(2,1)} %bitcast.9), channel_id=1, source_target_pairs={{0,1},{1,0},{2,3},{3,2},{4,5},{5,4},{6,7},{7,6},{8,9},{9,8},{10,11... | collective-permute-start | bytes 1179656 | tf_op jit(solution)/shard_map/ppermute | solution.py:795
  19.2 36.0 %collective-permute-start.5 = (bf16[1,256,768]{2,1,0:T(8,128)(2,1)}, bf16[1,256,768]{2,1,0:T(8,128)(2,1)}, u32[]{:S(2)}, u32[]{:S(2)}) collective-permute-start(bf16[1,256,768]{2,1,0:T(8,128)(2,1)} %bitcast.11), channel_id=1, source_target_pairs={{0,1},{1,0},{2,3},{3,2},{4,5},{5,4},{6,7},{7,6},{8,9},{9,8},{10,11... | collective-permute-start | bytes 1179656 | tf_op jit(solution)/shard_map/ppermute | solution.py:795
  23.9 7.3 %copy-start.20 = (s32[64]{0:T(128)S(1)}, s32[64]{0:T(128)}, u32[]{:S(2)}) copy-start(s32[64]{0:T(128)} %param.26) | copy-start | bytes 772
  25.2 57.3 %all-to-all-start = ((bf16[16,6,4992]{2,1,0:T(8,128)(2,1)}), bf16[16,6,4992]{2,1,0:T(8,128)(2,1)}, u32[]{:S(2)}, u32[]{:S(2)}) async-start(bf16[16,6,4992]{2,1,0:T(8,128)(2,1)} %pad_maximum_fusion.3), calls=%async_computation | async-start | bytes 2555904 | tf_op jit(solution)/shard_map/all_to_all | solution.py:718
  30.5 151.6 %all-gather.3.cloned.1.call-start = ((), (), s32[]{:S(2)}) async-start(), calls=%async_computation.4 | async-start | bytes 5013504 | tf_op jit(solution)/shard_map/all_gather | solution.py:734
  32.5 12.2 %copy-start.23 = (pred[4]{0:T(512)(128)(4,1)}, pred[4]{0:T(512)(128)(4,1)S(1)}, u32[]{:S(2)}) copy-start(pred[4]{0:T(512)(128)(4,1)S(1)} %broadcast_compare_fusion.5) | copy-start | bytes 16
  34.5 6.4 %copy-start.27 = (pred[3]{0:T(512)(128)(4,1)}, pred[3]{0:T(512)(128)(4,1)S(1)}, u32[]{:S(2)}) copy-start(pred[3]{0:T(512)(128)(4,1)S(1)} %fusion.48) | copy-start | bytes 13
  37.3 5.4 %slice-start.1 = ((bf16[4,512,768]{2,1,0:T(8,128)(2,1)}), bf16[3,512,768]{2,1,0:T(8,128)(2,1)S(1)}, s32[]{:S(2)}) async-start(bf16[4,512,768]{2,1,0:T(8,128)(2,1)} %refs_0_.5), calls=%async_computation.10 | async-start | bytes 4718592 | tf_op jit(solution)/shard_map/slice | solution.py:793
  45.9 29.1 %collective-permute-start = (bf16[3,256,768]{2,1,0:T(8,128)(2,1)}, bf16[3,256,768]{2,1,0:T(8,128)(2,1)}, u32[]{:S(2)}, u32[]{:S(2)}) collective-permute-start(bf16[3,256,768]{2,1,0:T(8,128)(2,1)} %bitcast.2), channel_id=1, source_target_pairs={{0,1},{1,0},{2,3},{3,2},{4,5},{5,4},{6,7},{7,6},{8,9},{9,8},{10,11... | collective-permute-start | bytes 3538952 | tf_op jit(solution)/shard_map/ppermute | solution.py:795
  55.2 8.8 %slice-start.3 = ((bf16[4,512,768]{2,1,0:T(8,128)(2,1)}), bf16[3,512,768]{2,1,0:T(8,128)(2,1)S(1)}, s32[]{:S(2)}) async-start(bf16[4,512,768]{2,1,0:T(8,128)(2,1)} %refs_0_.7), calls=%async_computation.12 | async-start | bytes 4718592 | tf_op jit(solution)/shard_map/slice | solution.py:793
  55.2 46.7 %collective-permute-start.8 = (bf16[4,48,3072]{2,1,0:T(8,128)(2,1)}, bf16[4,48,3072]{2,1,0:T(8,128)(2,1)}, u32[]{:S(2)}, u32[]{:S(2)}) collective-permute-start(bf16[4,48,3072]{2,1,0:T(8,128)(2,1)} %bitcast.168), channel_id=1, source_target_pairs={{0,4},{2,6},{4,0},{6,2},{8,12},{10,14},{12,8},{14,10},{16,20},{18,... | collective-permute-start | bytes 3538952 | tf_op jit(solution)/shard_map/ppermute | solution.py:588
  55.6 46.3 %collective-permute-start.6 = (bf16[1,512,768]{2,1,0:T(8,128)(2,1)}, bf16[1,512,768]{2,1,0:T(8,128)(2,1)}, u32[]{:S(2)}, u32[]{:S(2)}) collective-permute-start(bf16[1,512,768]{2,1,0:T(8,128)(2,1)} %arrange.5), channel_id=1, source_target_pairs={{0,16},{2,18},{4,20},{6,22},{8,24},{10,26},{12,28},{14,30},{16,0},... | collective-permute-start | bytes 2359304 | tf_op jit(solution)/shard_map/ppermute | solution.py:800
  65.2 36.7 %collective-permute-start.7 = (bf16[3,256,768]{2,1,0:T(8,128)(2,1)}, bf16[3,256,768]{2,1,0:T(8,128)(2,1)}, u32[]{:S(2)}, u32[]{:S(2)}) collective-permute-start(bf16[3,256,768]{2,1,0:T(8,128)(2,1)} %bitcast.22), channel_id=1, source_target_pairs={{0,1},{1,0},{2,3},{3,2},{4,5},{5,4},{6,7},{7,6},{8,9},{9,8},{10,11... | collective-permute-start | bytes 3538952 | tf_op jit(solution)/shard_map/ppermute | solution.py:795
  105.4 139.4 %all-gather.5.cloned.1.call-start = ((), (), s32[]{:S(2)}) async-start(), calls=%async_computation.5 | async-start | bytes 5013504 | tf_op jit(solution)/shard_map/all_gather | solution.py:734
  105.4 7.5 %collective-permute-start.9 = (bf16[4,2,48,3072]{3,2,1,0:T(8,128)(2,1)}, bf16[4,2,48,3072]{3,2,1,0:T(8,128)(2,1)}, u32[]{:S(2)}, u32[]{:S(2)}) collective-permute-start(bf16[4,2,48,3072]{3,2,1,0:T(8,128)(2,1)} %pad_maximum_fusion.1), channel_id=1, source_target_pairs={{0,2},{2,0},{4,6},{6,4},{8,10},{10,8},{12,14},{14,12},{16,18},{18,... | collective-permute-start | bytes 7077896 | tf_op jit(solution)/shard_map/ppermute | solution.py:588
  118.4 200.6 %reduce-scatter.4.cloned.1.call-start = ((), (), s32[]{:S(2)}) async-start(), calls=%async_computation.6 | async-start | bytes 5013504 | tf_op jit(solution)/shard_map/reduce_scatter | solution.py:881
  127.2 54.9 %collective-permute-start.10 = (bf16[1,512,768]{2,1,0:T(8,128)(2,1)}, bf16[1,512,768]{2,1,0:T(8,128)(2,1)}, u32[]{:S(2)}, u32[]{:S(2)}) collective-permute-start(bf16[1,512,768]{2,1,0:T(8,128)(2,1)} %arrange.7), channel_id=1, source_target_pairs={{0,16},{2,18},{4,20},{6,22},{8,24},{10,26},{12,28},{14,30},{16,0},... | collective-permute-start | bytes 2359304 | tf_op jit(solution)/shard_map/ppermute | solution.py:848
  243.5 168.7 %reduce-scatter.6.cloned.1.call-start = ((), (), s32[]{:S(2)}) async-start(), calls=%async_computation.7 | async-start | bytes 5222400 | tf_op jit(solution)/shard_map/reduce_scatter | solution.py:881
  318.9 4.8 copy-start.28
  319.0 175.0 %reduce-scatter.8.cloned.1.call-start = ((), (), s32[]{:S(2)}) async-start(), calls=%async_computation.8 | async-start | bytes 5013504 | tf_op jit(solution)/shard_map/reduce_scatter | solution.py:881
  320.4 61.6 %collective-permute-start.12 = (bf16[3,256,768]{2,1,0:T(8,128)(2,1)}, bf16[3,256,768]{2,1,0:T(8,128)(2,1)}, u32[]{:S(2)}, u32[]{:S(2)}) collective-permute-start(bf16[3,256,768]{2,1,0:T(8,128)(2,1)} %get-tuple-element.123), channel_id=1, source_target_pairs={{0,1},{1,0},{2,3},{3,2},{4,5},{5,4},{6,7},{7,6},{8,9},{9,8},{10,11... | collective-permute-start | bytes 3538952 | tf_op jit(solution)/shard_map/ppermute | solution.py:956
  326.0 56.1 %collective-permute-start.11 = (bf16[1,512,768]{2,1,0:T(8,128)(2,1)}, bf16[1,512,768]{2,1,0:T(8,128)(2,1)}, u32[]{:S(2)}, u32[]{:S(2)}) collective-permute-start(bf16[1,512,768]{2,1,0:T(8,128)(2,1)} %slice.238), channel_id=1, source_target_pairs={{0,16},{2,18},{4,20},{6,22},{8,24},{10,26},{12,28},{14,30},{16,0},... | collective-permute-start | bytes 2359304 | tf_op jit(solution)/shard_map/ppermute | solution.py:955
  385.7 23.1 %collective-permute-start.13 = (bf16[1,256,768]{2,1,0:T(8,128)(2,1)}, bf16[1,256,768]{2,1,0:T(8,128)(2,1)}, u32[]{:S(2)}, u32[]{:S(2)}) collective-permute-start(bf16[1,256,768]{2,1,0:T(8,128)(2,1)} %get-tuple-element.131), channel_id=1, source_target_pairs={{0,1},{1,0},{2,3},{3,2},{4,5},{5,4},{6,7},{7,6},{8,9},{9,8},{10,11... | collective-permute-start | bytes 1179656 | tf_op jit(solution)/shard_map/ppermute | solution.py:961
  404.0 33.9 %collective-permute-start.14 = (bf16[1,512,768]{2,1,0:T(8,128)(2,1)}, bf16[1,512,768]{2,1,0:T(8,128)(2,1)}, u32[]{:S(2)}, u32[]{:S(2)}) collective-permute-start(bf16[1,512,768]{2,1,0:T(8,128)(2,1)} %slice.240), channel_id=1, source_target_pairs={{0,16},{2,18},{4,20},{6,22},{8,24},{10,26},{12,28},{14,30},{16,0},... | collective-permute-start | bytes 2359304 | tf_op jit(solution)/shard_map/ppermute | solution.py:960
  404.0 40.9 %collective-permute-start.23 = (bf16[48,3072]{1,0:T(8,128)(2,1)}, bf16[48,3072]{1,0:T(8,128)(2,1)}, u32[]{:S(2)}, u32[]{:S(2)}) collective-permute-start(bf16[48,3072]{1,0:T(8,128)(2,1)} %reduce-scatter.4.cloned.1.call-done), channel_id=1, source_target_pairs={{0,1},{1,0},{2,3},{3,2},{4,5},{5,4},{6,7},{7,6},{8,9},{9,8},{10,11... | collective-permute-start | bytes 884744 | tf_op jit(solution)/shard_map/ppermute | solution.py:645
  439.8 4.4 collective-permute-start.17
  440.4 3.8 copy-start.8
  444.9 13.5 %collective-permute-start.18 = (bf16[1,2,8,4608]{3,2,1,0:T(8,128)(2,1)}, bf16[1,2,8,4608]{3,2,1,0:T(8,128)(2,1)}, u32[]{:S(2)}, u32[]{:S(2)}) collective-permute-start(bf16[1,2,8,4608]{3,2,1,0:T(8,128)(2,1)} %maximum_select_fusion.2), channel_id=1, source_target_pairs={{0,16},{2,18},{4,20},{6,22},{8,24},{10,26},{12,28},{14,30},{16,0},... | collective-permute-start | bytes 442376 | tf_op jit(solution)/shard_map/ppermute | solution.py:588
  446.8 12.8 %collective-permute-start.24 = (bf16[48,3200]{1,0:T(8,128)(2,1)}, bf16[48,3200]{1,0:T(8,128)(2,1)}, u32[]{:S(2)}, u32[]{:S(2)}) collective-permute-start(bf16[48,3200]{1,0:T(8,128)(2,1)} %reduce-scatter.6.cloned.1.call-done), channel_id=1, source_target_pairs={{0,1},{1,0},{2,3},{3,2},{4,5},{5,4},{6,7},{7,6},{8,9},{9,8},{10,11... | collective-permute-start | bytes 921608 | tf_op jit(solution)/shard_map/ppermute | solution.py:645
  451.2 50.6 %collective-permute-start.16 = (bf16[1,256,768]{2,1,0:T(8,128)(2,1)}, bf16[1,256,768]{2,1,0:T(8,128)(2,1)S(1)}, u32[]{:S(2)}, u32[]{:S(2)}) collective-permute-start(bf16[1,256,768]{2,1,0:T(8,128)(2,1)} %get-tuple-element.145), channel_id=1, source_target_pairs={{0,1},{1,0},{2,3},{3,2},{4,5},{5,4},{6,7},{7,6},{8,9},{9,8},{10,11... | collective-permute-start | bytes 1179656 | tf_op jit(solution)/shard_map/ppermute | solution.py:967
  452.7 57.3 %collective-permute-start.15 = (bf16[3,256,768]{2,1,0:T(8,128)(2,1)}, bf16[3,256,768]{2,1,0:T(8,128)(2,1)}, u32[]{:S(2)}, u32[]{:S(2)}) collective-permute-start(bf16[3,256,768]{2,1,0:T(8,128)(2,1)} %get-tuple-element.142), channel_id=1, source_target_pairs={{0,1},{1,0},{2,3},{3,2},{4,5},{5,4},{6,7},{7,6},{8,9},{9,8},{10,11... | collective-permute-start | bytes 3538952 | tf_op jit(solution)/shard_map/ppermute | solution.py:967
  459.6 14.3 %collective-permute-start.19 = (bf16[2,2,8,4608]{3,2,1,0:T(8,128)(2,1)S(1)}, bf16[2,2,8,4608]{3,2,1,0:T(8,128)(2,1)S(1)}, u32[]{:S(2)}, u32[]{:S(2)}) collective-permute-start(bf16[2,2,8,4608]{3,2,1,0:T(8,128)(2,1)S(1)} %maximum_bitcast_fusion), channel_id=1, source_target_pairs={{0,8},{2,10},{4,12},{6,14},{8,0},{10,2},{12,4},{14,6},{16,24},{18,... | collective-permute-start | bytes 884744 | tf_op jit(solution)/shard_map/ppermute | solution.py:588
  460.8 34.2 %copy-start.1 = (f32[1,48,3072]{2,1,0:T(8,128)S(1)}, f32[1,48,3072]{2,1,0:T(8,128)}, u32[]{:S(2)}) copy-start(f32[1,48,3072]{2,1,0:T(8,128)} %add_bitcast_fusion) | copy-start | bytes 1769476
  494.0 14.3 %collective-permute-start.20 = (bf16[4,2,8,4608]{3,2,1,0:T(8,128)(2,1)}, bf16[4,2,8,4608]{3,2,1,0:T(8,128)(2,1)}, u32[]{:S(2)}, u32[]{:S(2)}) collective-permute-start(bf16[4,2,8,4608]{3,2,1,0:T(8,128)(2,1)} %bitcast.58), channel_id=1, source_target_pairs={{0,4},{2,6},{4,0},{6,2},{8,12},{10,14},{12,8},{14,10},{16,20},{18,... | collective-permute-start | bytes 1769480 | tf_op jit(solution)/shard_map/ppermute | solution.py:588
  509.9 13.6 %collective-permute-start.21 = (bf16[8,2,8,4608]{3,2,1,0:T(8,128)(2,1)S(1)}, bf16[8,2,8,4608]{3,2,1,0:T(8,128)(2,1)S(1)}, u32[]{:S(2)}, u32[]{:S(2)}) collective-permute-start(bf16[8,2,8,4608]{3,2,1,0:T(8,128)(2,1)S(1)} %bitcast.170), channel_id=1, source_target_pairs={{0,2},{2,0},{4,6},{6,4},{8,10},{10,8},{12,14},{14,12},{16,18},{18,... | collective-permute-start | bytes 3538952 | tf_op jit(solution)/shard_map/ppermute | solution.py:588
  513.9 8.1 %collective-permute-start.22 = (bf16[48,3072]{1,0:T(8,128)(2,1)S(1)}, bf16[48,3072]{1,0:T(8,128)(2,1)S(1)}, u32[]{:S(2)}, u32[]{:S(2)}) collective-permute-start(bf16[48,3072]{1,0:T(8,128)(2,1)S(1)} %copy-done.12), channel_id=1, source_target_pairs={{0,1},{1,0},{2,3},{3,2},{4,5},{5,4},{6,7},{7,6},{8,9},{9,8},{10,11... | collective-permute-start | bytes 884744 | tf_op jit(solution)/shard_map/ppermute | solution.py:645
  (17 other events, 32.3 us)
Sparse Core Ops, SparseCore 0:
  105.5 71.3 all-gather.2
  179.1 52.5 all-gather.4
  243.6 75.2 reduce-scatter.3
  323.3 82.3 reduce-scatter.5
  412.3 81.6 reduce-scatter.7

commit v3 on v2

--- a/solution.py
+++ b/solution.py
@@ -435,7 +435,7 @@
         dout_o[...] = acc_out[...].astype(bf16)
 
 
-def backward_heads(meta, qkv, grad_att, prob, mix, dout, dqkv_o, grad_o, acc):
+def backward_heads(shard, meta, odd, qkv, grad_att, prob, mix, dout, dqkv_o, keep_o, send_o, acc):
     unit = pl.program_id(0)
     width = grad_att.shape[2]
 
@@ -487,13 +487,25 @@
 
     @pl.when(unit == pl.num_programs(0) - 1)
     def _():
-        grad_o[:, : 3 * width] = acc[...].astype(bf16)
-        grad_o[:, 3 * width :] = dout[...]
+        def put(parity):
+            for owner in range(width // shard):
+                out = keep_o if owner % 2 == parity else send_o
+                rows, to = slice(owner * shard, (owner + 1) * shard), slice(owner // 2 * shard, (owner // 2 + 1) * shard)
+                out[to, : 3 * width] = acc[rows, :].astype(bf16)
+                out[to, 3 * width :] = dout[rows, :]
+
+        @pl.when(odd[0] == 0)
+        def _():
+            put(0)
+
+        @pl.when(odd[0] != 0)
+        def _():
+            put(1)
 
 
 def backward_tokens(
     base, meta, dqkv, x, gm, mod, taps, spots, qkv_w,
-    dx_o, own_o, far_o, mod_o, tap_o, grad_mix, hidden, grad_hidden, dtap,
+    own_o, far_o, mod_o, dx_o, tap_o, grad_mix, hidden, grad_hidden, dtap,
 ):
     unit = pl.program_id(0) + base
     width = x.shape[2]
@@ -615,7 +627,26 @@
     return jnp.stack(ordered(values, other, bit), axis), *waits
 
 
-def gathered_everywhere(values, wait):
+def summed(keep, other):
+    return (keep.astype(f32) + other.astype(f32)).astype(keep.dtype)
+
+
+def between_pair(values, bit):
+    pairs = values.reshape((values.shape[0] // 2, 2) + values.shape[1:])
+    keep, send = ordered(pairs[:, 0], pairs[:, 1], bit)
+    return summed(keep, swapped(send, bit))
+
+
+def between_far(values):
+    place = lax.axis_index("wide") // 4
+    total = lax.dynamic_index_in_dim(values, place, 0, keepdims=False).astype(f32)
+    for mask in range(4, lax.axis_size("wide"), 4):
+        send = lax.dynamic_index_in_dim(values, place ^ (mask // 4), 0, keepdims=False)
+        total = total + swapped(send, mask).astype(f32)
+    return total.astype(values.dtype)
+
+
+def gathered_everywhere(values, *waits):
     lane, count = lax.axis_index("narrow"), lax.axis_size("narrow")
     if count == 2:
         other = lax.ppermute(values, "narrow", [(0, 1), (1, 0)])
@@ -625,10 +656,10 @@
     values = values[None]
     for bit in reversed(bits_of(lax.axis_size("wide"))):
         if bit == 2:
-            values = after(values, wait)
+            values, *waits = joined(values, *waits)
         values = jnp.stack(ordered(values, swapped(values, bit), bit), 1)
         values = values.reshape((-1,) + values.shape[2:])
-    return values
+    return values, *waits
 
 
 def joined(*values):
@@ -639,12 +670,14 @@
     return lax.optimization_barrier((value, *earlier))[0]
 
 
-def narrow_sum(values):
-    count = lax.axis_size("narrow")
-    if count == 2:
-        other = lax.ppermute(values, "narrow", [(0, 1), (1, 0)])
-        return values.astype(f32) + other.astype(f32)
-    return lax.psum(values, "narrow").astype(f32)
+def narrow_other(values):
+    return lax.ppermute(values, "narrow", [(0, 1), (1, 0)])
+
+
+def narrow_sum(values, other):
+    if other is None:
+        return lax.psum(values, "narrow").astype(f32)
+    return values.astype(f32) + other.astype(f32)
 
 
 def body(
@@ -886,9 +919,10 @@
         [gbb, ffn_in, ffn_second, unit_taps(conv_two[1]), branch_b, grad_ffn, middle, mod, spots, ffn_taps_0],
         [unit_spec, unit_spec, weight_spec, per_unit(9, columns), unit_spec, unit_spec, unit_spec,
          per_unit(2, 7, D), per_unit(1, HALF), tap_spec],
-        [unit_floats, unit_values, unit_values, struct(units, LATENT, D), struct(D, 2 * columns + 128), tap_grad,
-         unit_floats],
-        [unit_spec, unit_spec, unit_spec, per_unit(LATENT, D), whole(D, 2 * columns + 128), tap_spec, unit_spec],
+        [unit_floats, struct(1, *tokens_shape), unit_values, struct(units, LATENT, D), struct(D, 2 * columns + 128),
+         tap_grad, unit_floats],
+        [unit_spec, whole(1, *tokens_shape), unit_spec, per_unit(LATENT, D), whole(D, 2 * columns + 128), tap_spec,
+         unit_spec],
         work + slot_pair, 17e9,
     )
     sums_1 = owner_sum(after(ffn_grad_1, sums_0))
@@ -903,13 +937,15 @@
         [unit_spec, unit_spec, per_unit(2, 4, D), whole(D, D)],
         [pltpu.VMEM(tokens_shape, bf16), pltpu.VMEM((D, D), f32)], 4e9,
     )
-    head_grads, attn_grad = call(
-        backward_heads, "backward_heads", units, meta, [projected, grad_att, probs, mixed, out_grad],
-        [per_unit(HALF, 3 * D), unit_spec, unit_spec, unit_spec, whole(D, D)],
-        [struct(units, HALF, 3 * D), struct(D, 4 * D)], [per_unit(HALF, 3 * D), whole(D, 4 * D)],
+    head_grads, attn_keep, attn_send = call(
+        partial(backward_heads, shard), "backward_heads", units, meta,
+        [(owner % 2).reshape(1), projected, grad_att, probs, mixed, out_grad],
+        [pl.BlockSpec(memory_space=pltpu.SMEM), per_unit(HALF, 3 * D), unit_spec, unit_spec, unit_spec, whole(D, D)],
+        [struct(units, HALF, 3 * D), struct(D // 2, 4 * D), struct(D // 2, 4 * D)],
+        [per_unit(HALF, 3 * D), whole(D // 2, 4 * D), whole(D // 2, 4 * D)],
         [pltpu.VMEM((D, 3 * D), f32)], 12e9,
     )
-    attn_sums = owner_sum(after(attn_grad, sums_1))
+    attn_sums = summed(attn_keep, swapped(attn_send, 1)).reshape(owners // 2, shard, 4 * D)
 
     def tokens_call(base, count, before):
         spec = per_unit(*tokens_shape, base=base)
@@ -918,10 +954,10 @@
             [head_grads, x, grad_mid, mod, taps_one, spots, attn_full],
             [per_unit(HALF, 3 * D, base=base), spec, spec, per_unit(2, 7, D, base=base), per_unit(9, D, base=base), per_unit(1, HALF, base=base),
              whole(D, 3 * D)],
-            [unit_values, unit_values, struct(units, LATENT, D), struct(units, 2, 2, D, kind=f32),
+            [unit_values, struct(units, LATENT, D), struct(units, 2, 2, D, kind=f32), struct(1, *tokens_shape),
              struct(9, D, kind=f32)],
-            [spec, spec, per_unit(LATENT, D, base=base), per_unit(2, 2, D, base=base), whole(9, D)],
-            [pltpu.VMEM(tokens_shape, f32)] * 3 + [pltpu.VMEM((2, 72, D), f32)], 6e9, before,
+            [spec, per_unit(LATENT, D, base=base), per_unit(2, 2, D, base=base), whole(1, *tokens_shape), whole(9, D)],
+            [pltpu.VMEM(tokens_shape, f32)] * 3 + [pltpu.VMEM((2, 72, D), f32)], 60e9, before,
         )
 
     def finished(pieces):
@@ -952,47 +988,54 @@
         return lax.psum_scatter(full.reshape(slots, 2 * HALF, D), "narrow", scatter_dimension=1, tiled=True)
 
     if balanced:
-        y_back = lax.ppermute(y_units[2:], "wide", partner)
+        y_back = lax.ppermute(y_units, "wide", partner)
         y_far = lax.ppermute(y_far, "narrow", swap)
-        head_grads, y_back, y_far = lax.optimization_barrier((head_grads, y_back, y_far))
+        head_grads, y_back, y_far, other_0 = joined(head_grads, y_back, y_far, narrow_other(sums_0))
         y_last, y_last_far = placed(y_back)
-        dx_units, dx_own, dx_far, mod_early, taps_a = tokens_call(2, 1, ())
-        x_back = lax.ppermute(dx_units[2:], "wide", partner)
+        dx_own, dx_far, mod_early, dx_last, taps_a = tokens_call(2, 1, ())
+        x_back = lax.ppermute(dx_last, "wide", partner)
         y_last_far = lax.ppermute(y_last_far, "narrow", swap)
-        work_y = finished([(y_own, y_far), (y_last, y_last_far)])
-        head_grads, sums_1, work_y = lax.optimization_barrier((head_grads, sums_1, work_y))
-        _, dx_own, dx_far, mod_early, taps_b = tokens_call(0, 2, (dx_units, dx_own, dx_far, mod_early))
-        mod_early, x_back, dx_far = lax.optimization_barrier((mod_early, x_back, dx_far))
+        head_grads, sums_1, attn_sums = joined(head_grads, sums_1, attn_sums)
+        attn_sums = between_pair(attn_sums, 2)
+        other_1 = narrow_other(sums_1)
+        dx_own, dx_far, mod_early, _, taps_b = tokens_call(0, 2, (dx_own, dx_far, mod_early))
+        mod_early, x_back, dx_far, attn_sums, y_own, sums_0, other_1 = joined(
+            mod_early, x_back, dx_far, attn_sums, y_own, sums_0, other_1
+        )
+        attn_sums = between_far(attn_sums)
         x_last, x_last_far = placed(x_back)
         dx_far, x_last_far = [lax.ppermute(v, "narrow", swap) for v in (dx_far, x_last_far)]
-        work_x = finished([(dx_own, dx_far), (x_last, x_last_far)])
+        work_y = finished([(y_own, y_far), (y_last, y_last_far)])
         conv_one_grad = taps_a + taps_b
     else:
         work_y = rows_back(y_own, y_far)
-        dx_units, dx_own, dx_far, mod_early, taps_a = tokens_call(0, units, ())
+        dx_own, dx_far, mod_early, _, taps_a = tokens_call(0, units, ())
+        attn_sums, dx_far, other_0, other_1 = between_far(between_pair(attn_sums, 2)), dx_far, None, None
         work_x = rows_back(dx_own, dx_far)
         conv_one_grad = taps_a
-
-    attn_final = narrow_sum(attn_sums)
-    final_qkv, final_out = attn_final[:, : 3 * D], attn_final[:, 3 * D :]
-    second = narrow_sum(sums_1)
-    ffn_final = jnp.stack([narrow_sum(sums_0), second[:, : 2 * columns]])
-    final_up = ffn_final[:, :, :columns].reshape(PARTS, shard, per_part, owners, shard)
-    final_up = final_up.transpose(1, 3, 0, 2, 4).reshape(shard, hidden_width)
-    final_down = ffn_final[:, :, columns:].reshape(PARTS, shard, per_part, D).swapaxes(1, 2).reshape(-1, D)
-    final_taps = second[:, 2 * columns : 2 * columns + 9 * PARTS * per_part].reshape(shard, PARTS, per_part, 9)
-    final_taps = final_taps.transpose(3, 1, 2, 0).reshape(9, -1)
 
     mod_grads = jnp.concatenate([mod_early, mod_late], 2)
     mod_grads = jnp.where(active[:, None, None, None], mod_grads, 0.0).astype(bf16).reshape(rows_here, 6 * D)
     tap_rows = jnp.pad(conv_one_grad.astype(bf16).reshape(-1), (0, 3 * D)).reshape(2, 6 * D)
-    gathered = gathered_everywhere(jnp.concatenate([mod_grads, tap_rows], 0), attn_sums)
+    gathered, attn_sums, dx_far = gathered_everywhere(jnp.concatenate([mod_grads, tap_rows], 0), attn_sums, dx_far)
+    if balanced:
+        work_x = finished([(dx_own, dx_far), (x_last, x_last_far)])
     conv_one_sum = gathered[:, :, rows_here:].astype(f32).sum((0, 1)).reshape(-1)[: 9 * D].reshape(9, D)
     conv_one_sum = lax.dynamic_slice_in_dim(conv_one_sum, owner * shard, shard, axis=1)
     mod_all = gathered.reshape(-1, 6 * D)
     grad_ada = dot_tn(act_low, mod_all)
     grad_embed = jnp.where(real_row, silu_back(dot_nt(mod_all, ada_weight))[0], 0.0)
     grad_table = dot_tn(label_hot, grad_embed.astype(bf16))
+
+    attn_final = narrow_sum(attn_sums, narrow_other(attn_sums) if balanced else None)
+    final_qkv, final_out = attn_final[:, : 3 * D], attn_final[:, 3 * D :]
+    second = narrow_sum(sums_1, other_1)
+    ffn_final = jnp.stack([narrow_sum(sums_0, other_0), second[:, : 2 * columns]])
+    final_up = ffn_final[:, :, :columns].reshape(PARTS, shard, per_part, owners, shard)
+    final_up = final_up.transpose(1, 3, 0, 2, 4).reshape(shard, hidden_width)
+    final_down = ffn_final[:, :, columns:].reshape(PARTS, shard, per_part, D).swapaxes(1, 2).reshape(-1, D)
+    final_taps = second[:, 2 * columns : 2 * columns + 9 * PARTS * per_part].reshape(shard, PARTS, per_part, 9)
+    final_taps = final_taps.transpose(3, 1, 2, 0).reshape(9, -1)
     return (
         work_y, work_x, conv_one_sum, final_qkv, final_out, final_up,
         final_taps, final_down, grad_ada, grad_table,

time: 546 us -> 542 us (level)
  waiting for transfers between devices: 82.4 us -> 66.7 us
  starting transfers between devices: 36.3 us -> 45.7 us
  other arithmetic: 47.6 us -> 54.1 us
    reduce_scatter x3 -> x2, waiting for transfers between devices: 26.4 us -> 5.31 us  [owner_sum(): return lax.psum_scatter(values, 'wide', scatter_dimension=0, tiled=True)]
    ppermute x2, waiting for transfers between devices: 0.01 us -> 9.89 us  [body(): lax.ppermute(v, 'narrow', swap)]
    ppermute x9 -> x14, starting transfers between devices: 7.03 us -> 16.6 us  [swapped(): return lax.ppermute(values, 'wide', [(i, i ^ bit) for i in range(count)])]
    convert_element_type x0 -> x3, other arithmetic: none -> 7.26 us  [the longest x2 5.88 us: summed(): return (keep.astype(f32) + other.astype(f32)).astype(keep.dtype)]
    ppermute x9 -> x14, waiting for transfers between devices: 24.6 us -> 20.3 us  [swapped(): return lax.ppermute(values, 'wide', [(i, i ^ bit) for i in range(count)])]
  transfers between devices with their start and end apart: 31 -> 35, of which waited for: 10 -> 8; matrix products, arithmetic and copies ran while one was open for 15% -> 15% of each run, Pallas kernels for 57% -> 58%
where the time goes in v3:
time: 542 us; the launch traced here: 533 us
  Pallas kernels  307 us (57%)
  waiting for transfers between devices  66.7 us (12%)
  other arithmetic  54.1 us (10%)
  starting transfers between devices  45.7 us (8%)
  local copies, waits for them, and re-layouts  38.7 us (7%)
  between operations  15.4 us (3%)
    pallas_call x16, Pallas kernels, call(): pl.pallas_call(run, grid_spec=pltpu.PrefetchScalarGridSpec(num_scalar_pre...  307 us
    ppermute x14, waiting for transfers between devices, swapped(): return lax.ppermute(values, 'wide', [(i, i ^ bit) for i in range(count)])  20.3 us
    ppermute x14, starting transfers between devices, swapped(): return lax.ppermute(values, 'wide', [(i, i ^ bit) for i in range(count)])  16.6 us
  transfers between devices with their start and end apart: 35, of which 8 were waited for; matrix products, arithmetic and copies ran while one was open for 15% of the time, Pallas kernels for 58%

profile of v3, /device:TPU:0, one launch (start us, length us, event | category | flops | bytes accessed | tf_op | source)
XLA Modules:
  0.0 532.7 jit_solution(14270245281077474790)
XLA Ops:
  7.2 1.8 constant_dynamic-update-slice_fusion.1
  10.5 4.0 collective-permute-start.2
  25.2 5.3 all-to-all-start
  35.6 1.7 reshape.741
  38.7 2.1 reshape.742
  51.0 4.3 arrange.5
  55.7 8.3 %collective-permute-start.6 = (bf16[1,512,768]{2,1,0:T(8,128)(2,1)}, bf16[1,512,768]{2,1,0:T(8,128)(2,1)}, u32[]{:S(2)}, u32[]{:S(2)}) collective-permute-start(bf16[1,512,768]{2,1,0:T(8,128)(2,1)} %arrange.5), channel_id=1, source_target_pairs={{0,16},{2,18},{4,20},{6,22},{8,24},{10,26},{12,28},{14,30},{16,0},... | collective-permute-start | bytes 2359304 | tf_op jit(solution)/shard_map/ppermute | solution.py:833
  66.6 8.5 %collective-permute-done.refs_1_ = bf16[3,256,768]{2,1,0:T(8,128)(2,1)} collective-permute-done((bf16[3,256,768]{2,1,0:T(8,128)(2,1)}, bf16[3,256,768]{2,1,0:T(8,128)(2,1)}, u32[]{:S(2)}, u32[]{:S(2)}) %collective-permute-start) | collective-permute-done | bytes 1179680 | tf_op jit(solution)/shard_map/ppermute | solution.py:828
  75.1 7.4 %arrange.4.refs_0_ = bf16[3,512,768]{2,1,0:T(8,128)(2,1)} custom-call(s32[8]{0:T(128)} %pad_add_fusion.3.meta, bf16[4,512,768]{2,1,0:T(8,128)(2,1)} %refs_0_.5, bf16[3,256,768]{2,1,0:T(8,128)(2,1)} %collective-permute-done.refs_1_, s32[4,512,1]{2,1,0:T(8,128)} %select_select_fusion.refs_2_), custom_call_target="tpu_custom_call" | custom-call | flops 1500000000 | bytes 3000000 | tf_op jit(solution)/shard_map/arrange/pallas_call | solution.py:795
  87.8 7.5 %mix_tokens.2 = (bf16[3,512,768]{2,1,0:T(8,128)(2,1)}, bf16[3,512,768]{2,1,0:T(8,128)(2,1)}) custom-call(s32[6]{0:T(128)} %pad_add_fusion.2.meta, bf16[3,512,768]{2,1,0:T(8,128)(2,1)} %arrange.4.refs_0_, f32[3,2,7,768]{3,2,1,0:T(8,128)} %pad_maximum_fusion.10.refs_1_.refs_2_.refs_7_.refs_3_, f32[3,9,768]{2,1,0:T(8,128)} %broadcast_select_fusion.4.refs_2_.refs_3_.refs_4_), custom_call_target="tpu_custom_call" | custom-call | flops 1500000000 | bytes 2000000 | tf_op jit(solution)/shard_map/mix_tokens/pallas_call | solution.py:795
  95.3 6.6 %collective-permute-done.6.refs_1_ = bf16[1,512,768]{2,1,0:T(8,128)(2,1)} collective-permute-done((bf16[1,512,768]{2,1,0:T(8,128)(2,1)}, bf16[1,512,768]{2,1,0:T(8,128)(2,1)}, u32[]{:S(2)}, u32[]{:S(2)}) %collective-permute-start.6) | collective-permute-done | bytes 786464 | tf_op jit(solution)/shard_map/ppermute | solution.py:833
  101.9 1.8 select_bitcast_fusion.5
  103.7 1.6 pad_maximum_fusion.1
  105.5 7.5 %arrange.6.refs_0_ = bf16[3,512,768]{2,1,0:T(8,128)(2,1)} custom-call(s32[8]{0:T(128)} %pad_add_fusion.3.meta, bf16[4,512,768]{2,1,0:T(8,128)(2,1)} %refs_0_.7, bf16[3,256,768]{2,1,0:T(8,128)(2,1)} %collective-permute-done.7.refs_1_, s32[4,512,1]{2,1,0:T(8,128)} %select_select_fusion.refs_2_), custom_call_target="tpu_custom_call" | custom-call | flops 1500000000 | bytes 3000000 | tf_op jit(solution)/shard_map/arrange/pallas_call | solution.py:795
  113.0 2.9 select_bitcast_fusion.1
  115.9 2.6 pad_maximum_fusion
  122.8 4.3 arrange.7
  127.1 2.0 broadcast_select_fusion.2
  129.1 24.3 %attend.2 = (bf16[3,512,2304]{2,1,0:T(8,128)(2,1)}, bf16[3,512,768]{2,1,0:T(8,128)(2,1)}, bf16[3,512,768]{2,1,0:T(8,128)(2,1)}, bf16[3,512,768]{2,1,0:T(8,128)(2...) custom-call(s32[6]{0:T(128)} %pad_add_fusion.2.meta, bf16[3,512,768]{2,1,0:T(8,128)(2,1)} %get-tuple-element.94.refs_4_.refs_0_, ...), custom_call_target="tpu_custom_call" | custom-call | flops 4000000000 | bytes 2000000 | tf_op jit(solution)/shard_map/attend/pallas_call | solution.py:795
  153.4 5.4 %mix_tokens.3 = (bf16[3,512,768]{2,1,0:T(8,128)(2,1)}, bf16[3,512,768]{2,1,0:T(8,128)(2,1)}) custom-call(s32[6]{0:T(128)} %pad_add_fusion.2.meta, bf16[3,512,768]{2,1,0:T(8,128)(2,1)} %arrange.4.refs_0_, bf16[1,512,768]{2,1,0:T(8,128)(2,1)} %collective-permute-done.6.refs_1_, ...), custom_call_target="tpu_custom_call", output_to_operand_aliasing={{0}: (5, {}), {1}: (6, {})} | custom-call | flops 750000000 | bytes 1000000 | tf_op jit(solution)/shard_map/mix_tokens/pallas_call | solution.py:795
  158.8 15.2 %attend.3 = (bf16[3,512,2304]{2,1,0:T(8,128)(2,1)}, bf16[3,512,768]{2,1,0:T(8,128)(2,1)}, bf16[3,512,768]{2,1,0:T(8,128)(2,1)}, bf16[3,512,768]{2,1,0:T(8,128)(2...) custom-call(s32[6]{0:T(128)} %pad_add_fusion.2.meta, ...), custom_call_target="tpu_custom_call", output_to_operand_aliasing={{0}: (5, {}), {1}: (6, {}), {2}: (7, {}), {3}: (8, {}), {4}... | custom-call | flops 2000000000 | bytes 1000000 | tf_op jit(solution)/shard_map/attend/pallas_call | solution.py:795
  174.0 10.1 %collective-permute-done.10.refs_1_ = bf16[1,512,768]{2,1,0:T(8,128)(2,1)} collective-permute-done((bf16[1,512,768]{2,1,0:T(8,128)(2,1)}, bf16[1,512,768]{2,1,0:T(8,128)(2,1)}, u32[]{:S(2)}, u32[]{:S(2)}) %collective-permute-start.10) | collective-permute-done | bytes 786464 | tf_op jit(solution)/shard_map/ppermute | solution.py:881
  184.0 61.6 %feed_forward.2 = (bf16[3,512,768]{2,1,0:T(8,128)(2,1)}, f32[3,512,768]{2,1,0:T(8,128)}, f32[3,512,768]{2,1,0:T(8,128)}, bf16[768,3072]{1,0:T(8,128)(2,1)}, f32[9,1536]{1,0:T(8,128)}) custom-call(s32[6]{0:T(128)} %pad_add_fusion.2.meta, bf16[3,512,768]{2,1,0:T(8,128)(2,1)} %arrange.6.refs_0_, bf16[1,512,768]{2,1,0:T(8,128)(2,1)} %collective-permute-done.10.refs_1_, ...), custom_call_target="tpu_custom_call" | custom-call | flops 12000000000 | bytes 3000000 | tf_op jit(solution)/shard_map/feed_forward/pallas_call | solution.py:795
  246.6 67.3 %feed_forward.3 = (f32[3,512,768]{2,1,0:T(8,128)}, bf16[1,512,768]{2,1,0:T(8,128)(2,1)}, bf16[3,512,768]{2,1,0:T(8,128)(2,1)}, bf16[3,256,768]{2,1,0:T(8,128)(2,...) custom-call(s32[6]{0:T(128)} %pad_add_fusion.2.meta, ...), custom_call_target="tpu_custom_call" | custom-call | flops 12750000128 | bytes 3000000 | tf_op jit(solution)/shard_map/feed_forward/pallas_call | solution.py:795
  313.9 5.3 reduce-scatter.3.cloned.1.call-done
  322.1 21.2 %backward_middle.1 = (f32[3,512,768]{2,1,0:T(8,128)}, bf16[3,512,768]{2,1,0:T(8,128)(2,1)}, f32[3,2,4,768]{3,2,1,0:T(4,128)}, bf16[768,768]{1,0:T(8,128)(2,1)}) custom-call(s32[6]{0:T(128)} %pad_add_fusion.2.meta, bf16[3,512,768]{2,1,0:T(8,128)(2,1)} %arrange.6.refs_0_, bf16[1,512,768]{2,1,0:T(8,128)(2,1)} %collective-permute-done.10.refs_1_, ...), custom_call_target="tpu_custom_call" | custom-call | flops 3000000000 | bytes 3000000 | tf_op jit(solution)/shard_map/backward_middle/pallas_call | solution.py:795
  343.3 32.3 %backward_heads.1 = (bf16[3,512,2304]{2,1,0:T(8,128)(2,1)}, bf16[384,3072]{1,0:T(8,128)(2,1)}, bf16[384,3072]{1,0:T(8,128)(2,1)}) custom-call(s32[6]{0:T(128)} %pad_add_fusion.2.meta, s32[1]{0:T(128)} %bitcast.1.refs_0_, bf16[3,512,2304]{2,1,0:T(8,128)(2,1)} %get-tuple-element.107.refs_1_, bf16[3,512,768]{2,1,0:T(8,128)(2,1)} %get-tuple-element.125.refs_2_, ...), custom_call_target="tpu_custom_call" | custom-call | flops 8999999488 | bytes 3000000 | tf_op jit(solution)/shard_map/backward_heads/pallas_call | solution.py:795
  377.6 1.9 fusion.44.refs_1_
  379.5 5.9 %collective-permute-done.13 = bf16[48,3072]{1,0:T(8,128)(2,1)} collective-permute-done((bf16[48,3072]{1,0:T(8,128)(2,1)}, bf16[48,3072]{1,0:T(8,128)(2,1)}, u32[]{:S(2)}, u32[]{:S(2)}) %collective-permute-start.13) | collective-permute-done | bytes 294944 | tf_op jit(solution)/shard_map/ppermute | solution.py:674
  385.4 3.6 place_back.2
  389.5 15.7 %backward_tokens.2 = (bf16[3,512,768]{2,1,0:T(8,128)(2,1)}, bf16[3,256,768]{2,1,0:T(8,128)(2,1)}, f32[3,2,2,768]{3,2,1,0:T(2,128)}, bf16[1,512,768]{2,1,0:T(8,128)(2,1)}, f32[9,768]{1,0:T(8,128)}) custom-call(s32[6]{0:T(128)} %pad_add_fusion.2.meta, bf16[3,512,2304]{2,1,0:T(8,128)(2,1)} %get-tuple-element.136.refs_0_, ...), custom_call_target="tpu_custom_call" | custom-call | flops 15000000512 | bytes 1000000 | tf_op jit(solution)/shard_map/backward_tokens/pallas_call | solution.py:795
  405.3 2.6 select_add_fusion.3
  407.8 3.3 add_convert_fusion
  411.1 1.5 collective-permute-start.17
  414.6 25.8 %backward_tokens.3 = (bf16[3,512,768]{2,1,0:T(8,128)(2,1)}, bf16[3,256,768]{2,1,0:T(8,128)(2,1)}, f32[3,2,2,768]{3,2,1,0:T(2,128)}, bf16[1,512,768]{2,1,0:T(8,128)(2,1)}, f32[9,768]{1,0:T(8,128)}) custom-call(s32[6]{0:T(128)} %pad_add_fusion.2.meta, ...), custom_call_target="tpu_custom_call", output_to_operand_aliasing={{0}: (8, {}), {1}: (9, {}), {2}: (10, {})} | custom-call | flops 30000001024 | bytes 2000000 | tf_op jit(solution)/shard_map/backward_tokens/pallas_call | solution.py:795
  441.4 2.6 fusion
  449.1 4.0 select_add_fusion.1
  453.8 2.6 collective-permute-start.20
  462.8 3.9 place_back.3
  467.3 1.7 reshape.764
  469.9 3.2 reshape.765
  475.5 1.5 collective-permute-start.21
  477.0 11.8 %collective-permute-done.23 = bf16[48,3072]{1,0:T(8,128)(2,1)} collective-permute-done((bf16[48,3072]{1,0:T(8,128)(2,1)}, bf16[48,3072]{1,0:T(8,128)(2,1)}, u32[]{:S(2)}, u32[]{:S(2)}) %collective-permute-start.23) | collective-permute-done | bytes 294944 | tf_op jit(solution)/shard_map/ppermute | solution.py:600
  490.4 9.9 %collective-permute-done.25 = bf16[3,256,768]{2,1,0:T(8,128)(2,1)S(1)} collective-permute-done((bf16[3,256,768]{2,1,0:T(8,128)(2,1)}, bf16[3,256,768]{2,1,0:T(8,128)(2,1)S(1)}, u32[]{:S(2)}, u32[]{:S(2)}) %collective-permute-start.25) | collective-permute-done | bytes 1179680 | tf_op jit(solution)/shard_map/ppermute | solution.py:1007
  500.3 2.1 collective-permute-start.27
  505.2 8.5 %collective-permute-done.27 = bf16[4,2,8,4608]{3,2,1,0:T(8,128)(2,1)S(1)} collective-permute-done((bf16[4,2,8,4608]{3,2,1,0:T(8,128)(2,1)S(1)}, bf16[4,2,8,4608]{3,2,1,0:T(8,128)(2,1)S(1)}, u32[]{:S(2)}, u32[]{:S(2)}) %collective-permute-start.27) | collective-permute-done | bytes 589856 | tf_op jit(solution)/shard_map/ppermute | solution.py:600
  515.6 3.1 maximum_select_fusion.1
  523.2 1.8 fusion.3
  (307 shorter events, 77.4 us)
Async XLA Ops:
  7.2 9.0 %slice-start = ((bf16[4,512,768]{2,1,0:T(8,128)(2,1)}), bf16[1,512,768]{2,1,0:T(8,128)(2,1)S(1)}, s32[]{:S(2)}) async-start(bf16[4,512,768]{2,1,0:T(8,128)(2,1)} %refs_0_.5), calls=%async_computation.7 | async-start | bytes 1572864 | tf_op jit(solution)/shard_map/slice | solution.py:826
  7.2 11.2 %slice-start.2 = ((bf16[4,512,768]{2,1,0:T(8,128)(2,1)}), bf16[1,512,768]{2,1,0:T(8,128)(2,1)S(1)}, s32[]{:S(2)}) async-start(bf16[4,512,768]{2,1,0:T(8,128)(2,1)} %refs_0_.7), calls=%async_computation.9 | async-start | bytes 1572864 | tf_op jit(solution)/shard_map/slice | solution.py:826
  10.5 38.1 %collective-permute-start.2 = (bf16[48,3072]{1,0:T(8,128)(2,1)}, bf16[48,3072]{1,0:T(8,128)(2,1)}, u32[]{:S(2)}, u32[]{:S(2)}) collective-permute-start(bf16[48,3072]{1,0:T(8,128)(2,1)} %constant_dynamic-update-slice_fusion), channel_id=1, source_target_pairs={{0,16},{2,18},{4,20},{6,22},{8,24},{10,26},{12,28},{14,30},{16,0},... | collective-permute-start | bytes 884744 | tf_op jit(solution)/shard_map/ppermute | solution.py:600
  14.5 34.1 %collective-permute-start.3 = (bf16[48,3072]{1,0:T(8,128)(2,1)}, bf16[48,3072]{1,0:T(8,128)(2,1)}, u32[]{:S(2)}, u32[]{:S(2)}) collective-permute-start(bf16[48,3072]{1,0:T(8,128)(2,1)} %constant_dynamic-update-slice_fusion), channel_id=1, source_target_pairs={{0,24},{2,26},{4,28},{6,30},{8,16},{10,18},{12,20},{14,22},{16,8},... | collective-permute-start | bytes 884744 | tf_op jit(solution)/shard_map/ppermute | solution.py:600
  15.9 30.1 %collective-permute-start.1 = (bf16[48,3072]{1,0:T(8,128)(2,1)}, bf16[48,3072]{1,0:T(8,128)(2,1)}, u32[]{:S(2)}, u32[]{:S(2)}) collective-permute-start(bf16[48,3072]{1,0:T(8,128)(2,1)} %constant_dynamic-update-slice_fusion), channel_id=1, source_target_pairs={{0,8},{2,10},{4,12},{6,14},{8,0},{10,2},{12,4},{14,6},{16,24},{18,... | collective-permute-start | bytes 884744 | tf_op jit(solution)/shard_map/ppermute | solution.py:600
  16.1 5.4 %copy-start.35 = (bf16[1000,48]{0,1:T(8,128)(2,1)S(1)}, bf16[1000,48]{0,1:T(8,128)(2,1)}, u32[]{:S(2)}) copy-start(bf16[1000,48]{0,1:T(8,128)(2,1)} %param.23) | copy-start | bytes 288004
  16.1 7.1 %copy-start.6 = (bf16[48,4608]{1,0:T(8,128)(2,1)S(1)}, bf16[48,4608]{1,0:T(8,128)(2,1)}, u32[]{:S(2)}) copy-start(bf16[48,4608]{1,0:T(8,128)(2,1)} %param.22) | copy-start | bytes 1327108
  16.9 34.0 %collective-permute-start.4 = (bf16[1,256,768]{2,1,0:T(8,128)(2,1)}, bf16[1,256,768]{2,1,0:T(8,128)(2,1)}, u32[]{:S(2)}, u32[]{:S(2)}) collective-permute-start(bf16[1,256,768]{2,1,0:T(8,128)(2,1)} %bitcast.10), channel_id=1, source_target_pairs={{0,1},{1,0},{2,3},{3,2},{4,5},{5,4},{6,7},{7,6},{8,9},{9,8},{10,11... | collective-permute-start | bytes 1179656 | tf_op jit(solution)/shard_map/ppermute | solution.py:828
  19.2 36.1 %collective-permute-start.5 = (bf16[1,256,768]{2,1,0:T(8,128)(2,1)}, bf16[1,256,768]{2,1,0:T(8,128)(2,1)}, u32[]{:S(2)}, u32[]{:S(2)}) collective-permute-start(bf16[1,256,768]{2,1,0:T(8,128)(2,1)} %bitcast.12), channel_id=1, source_target_pairs={{0,1},{1,0},{2,3},{3,2},{4,5},{5,4},{6,7},{7,6},{8,9},{9,8},{10,11... | collective-permute-start | bytes 1179656 | tf_op jit(solution)/shard_map/ppermute | solution.py:828
  23.9 7.3 %copy-start.31 = (s32[64]{0:T(128)S(1)}, s32[64]{0:T(128)}, u32[]{:S(2)}) copy-start(s32[64]{0:T(128)} %param.26) | copy-start | bytes 772
  25.2 57.3 %all-to-all-start = ((bf16[16,6,4992]{2,1,0:T(8,128)(2,1)}), bf16[16,6,4992]{2,1,0:T(8,128)(2,1)}, u32[]{:S(2)}, u32[]{:S(2)}) async-start(bf16[16,6,4992]{2,1,0:T(8,128)(2,1)} %pad_maximum_fusion.3), calls=%async_computation | async-start | bytes 2555904 | tf_op jit(solution)/shard_map/all_to_all | solution.py:751
  30.5 153.6 %all-gather.3.cloned.1.call-start = ((), (), s32[]{:S(2)}) async-start(), calls=%async_computation.3 | async-start | bytes 5013504 | tf_op jit(solution)/shard_map/all_gather | solution.py:767
  37.3 5.4 %slice-start.1 = ((bf16[4,512,768]{2,1,0:T(8,128)(2,1)}), bf16[3,512,768]{2,1,0:T(8,128)(2,1)S(1)}, s32[]{:S(2)}) async-start(bf16[4,512,768]{2,1,0:T(8,128)(2,1)} %refs_0_.5), calls=%async_computation.8 | async-start | bytes 4718592 | tf_op jit(solution)/shard_map/slice | solution.py:826
  46.0 29.1 %collective-permute-start = (bf16[3,256,768]{2,1,0:T(8,128)(2,1)}, bf16[3,256,768]{2,1,0:T(8,128)(2,1)}, u32[]{:S(2)}, u32[]{:S(2)}) collective-permute-start(bf16[3,256,768]{2,1,0:T(8,128)(2,1)} %bitcast.3), channel_id=1, source_target_pairs={{0,1},{1,0},{2,3},{3,2},{4,5},{5,4},{6,7},{7,6},{8,9},{9,8},{10,11... | collective-permute-start | bytes 3538952 | tf_op jit(solution)/shard_map/ppermute | solution.py:828
  55.3 8.7 %slice-start.3 = ((bf16[4,512,768]{2,1,0:T(8,128)(2,1)}), bf16[3,512,768]{2,1,0:T(8,128)(2,1)S(1)}, s32[]{:S(2)}) async-start(bf16[4,512,768]{2,1,0:T(8,128)(2,1)} %refs_0_.7), calls=%async_computation.10 | async-start | bytes 4718592 | tf_op jit(solution)/shard_map/slice | solution.py:826
  55.3 46.7 %collective-permute-start.8 = (bf16[4,48,3072]{2,1,0:T(8,128)(2,1)}, bf16[4,48,3072]{2,1,0:T(8,128)(2,1)}, u32[]{:S(2)}, u32[]{:S(2)}) collective-permute-start(bf16[4,48,3072]{2,1,0:T(8,128)(2,1)} %bitcast.202), channel_id=1, source_target_pairs={{0,4},{2,6},{4,0},{6,2},{8,12},{10,14},{12,8},{14,10},{16,20},{18,... | collective-permute-start | bytes 3538952 | tf_op jit(solution)/shard_map/ppermute | solution.py:600
  55.7 46.3 %collective-permute-start.6 = (bf16[1,512,768]{2,1,0:T(8,128)(2,1)}, bf16[1,512,768]{2,1,0:T(8,128)(2,1)}, u32[]{:S(2)}, u32[]{:S(2)}) collective-permute-start(bf16[1,512,768]{2,1,0:T(8,128)(2,1)} %arrange.5), channel_id=1, source_target_pairs={{0,16},{2,18},{4,20},{6,22},{8,24},{10,26},{12,28},{14,30},{16,0},... | collective-permute-start | bytes 2359304 | tf_op jit(solution)/shard_map/ppermute | solution.py:833
  65.1 36.8 %collective-permute-start.7 = (bf16[3,256,768]{2,1,0:T(8,128)(2,1)}, bf16[3,256,768]{2,1,0:T(8,128)(2,1)}, u32[]{:S(2)}, u32[]{:S(2)}) collective-permute-start(bf16[3,256,768]{2,1,0:T(8,128)(2,1)} %bitcast.23), channel_id=1, source_target_pairs={{0,1},{1,0},{2,3},{3,2},{4,5},{5,4},{6,7},{7,6},{8,9},{9,8},{10,11... | collective-permute-start | bytes 3538952 | tf_op jit(solution)/shard_map/ppermute | solution.py:828
  105.4 141.2 %all-gather.5.cloned.1.call-start = ((), (), s32[]{:S(2)}) async-start(), calls=%async_computation.4 | async-start | bytes 5013504 | tf_op jit(solution)/shard_map/all_gather | solution.py:767
  105.4 7.6 %collective-permute-start.9 = (bf16[4,2,48,3072]{3,2,1,0:T(8,128)(2,1)}, bf16[4,2,48,3072]{3,2,1,0:T(8,128)(2,1)}, u32[]{:S(2)}, u32[]{:S(2)}) collective-permute-start(bf16[4,2,48,3072]{3,2,1,0:T(8,128)(2,1)} %pad_maximum_fusion.1), channel_id=1, source_target_pairs={{0,2},{2,0},{4,6},{6,4},{8,10},{10,8},{12,14},{14,12},{16,18},{18,... | collective-permute-start | bytes 7077896 | tf_op jit(solution)/shard_map/ppermute | solution.py:600
  118.5 200.7 %reduce-scatter.3.cloned.1.call-start = ((), (), s32[]{:S(2)}) async-start(), calls=%async_computation.5 | async-start | bytes 5013504 | tf_op jit(solution)/shard_map/reduce_scatter | solution.py:914
  127.1 57.0 %collective-permute-start.10 = (bf16[1,512,768]{2,1,0:T(8,128)(2,1)}, bf16[1,512,768]{2,1,0:T(8,128)(2,1)}, u32[]{:S(2)}, u32[]{:S(2)}) collective-permute-start(bf16[1,512,768]{2,1,0:T(8,128)(2,1)} %arrange.7), channel_id=1, source_target_pairs={{0,16},{2,18},{4,20},{6,22},{8,24},{10,26},{12,28},{14,30},{16,0},... | collective-permute-start | bytes 2359304 | tf_op jit(solution)/shard_map/ppermute | solution.py:881
  245.7 165.4 %reduce-scatter.5.cloned.1.call-start = ((), (), s32[]{:S(2)}) async-start(), calls=%async_computation.6 | async-start | bytes 5222400 | tf_op jit(solution)/shard_map/reduce_scatter | solution.py:914
  319.2 60.3 %collective-permute-start.11 = (bf16[1,512,768]{2,1,0:T(8,128)(2,1)}, bf16[1,512,768]{2,1,0:T(8,128)(2,1)}, u32[]{:S(2)}, u32[]{:S(2)}) collective-permute-start(bf16[1,512,768]{2,1,0:T(8,128)(2,1)} %get-tuple-element.129), channel_id=1, source_target_pairs={{0,16},{2,18},{4,20},{6,22},{8,24},{10,26},{12,28},{14,30},{16,0},... | collective-permute-start | bytes 2359304 | tf_op jit(solution)/shard_map/ppermute | solution.py:991
  320.7 58.8 %collective-permute-start.12 = (bf16[3,256,768]{2,1,0:T(8,128)(2,1)}, bf16[3,256,768]{2,1,0:T(8,128)(2,1)}, u32[]{:S(2)}, u32[]{:S(2)}) collective-permute-start(bf16[3,256,768]{2,1,0:T(8,128)(2,1)} %get-tuple-element.130), channel_id=1, source_target_pairs={{0,1},{1,0},{2,3},{3,2},{4,5},{5,4},{6,7},{7,6},{8,9},{9,8},{10,11... | collective-permute-start | bytes 3538952 | tf_op jit(solution)/shard_map/ppermute | solution.py:992
  375.6 32.2 %collective-permute-start.14 = (bf16[384,3072]{1,0:T(8,128)(2,1)}, bf16[384,3072]{1,0:T(8,128)(2,1)}, u32[]{:S(2)}, u32[]{:S(2)}) collective-permute-start(bf16[384,3072]{1,0:T(8,128)(2,1)} %get-tuple-element.135), channel_id=1, source_target_pairs={{0,2},{2,0},{4,6},{6,4},{8,10},{10,8},{12,14},{14,12},{16,18},{18,... | collective-permute-start | bytes 7077896 | tf_op jit(solution)/shard_map/ppermute | solution.py:600
  375.7 9.7 %collective-permute-start.13 = (bf16[48,3072]{1,0:T(8,128)(2,1)}, bf16[48,3072]{1,0:T(8,128)(2,1)}, u32[]{:S(2)}, u32[]{:S(2)}) collective-permute-start(bf16[48,3072]{1,0:T(8,128)(2,1)} %reduce-scatter.3.cloned.1.call-done), channel_id=1, source_target_pairs={{0,1},{1,0},{2,3},{3,2},{4,5},{5,4},{6,7},{7,6},{8,9},{9,8},{10,11... | collective-permute-start | bytes 884744 | tf_op jit(solution)/shard_map/ppermute | solution.py:674
  389.0 16.3 %collective-permute-start.18 = (bf16[1,256,768]{2,1,0:T(8,128)(2,1)}, bf16[1,256,768]{2,1,0:T(8,128)(2,1)}, u32[]{:S(2)}, u32[]{:S(2)}) collective-permute-start(bf16[1,256,768]{2,1,0:T(8,128)(2,1)} %get-tuple-element.151), channel_id=1, source_target_pairs={{0,1},{1,0},{2,3},{3,2},{4,5},{5,4},{6,7},{7,6},{8,9},{9,8},{10,11... | collective-permute-start | bytes 1179656 | tf_op jit(solution)/shard_map/ppermute | solution.py:997
  405.3 38.8 %collective-permute-start.15 = (bf16[1,512,768]{2,1,0:T(8,128)(2,1)}, bf16[1,512,768]{2,1,0:T(8,128)(2,1)}, u32[]{:S(2)}, u32[]{:S(2)}) collective-permute-start(bf16[1,512,768]{2,1,0:T(8,128)(2,1)} %get-tuple-element.142), channel_id=1, source_target_pairs={{0,16},{2,18},{4,20},{6,22},{8,24},{10,26},{12,28},{14,30},{16,0},... | collective-permute-start | bytes 2359304 | tf_op jit(solution)/shard_map/ppermute | solution.py:996
  411.1 33.0 %collective-permute-start.17 = (bf16[48,3200]{1,0:T(8,128)(2,1)}, bf16[48,3200]{1,0:T(8,128)(2,1)}, u32[]{:S(2)}, u32[]{:S(2)}) collective-permute-start(bf16[48,3200]{1,0:T(8,128)(2,1)} %reduce-scatter.5.cloned.1.call-done), channel_id=1, source_target_pairs={{0,1},{1,0},{2,3},{3,2},{4,5},{5,4},{6,7},{7,6},{8,9},{9,8},{10,11... | collective-permute-start | bytes 921608 | tf_op jit(solution)/shard_map/ppermute | solution.py:674
  413.8 27.6 %collective-permute-start.16 = (bf16[4,48,3072]{2,1,0:T(8,128)(2,1)}, bf16[4,48,3072]{2,1,0:T(8,128)(2,1)}, u32[]{:S(2)}, u32[]{:S(2)}) collective-permute-start(bf16[4,48,3072]{2,1,0:T(8,128)(2,1)} %fusion.1), channel_id=1, source_target_pairs={{0,4},{2,6},{4,0},{6,2},{8,12},{10,14},{12,8},{14,10},{16,20},{18,... | collective-permute-start | bytes 3538952 | tf_op jit(solution)/shard_map/ppermute | solution.py:600
  444.1 5.0 copy-start.2
  444.3 8.8 %copy-start.11 = (bf16[1,1,8,4608]{3,2,1,0:T(8,128)(2,1)}, bf16[1,1,8,4608]{3,2,1,0:T(8,128)(2,1)S(1)}, u32[]{:S(2)}) copy-start(bf16[1,1,8,4608]{3,2,1,0:T(8,128)(2,1)S(1)} %fusion.80) | copy-start | bytes 221188
  444.4 8.7 %collective-permute-start.19 = (bf16[8,4608]{1,0:T(8,128)(2,1)S(1)}, bf16[8,4608]{1,0:T(8,128)(2,1)S(1)}, u32[]{:S(2)}, u32[]{:S(2)}) collective-permute-start(bf16[8,4608]{1,0:T(8,128)(2,1)S(1)} %pad_maximum_fusion.12), channel_id=1, source_target_pairs={{0,1},{1,0},{2,3},{3,2},{4,5},{5,4},{6,7},{7,6},{8,9},{9,8},{10,11... | collective-permute-start | bytes 221192 | tf_op jit(solution)/shard_map/ppermute | solution.py:652
  453.8 19.2 %collective-permute-start.20 = (bf16[1,2,8,4608]{3,2,1,0:T(8,128)(2,1)}, bf16[1,2,8,4608]{3,2,1,0:T(8,128)(2,1)}, u32[]{:S(2)}, u32[]{:S(2)}) collective-permute-start(bf16[1,2,8,4608]{3,2,1,0:T(8,128)(2,1)} %maximum_select_fusion.2), channel_id=1, source_target_pairs={{0,16},{2,18},{4,20},{6,22},{8,24},{10,26},{12,28},{14,30},{16,0},... | collective-permute-start | bytes 442376 | tf_op jit(solution)/shard_map/ppermute | solution.py:600
  459.3 16.2 %collective-permute-start.22 = (bf16[48,3072]{1,0:T(8,128)(2,1)}, bf16[48,3072]{1,0:T(8,128)(2,1)}, u32[]{:S(2)}, u32[]{:S(2)}) collective-permute-start(bf16[48,3072]{1,0:T(8,128)(2,1)} %get-tuple-element.184), channel_id=1, source_target_pairs={{0,8},{2,10},{4,12},{6,14},{8,0},{10,2},{12,4},{14,6},{16,24},{18,... | collective-permute-start | bytes 884744 | tf_op jit(solution)/shard_map/ppermute | solution.py:600
  460.7 16.3 %collective-permute-start.24 = (bf16[48,3072]{1,0:T(8,128)(2,1)}, bf16[48,3072]{1,0:T(8,128)(2,1)}, u32[]{:S(2)}, u32[]{:S(2)}) collective-permute-start(bf16[48,3072]{1,0:T(8,128)(2,1)} %get-tuple-element.185), channel_id=1, source_target_pairs={{0,24},{2,26},{4,28},{6,30},{8,16},{10,18},{12,20},{14,22},{16,8},... | collective-permute-start | bytes 884744 | tf_op jit(solution)/shard_map/ppermute | solution.py:600
  461.4 27.5 %collective-permute-start.23 = (bf16[48,3072]{1,0:T(8,128)(2,1)}, bf16[48,3072]{1,0:T(8,128)(2,1)}, u32[]{:S(2)}, u32[]{:S(2)}) collective-permute-start(bf16[48,3072]{1,0:T(8,128)(2,1)} %get-tuple-element.186), channel_id=1, source_target_pairs={{0,16},{2,18},{4,20},{6,22},{8,24},{10,26},{12,28},{14,30},{16,0},... | collective-permute-start | bytes 884744 | tf_op jit(solution)/shard_map/ppermute | solution.py:600
  466.7 35.7 %collective-permute-start.26 = (bf16[1,256,768]{2,1,0:T(8,128)(2,1)}, bf16[1,256,768]{2,1,0:T(8,128)(2,1)}, u32[]{:S(2)}, u32[]{:S(2)}) collective-permute-start(bf16[1,256,768]{2,1,0:T(8,128)(2,1)} %get-tuple-element.162), channel_id=1, source_target_pairs={{0,1},{1,0},{2,3},{3,2},{4,5},{5,4},{6,7},{7,6},{8,9},{9,8},{10,11... | collective-permute-start | bytes 1179656 | tf_op jit(solution)/shard_map/ppermute | solution.py:1007
  469.0 5.5 %copy-start.12 = (bf16[1,1,8,4608]{3,2,1,0:T(8,128)(2,1)S(1)}, bf16[1,1,8,4608]{3,2,1,0:T(8,128)(2,1)}, u32[]{:S(2)}) copy-start(bf16[1,1,8,4608]{3,2,1,0:T(8,128)(2,1)} %copy-done.11) | copy-start | bytes 221188
  469.0 5.5 %copy-start.15 = (bf16[8,4608]{1,0:T(8,128)(2,1)S(1)}, bf16[8,4608]{1,0:T(8,128)(2,1)}, u32[]{:S(2)}) copy-start(bf16[8,4608]{1,0:T(8,128)(2,1)} %copy-done.14) | copy-start | bytes 221188
  473.0 27.3 %collective-permute-start.25 = (bf16[3,256,768]{2,1,0:T(8,128)(2,1)}, bf16[3,256,768]{2,1,0:T(8,128)(2,1)S(1)}, u32[]{:S(2)}, u32[]{:S(2)}) collective-permute-start(bf16[3,256,768]{2,1,0:T(8,128)(2,1)} %get-tuple-element.158), channel_id=1, source_target_pairs={{0,1},{1,0},{2,3},{3,2},{4,5},{5,4},{6,7},{7,6},{8,9},{9,8},{10,11... | collective-permute-start | bytes 3538952 | tf_op jit(solution)/shard_map/ppermute | solution.py:1007
  475.5 26.9 %copy-start.10 = (bf16[1,512,768]{2,1,0:T(8,128)(2,1)S(1)}, bf16[1,512,768]{2,1,0:T(8,128)(2,1)}, u32[]{:S(2)}) copy-start(bf16[1,512,768]{2,1,0:T(8,128)(2,1)} %get-tuple-element.161) | copy-start | bytes 2359300
  475.5 14.7 %collective-permute-start.21 = (bf16[2,2,8,4608]{3,2,1,0:T(8,128)(2,1)S(1)}, bf16[2,2,8,4608]{3,2,1,0:T(8,128)(2,1)S(1)}, u32[]{:S(2)}, u32[]{:S(2)}) collective-permute-start(bf16[2,2,8,4608]{3,2,1,0:T(8,128)(2,1)S(1)} %maximum_bitcast_fusion), channel_id=1, source_target_pairs={{0,8},{2,10},{4,12},{6,14},{8,0},{10,2},{12,4},{14,6},{16,24},{18,... | collective-permute-start | bytes 884744 | tf_op jit(solution)/shard_map/ppermute | solution.py:600
  490.3 14.1 %copy-start.5 = (bf16[3,512,768]{2,1,0:T(8,128)(2,1)S(1)}, bf16[3,512,768]{2,1,0:T(8,128)(2,1)}, u32[]{:S(2)}) copy-start(bf16[3,512,768]{2,1,0:T(8,128)(2,1)} %get-tuple-element.152) | copy-start | bytes 7077892
  500.3 13.3 %collective-permute-start.27 = (bf16[4,2,8,4608]{3,2,1,0:T(8,128)(2,1)S(1)}, bf16[4,2,8,4608]{3,2,1,0:T(8,128)(2,1)S(1)}, u32[]{:S(2)}, u32[]{:S(2)}) collective-permute-start(bf16[4,2,8,4608]{3,2,1,0:T(8,128)(2,1)S(1)} %bitcast.210), channel_id=1, source_target_pairs={{0,4},{2,6},{4,0},{6,2},{8,12},{10,14},{12,8},{14,10},{16,20},{18,... | collective-permute-start | bytes 1769480 | tf_op jit(solution)/shard_map/ppermute | solution.py:600
  503.8 14.9 %collective-permute-start.29 = (bf16[48,3072]{1,0:T(8,128)(2,1)S(1)}, bf16[48,3072]{1,0:T(8,128)(2,1)S(1)}, u32[]{:S(2)}, u32[]{:S(2)}) collective-permute-start(bf16[48,3072]{1,0:T(8,128)(2,1)S(1)} %fusion.7), channel_id=1, source_target_pairs={{0,1},{1,0},{2,3},{3,2},{4,5},{5,4},{6,7},{7,6},{8,9},{9,8},{10,11... | collective-permute-start | bytes 884744 | tf_op jit(solution)/shard_map/ppermute | solution.py:674
  514.0 6.3 %collective-permute-start.28 = (bf16[8,2,8,4608]{3,2,1,0:T(8,128)(2,1)S(1)}, bf16[8,2,8,4608]{3,2,1,0:T(8,128)(2,1)S(1)}, u32[]{:S(2)}, u32[]{:S(2)}) collective-permute-start(bf16[8,2,8,4608]{3,2,1,0:T(8,128)(2,1)S(1)} %bitcast.204), channel_id=1, source_target_pairs={{0,2},{2,0},{4,6},{6,4},{8,10},{10,8},{12,14},{14,12},{16,18},{18,... | collective-permute-start | bytes 3538952 | tf_op jit(solution)/shard_map/ppermute | solution.py:600
  (27 other events, 68.7 us)
Sparse Core Ops, SparseCore 0:
  105.5 73.8 all-gather.2
  181.7 50.5 all-gather.4
  245.8 73.2 reduce-scatter.2
  323.5 76.2 reduce-scatter.4
